TPU v7x, 32 devices: a whole 2x2x4 slice. The times are simulated.
32 devices in a mesh: groups: 2 (over y), tile: 4 (over z), pos: 4 (over x, core).
Axes of the slice: x: 2, y: 2, z: 4, core: 2. Of those that a mesh axis runs over, the one named last changes fastest.
Arguments:
- object_field: bfloat16 [2, 2048, 4096], P(None, ('groups', 'tile')), parts along dimension 1, may hold values from -6 to 6
- probe: float32 [4, 2, 256, 256], P('groups'), parts along dimension 0, may hold values from -6 to 6
- amplitude: bfloat16 [64, 256, 256], P(('groups', 'tile', 'pos')), parts along dimension 0, may hold values from 0.5 to 6
- offsets: int32 [64, 2], P(('groups', 'tile', 'pos')), parts along dimension 0, may hold values from 0 to 3840, as said below
- strip_owner: int32 [8], P('groups'), parts along dimension 0, may hold values from 0 to 3, each once
- chirp: float32 [256], replicated, may hold values from -3.140625 to 3.140625
Outputs:
- obj_grad: float32 [2, 2048, 4096], P(None, ('groups', 'tile'), 'pos'), parts along dimension 1
- probe_grad: float32 [4, 2, 256, 256], P('groups', None, 'pos'), parts along dimension 0
There are 2 independent parts, one for each index of `groups`. A program takes and returns all parts, laid end to end along the dimension named above; an argument that names none is the same for every part. Nothing has to cross between parts.
Inputs may be any that keep to these rules, and one draw needn't show every extreme that they name: Position j's window covers object rows offsets[j, 0] to offsets[j, 0] + 255 and columns offsets[j, 1] to offsets[j, 1] + 255, inside the object of 1024 x 4096 cells. The 2 positions of one device differ by at most 128 in their rows and by at most 128 in their columns, and both differences are reached on every device. `strip_owner`: A permutation.
All inputs are finite; a program needn't handle non-finite values.
Results may differ from a plain program's by a relative error of at most 0.0003.
Values may be sent and summed in bfloat16 or wider, within the bound.
No kernel may reach another device: no remote copies, remote signals or barrier semaphores. Data moves between devices by JAX's collectives and lax.ppermute only.
A program may use at most 128 MiB of HBM per device.

v0:
```python
import functools
import math

import jax
import jax.numpy as jnp
from jax import lax
from jax.experimental import pallas as pl
from jax.experimental.pallas import tpu as pltpu
from jax.sharding import PartitionSpec as P

HIGHEST_PREC = lax.Precision.HIGHEST


def build_propagator(chirp):
    win_size = chirp.shape[0]
    freq_index = jnp.arange(win_size, dtype=jnp.int32)
    phase_grid = (
        2.0
        * math.pi
        / win_size
        * (freq_index[:, None] * freq_index[None, :] % win_size).astype(jnp.float32)
    )
    unit_norm = 1.0 / math.sqrt(win_size)
    fourier_re = jnp.cos(phase_grid) * unit_norm
    fourier_im = -jnp.sin(phase_grid) * unit_norm
    chirp_re = jnp.cos(chirp)[:, None]
    chirp_im = jnp.sin(chirp)[:, None]
    middle_re = chirp_re * fourier_re - chirp_im * fourier_im
    middle_im = chirp_re * fourier_im + chirp_im * fourier_re
    prop_re = jnp.dot(fourier_re, middle_re, precision=HIGHEST_PREC) + jnp.dot(
        fourier_im, middle_im, precision=HIGHEST_PREC
    )
    prop_im = jnp.dot(fourier_re, middle_im, precision=HIGHEST_PREC) - jnp.dot(
        fourier_im, middle_re, precision=HIGHEST_PREC
    )
    return (prop_re, prop_im)


def apply_both(left_re, left_im, part_re, part_im):
    first_re = jnp.einsum("ab,...bc->...ac", left_re, part_re, precision=HIGHEST_PREC) - jnp.einsum(
        "ab,...bc->...ac", left_im, part_im, precision=HIGHEST_PREC
    )
    first_im = jnp.einsum("ab,...bc->...ac", left_re, part_im, precision=HIGHEST_PREC) + jnp.einsum(
        "ab,...bc->...ac", left_im, part_re, precision=HIGHEST_PREC
    )
    out_re = jnp.einsum("...ab,cb->...ac", first_re, left_re, precision=HIGHEST_PREC) - jnp.einsum(
        "...ab,cb->...ac", first_im, left_im, precision=HIGHEST_PREC
    )
    out_im = jnp.einsum("...ab,cb->...ac", first_re, left_im, precision=HIGHEST_PREC) + jnp.einsum(
        "...ab,cb->...ac", first_im, left_re, precision=HIGHEST_PREC
    )
    return (out_re, out_im)


def position_terms(window, probe, amplitude, prop_re, prop_im, grad_scale):
    obj_re = window[:, None, 0]
    obj_im = window[:, None, 1]
    probe_re = probe[None, :, 0]
    probe_im = probe[None, :, 1]
    exit_re = probe_re * obj_re - probe_im * obj_im
    exit_im = probe_re * obj_im + probe_im * obj_re
    far_re, far_im = apply_both(prop_re, prop_im, exit_re, exit_im)
    intensity = jnp.sum(far_re * far_re + far_im * far_im, axis=1, keepdims=True)
    factor = (
        1.0 - amplitude[:, None].astype(jnp.float32) / jnp.maximum(jnp.sqrt(intensity), 1.0)
    ) * grad_scale
    back_re, back_im = apply_both(prop_re.T, -prop_im.T, far_re * factor, far_im * factor)
    obj_part_re = jnp.sum(probe_re * back_re + probe_im * back_im, axis=1)
    obj_part_im = jnp.sum(probe_re * back_im - probe_im * back_re, axis=1)
    probe_part_re = jnp.sum(obj_re * back_re + obj_im * back_im, axis=0)
    probe_part_im = jnp.sum(obj_re * back_im - obj_im * back_re, axis=0)
    return (
        jnp.stack([obj_part_re, obj_part_im], axis=1),
        jnp.stack([probe_part_re, probe_part_im], axis=1),
    )


def owner_of(strips, strip_owner):
    table = jnp.arange(strip_owner.shape[0], dtype=jnp.int32)
    return jnp.sum(jnp.where(strips[..., None] == table, strip_owner, 0), axis=-1)


def place_columns(strip_grad, start_cols, pieces):
    span_width = pieces.shape[-1]
    column_ids = start_cols[:, None] + jnp.arange(span_width, dtype=jnp.int32)[None, :]
    return strip_grad.at[:, :, column_ids].add(pieces.transpose(1, 2, 0, 3))


def per_device_general(object_field, probe, amplitude, offsets, strip_owner, chirp):
    tile_count = lax.axis_size("tile")
    pos_groups = lax.axis_size("pos")
    pos_count = amplitude.shape[0]
    win_size = probe.shape[-1]
    strip_rows = object_field.shape[1]
    width_all = object_field.shape[2]
    last_strip = tile_count - 1
    grad_scale = 1.0 / math.sqrt(pos_count * tile_count * pos_groups)
    prop_re, prop_im = build_propagator(chirp)
    everyone = lax.all_gather(offsets, "tile", axis=0, tiled=True)
    row_off = offsets[:, 0]
    strip_grad = jnp.zeros((2, strip_rows, width_all), jnp.float32)
    reach_strips = (win_size - 1) // strip_rows + 2
    flat_cols = everyone[:, 1]

    def cut_piece(start_col):
        return lax.dynamic_slice_in_dim(object_field, start_col, win_size, 2)

    pieces = jax.vmap(cut_piece)(flat_cols).reshape(tile_count, pos_count, 2, strip_rows, win_size)
    arrived = lax.all_to_all(pieces, "tile", split_axis=0, concat_axis=0, tiled=True)
    strip_of = row_off // strip_rows
    inside = row_off - strip_of * strip_rows
    strips = jnp.minimum(
        strip_of[:, None] + jnp.arange(reach_strips, dtype=jnp.int32)[None, :], last_strip
    )
    owners = owner_of(strips, strip_owner)
    slot_ids = jnp.arange(pos_count, dtype=jnp.int32)[:, None]
    stacked = (
        arrived[owners, slot_ids]
        .transpose(0, 2, 1, 3, 4)
        .reshape(pos_count, 2, reach_strips * strip_rows, win_size)
    )

    def cut_rows(stack_one, row_at):
        return lax.dynamic_slice_in_dim(stack_one, row_at, win_size, 1)

    windows = jax.vmap(cut_rows)(stacked, inside)
    obj_part, probe_sum = position_terms(
        windows.astype(jnp.float32), probe, amplitude, prop_re, prop_im, grad_scale
    )

    def put_rows(base_one, piece_one, row_at):
        return lax.dynamic_update_slice_in_dim(base_one, piece_one, row_at, 1)

    padded = jnp.zeros((pos_count, 2, reach_strips * strip_rows, win_size), jnp.float32)
    padded = jax.vmap(put_rows)(padded, obj_part, inside)
    split_grad = padded.reshape(pos_count, 2, reach_strips, strip_rows, win_size).transpose(
        0, 2, 1, 3, 4
    )
    outgoing = (
        jnp.zeros((tile_count, pos_count, 2, strip_rows, win_size), jnp.float32)
        .at[owners, slot_ids]
        .add(split_grad)
    )
    returned = lax.all_to_all(outgoing, "tile", split_axis=0, concat_axis=0, tiled=True)
    flat_back = returned.reshape(tile_count * pos_count, 2, strip_rows, win_size)
    strip_grad = place_columns(strip_grad, flat_cols, flat_back)
    strip_part = lax.psum_scatter(strip_grad, "pos", scatter_dimension=2, tiled=True)
    probe_total = lax.psum(probe_sum, ("tile", "pos"))
    row_share = win_size // pos_groups
    probe_out = lax.dynamic_slice_in_dim(
        probe_total, lax.axis_index("pos") * row_share, row_share, 2
    )
    return (strip_part, probe_out)


def strip_held(owner_ref, me, count):
    held = jnp.int32(0)
    for s in range(count):
        held = held + jnp.where(owner_ref[s] == me, s, 0).astype(jnp.int32)
    return held


def geometry(y_a, x_a, y_b, x_b):
    first = y_a < y_b
    return (
        jnp.where(first, y_a, y_b),
        jnp.where(first, x_a, x_b),
        jnp.where(first, x_b, x_a),
        first,
    )


def lane_iota(shape):
    return lax.broadcasted_iota(jnp.int32, shape, 1)


def row_iota(shape):
    return lax.broadcasted_iota(jnp.int32, shape, 0)


def pack_kernel(tiles, win, width, me_ref, owner_ref, *refs):
    offs = refs[:tiles]
    obj_ref = refs[tiles]
    outs = refs[tiles + 1 : 2 * tiles + 1]
    buf, pack, params, in_sem, out_sem = refs[2 * tiles + 1 :]
    half = win // 2
    quarter = win // 4
    strip = strip_held(owner_ref, me_ref[0], tiles)

    def fetch(k):
        start = pl.multiple_of(params[k, 3], 128)
        return pltpu.make_async_copy(
            obj_ref.at[:, :, pl.ds(start, 2 * win)], buf.at[k], in_sem.at[k]
        )

    for k in range(tiles):
        y_up, x_up, x_low, _ = geometry(offs[k][0, 0], offs[k][0, 1], offs[k][1, 0], offs[k][1, 1])
        left = jnp.minimum(x_up, x_low)
        params[k, 0] = y_up
        params[k, 1] = (x_low > x_up).astype(jnp.int32)
        params[k, 3] = jnp.minimum((left // 128) * 128, width - 2 * win)
        params[k, 2] = left - params[k, 3]
        fetch(k).start()

    def one(k, carry):
        fetch(k).wait()
        y_up = params[k, 0]
        right = params[k, 1]
        rem = params[k, 2]
        turn = lax.rem(half - rem, half)
        keep = lane_iota((quarter, half)) < half - rem
        base = strip * win
        for part in range(2):
            for chunk in range(2):
                outer = []
                for level in range(2):
                    row0 = level * half + chunk * quarter
                    wide = buf[k, part, row0 : row0 + quarter, :].astype(jnp.float32)
                    spun = [
                        pltpu.roll(wide[:, half * b : half * (b + 1)], turn, 1) for b in range(4)
                    ]
                    cols = [jnp.where(keep, spun[b], spun[b + 1]) for b in range(3)]
                    rows = base + row0 + row_iota((quarter, half))
                    in_upper = (rows < y_up + win).astype(jnp.int32)
                    low_first = in_upper == right
                    pack[k, part, row0 : row0 + quarter, 0:half] = jnp.where(
                        low_first, cols[0], cols[1]
                    ).astype(pack.dtype)
                    pack[k, part, row0 : row0 + quarter, half:win] = jnp.where(
                        low_first, cols[1], cols[2]
                    ).astype(pack.dtype)
                    outer.append(jnp.where(right == 1, cols[2], cols[0]))
                high = base + half + chunk * quarter + row_iota((quarter, half))
                use_high = (high >= y_up + half) & (high < y_up + win)
                pack[k, part, win : win + quarter, half * chunk : half * (chunk + 1)] = jnp.where(
                    use_high, outer[1], outer[0]
                ).astype(pack.dtype)
        return carry

    for k in range(tiles):
        one(k, 0)
        pltpu.make_async_copy(pack.at[k], outs[k], out_sem.at[k]).start()
    for k in range(tiles):
        pltpu.make_async_copy(pack.at[k], outs[k], out_sem.at[k]).wait()


def halves(x):
    high = x.astype(jnp.bfloat16)
    return high, (x - high.astype(jnp.float32)).astype(jnp.bfloat16)


def dot(a, b):
    return lax.dot_general(a, b, (((1,), (0,)), ((), ())), preferred_element_type=jnp.float32)


def rows_from(ref, part, start, count):
    down = pl.multiple_of((start // 8) * 8, 8)
    rows = ref[part, pl.ds(down, count + 8), :]
    return pltpu.roll(rows, lax.rem(count + 8 - (start - down), count + 8), 0)[0:count]


def rows_to(ref, part, start, blocks):
    down = pl.multiple_of((start // 8) * 8, 8)
    rows = jnp.concatenate(blocks + [jnp.zeros((8, blocks[0].shape[1]), jnp.float32)], axis=0)
    ref[part, pl.ds(down, rows.shape[0]), :] = pltpu.roll(rows, start - down, 0)


def compute_kernel(tiles, pos_groups, win, modes, grad_scale, me_ref, owner_ref, off_ref, *refs):
    packs = refs[:tiles]
    probe, amp, prop_re, prop_im, prop_t_re, prop_t_im, spot_ref = refs[tiles : tiles + 7]
    grads = refs[tiles + 7 : 2 * tiles + 7]
    pieces = refs[2 * tiles + 7 : 2 * tiles + 7 + pos_groups]
    (
        held, cat, wins, far, factor, right_a, right_b, left_a, left_b, obj_acc, probe_acc, gcat, outer_acc, gpack,
        in_sem, out_sem, piece_sem,
    ) = refs[2 * tiles + 7 + pos_groups :]
    half = win // 2
    quarter = win // 4
    me = me_ref[0]
    fetches = [pltpu.make_async_copy(packs[k], held.at[k], in_sem.at[k]) for k in range(tiles)]
    for fetch in fetches:
        fetch.start()

    for way in range(2):
        if way == 0:
            r_re, r_im = prop_t_re[...], prop_t_im[...]
            l_re, l_im = prop_re[...], prop_im[...]
        else:
            r_re, r_im = prop_re[...], -prop_im[...]
            l_re, l_im = prop_t_re[...], -prop_t_im[...]
        (rr, rr_low), (ri, ri_low) = halves(r_re), halves(r_im)
        for row, (a, b) in enumerate([(rr, ri), (rr, ri), (-ri, rr), (-ri, rr)]):
            right_a[way, row * win : (row + 1) * win, 0:win] = a
            right_a[way, row * win : (row + 1) * win, win : 2 * win] = b
        for row, (a, b) in enumerate([(rr_low, ri_low), (-ri_low, rr_low)]):
            right_b[way, row * win : (row + 1) * win, 0:win] = a
            right_b[way, row * win : (row + 1) * win, win : 2 * win] = b
        (lr, lr_low), (li, li_low) = halves(l_re), halves(l_im)
        for col, (a, b) in enumerate([(lr, li), (lr, li), (-li, lr), (-li, lr)]):
            left_a[way, 0:win, col * win : (col + 1) * win] = a
            left_a[way, win : 2 * win, col * win : (col + 1) * win] = b
        for col, (a, b) in enumerate([(lr_low, li_low), (-li_low, lr_low)]):
            left_b[way, 0:win, col * win : (col + 1) * win] = a
            left_b[way, win : 2 * win, col * win : (col + 1) * win] = b

    y_up, x_up, x_low, first = geometry(off_ref[0, 0], off_ref[0, 1], off_ref[1, 0], off_ref[1, 1])
    right = x_low > x_up
    strip = y_up // win
    rem = y_up - strip * win
    low_rem = lax.rem(rem, half)
    mid_block = (y_up + half) // half

    def slot_of(s):
        return lax.rem(me - owner_ref[jnp.minimum(s, tiles - 1)] + tiles, tiles)

    for fetch in fetches:
        fetch.wait()
    slots = [slot_of(strip + d) for d in range(3)]
    for part in range(2):
        for d in range(3):
            cat[part, d * win : (d + 1) * win, :] = held[slots[d], part, 0:win, :].astype(jnp.float32)
        for d in range(2):
            slot = slot_of((mid_block + d) // 2)
            for chunk in range(2):
                outer_acc[part, d * half + chunk * quarter : d * half + (chunk + 1) * quarter, :] = held[
                    slot, part, win : win + quarter, half * chunk : half * (chunk + 1)
                ].astype(jnp.float32)
    for part in range(2):
        upper = rows_from(cat, part, rem, win)
        wins[0, part] = upper
        wins[1, part, half:win, :] = rows_from(cat, part, rem + win, half)
        outer = rows_from(outer_acc, part, low_rem, half)
        wins[1, part, 0:half, 0:half] = jnp.where(right, upper[half:win, half:win], outer)
        wins[1, part, 0:half, half:win] = jnp.where(right, outer, upper[half:win, 0:half])

    def both(way, re, im):
        (re_h, re_l), (im_h, im_l) = halves(re), halves(im)
        mid = dot(jnp.concatenate([re_h, re_l, im_h, im_l], axis=1), right_a[way]) + dot(
            jnp.concatenate([re_h, im_h], axis=1), right_b[way]
        )
        (re_h, re_l), (im_h, im_l) = halves(mid[:, 0:win]), halves(mid[:, win : 2 * win])
        return dot(left_a[way], jnp.concatenate([re_h, re_l, im_h, im_l], axis=0)) + dot(
            left_b[way], jnp.concatenate([re_h, im_h], axis=0)
        )

    def forward(n, carry):
        q = n // modes
        m = lax.rem(n, modes)
        p_re, p_im = probe[m, 0], probe[m, 1]
        w_re, w_im = wins[q, 0], wins[q, 1]
        far[n] = both(0, p_re * w_re - p_im * w_im, p_re * w_im + p_im * w_re)
        return carry

    lax.fori_loop(0, 2 * modes, forward, 0)
    for q in range(2):
        total = jnp.zeros((win, win), jnp.float32)
        for m in range(modes):
            f_re, f_im = far[q * modes + m, 0:win, :], far[q * modes + m, win : 2 * win, :]
            total = total + (f_re * f_re + f_im * f_im)
        frame = jnp.where(first, q, 1 - q)
        measured = amp[frame].astype(jnp.float32)
        factor[q] = (1.0 - measured / jnp.maximum(jnp.sqrt(total), 1.0)) * grad_scale
    obj_acc[...] = jnp.zeros_like(obj_acc)
    probe_acc[...] = jnp.zeros_like(probe_acc)

    def backward(n, carry):
        q = n // modes
        m = lax.rem(n, modes)
        scale = factor[q]
        back = both(1, far[n, 0:win, :] * scale, far[n, win : 2 * win, :] * scale)
        b_re, b_im = back[0:win, :], back[win : 2 * win, :]
        p_re, p_im = probe[m, 0], probe[m, 1]
        w_re, w_im = wins[q, 0], wins[q, 1]
        obj_acc[q, 0] = obj_acc[q, 0] + (p_re * b_re + p_im * b_im)
        obj_acc[q, 1] = obj_acc[q, 1] + (p_re * b_im - p_im * b_re)
        probe_acc[m, 0] = probe_acc[m, 0] + (w_re * b_re + w_im * b_im)
        probe_acc[m, 1] = probe_acc[m, 1] + (w_re * b_im - w_im * b_re)
        return carry

    lax.fori_loop(0, 2 * modes, backward, 0)
    share = win // pos_groups
    spot = spot_ref[0]
    piece_copies = []
    for j in range(pos_groups):
        start = pl.multiple_of(jnp.bitwise_xor(spot, j) * share, share)
        piece_copies.append(
            pltpu.make_async_copy(
                probe_acc.at[:, :, pl.ds(start, share), :], pieces[j], piece_sem.at[j]
            )
        )
        piece_copies[-1].start()

    gcat[...] = jnp.zeros_like(gcat)
    outer_acc[...] = jnp.zeros_like(outer_acc)
    for part in range(2):
        low_a = obj_acc[1, part, 0:half, 0:half]
        low_b = obj_acc[1, part, 0:half, half:win]
        zero = jnp.zeros_like(low_a)
        obj_acc[0, part, half:win, 0:half] += jnp.where(right, zero, low_b)
        obj_acc[0, part, half:win, half:win] += jnp.where(right, low_a, zero)
        rows_to(gcat, part, rem, [obj_acc[0, part], obj_acc[1, part, half:win, :]])
        rows_to(outer_acc, part, low_rem, [jnp.where(right, low_b, low_a)])
        outer = outer_acc[part, 0:half, :] + outer_acc[part, half:win, :]
        for d in range(3):
            gpack[d, part, 0:win, :] = gcat[part, d * win : (d + 1) * win, :]
            for chunk in range(2):
                gpack[d, part, win : win + quarter, half * chunk : half * (chunk + 1)] = outer[
                    chunk * quarter : (chunk + 1) * quarter, :
                ]
    grad_copies = []
    for k in range(tiles):
        there = strip_held(owner_ref, lax.rem(me + k, tiles), tiles)
        d = jnp.clip(there - strip, 0, 2)
        grad_copies.append(pltpu.make_async_copy(gpack.at[d], grads[k], out_sem.at[k]))
        grad_copies[-1].start()
    for copy in piece_copies + grad_copies:
        copy.wait()


def place_kernel(tiles, pos_groups, win, slab, me_ref, spot_ref, owner_ref, *refs):
    count = tiles * pos_groups
    offs = refs[:pos_groups]
    packs = refs[pos_groups : pos_groups + count]
    parts_in = refs[pos_groups + count : pos_groups + count + tiles]
    out_ref, probe_ref = refs[pos_groups + count + tiles : pos_groups + count + tiles + 2]
    held, acc, probe_acc, params, in_sem, out_sem, part_sem = refs[pos_groups + count + tiles + 2 :]
    half = win // 2
    quarter = win // 4
    me = me_ref[0]
    strip = strip_held(owner_ref, me, tiles)
    base = strip * win
    first_col = spot_ref[0] * slab
    margin = 2 * win
    span = 3 * half
    rows_each = probe_acc.shape[2] // tiles
    part_copies = []
    for k in range(tiles):
        turn = lax.rem(me + tiles - k, tiles)
        start = pl.multiple_of(turn * rows_each, rows_each)
        part_copies.append(
            pltpu.make_async_copy(
                parts_in[k], probe_acc.at[:, :, pl.ds(start, rows_each), :], part_sem.at[k]
            )
        )
        part_copies[-1].start()

    for n in range(count):
        j, k = n // tiles, n % tiles
        off = offs[j]
        y_up, x_up, x_low, _ = geometry(off[2 * k, 0], off[2 * k, 1], off[2 * k + 1, 0], off[2 * k + 1, 1])
        left = jnp.minimum(x_up, x_low)
        hit = (y_up < base + win) & (y_up + span > base) & (left < first_col + slab) & (left + span > first_col)
        params[n, 0] = hit.astype(jnp.int32)
        params[n, 1] = y_up
        params[n, 2] = (x_low > x_up).astype(jnp.int32)
        params[n, 3] = left - first_col + margin

        @pl.when(hit)
        def _():
            pltpu.make_async_copy(packs[n], held.at[n], in_sem.at[n]).start()

    def clear(i, carry):
        acc[:, pl.ds(pl.multiple_of(i * 8, 8), 8), :] = jnp.zeros((2, 8, acc.shape[2]), jnp.float32)
        return carry

    lax.fori_loop(0, win // 8, clear, 0)
    for copy in part_copies:
        copy.wait()
    probe_out = pltpu.make_async_copy(probe_acc, probe_ref, part_sem.at[tiles])
    probe_out.start()

    def one(n, carry):
        @pl.when(params[n, 0] == 1)
        def _():
            pltpu.make_async_copy(packs[0], held.at[n], in_sem.at[n]).wait()
            y_up = params[n, 1]
            right = params[n, 2]
            col = params[n, 3]
            start = pl.multiple_of((col // 128) * 128, 128)
            rem = col - start
            lanes = lane_iota((quarter, half))
            stay = lanes >= rem

            for part in range(2):
                for chunk in range(4):
                    row0 = chunk * quarter
                    rows = base + row0 + row_iota((quarter, half))
                    low_first = (rows < y_up + win).astype(jnp.int32) == right
                    in_outer = (rows >= y_up + half) & (rows < y_up + win)
                    m0 = held[n, part, row0 : row0 + quarter, 0:half]
                    m1 = held[n, part, row0 : row0 + quarter, half:win]
                    side = held[n, part, win : win + quarter, half * (chunk % 2) : half * (chunk % 2 + 1)]
                    side = jnp.where(in_outer, side, 0.0)
                    cols = [
                        jnp.where(low_first, m0, jnp.where(right == 0, side, 0.0)),
                        jnp.where(low_first, m1, m0),
                        jnp.where(low_first, jnp.where(right == 1, side, 0.0), m1),
                    ]
                    spun = [pltpu.roll(c, rem, 1) for c in cols]
                    zero = jnp.zeros_like(m0)
                    shifted = [
                        jnp.where(stay, spun[0], zero),
                        jnp.where(stay, spun[1], spun[0]),
                        jnp.where(stay, spun[2], spun[1]),
                        jnp.where(stay, zero, spun[2]),
                    ]
                    for b in range(4):
                        at = pl.ds(pl.multiple_of(start + b * half, 128), half)
                        acc[part, row0 : row0 + quarter, at] += shifted[b]

        return carry

    lax.fori_loop(0, count, one, 0)
    out = pltpu.make_async_copy(acc.at[:, :, margin : margin + slab], out_ref, out_sem)
    out.start()
    out.wait()
    probe_out.wait()


def shifted(x, axis, count, k):
    return lax.ppermute(x, axis, [(i, (i + k) % count) for i in range(count)])


def swapped(x, axis, count, bit):
    return lax.ppermute(x, axis, [(i, i ^ bit) for i in range(count)])


def per_device_packed(object_field, probe, amplitude, offsets, strip_owner, chirp):
    tiles = lax.axis_size("tile")
    pos_groups = lax.axis_size("pos")
    pos_count, win, _ = amplitude.shape
    modes = probe.shape[0]
    width = object_field.shape[2]
    slab = width // pos_groups
    half = win // 2
    quarter = win // 4
    grad_scale = 1.0 / math.sqrt(pos_count * tiles * pos_groups)
    me = lax.axis_index("tile").astype(jnp.int32).reshape(1)
    spot = lax.axis_index("pos").astype(jnp.int32).reshape(1)
    smem = pl.BlockSpec(memory_space=pltpu.SMEM)
    vmem = pl.BlockSpec(memory_space=pltpu.VMEM)
    anywhere = pl.BlockSpec(memory_space=pl.ANY)
    pack_shape = (2, win + quarter, win)

    offs = [offsets] + [shifted(offsets, "tile", tiles, tiles - k) for k in range(1, tiles)]
    packs = pl.pallas_call(
        functools.partial(pack_kernel, tiles, win, width),
        out_shape=[jax.ShapeDtypeStruct(pack_shape, jnp.bfloat16)] * tiles,
        in_specs=[smem] * (2 + tiles) + [anywhere],
        out_specs=[anywhere] * tiles,
        scratch_shapes=[
            pltpu.VMEM((tiles, 2, win, 2 * win), jnp.bfloat16),
            pltpu.VMEM((tiles,) + pack_shape, jnp.bfloat16),
            pltpu.SMEM((tiles, 4), jnp.int32),
            pltpu.SemaphoreType.DMA((tiles,)),
            pltpu.SemaphoreType.DMA((tiles,)),
        ],
        name="pack",
    )(me, strip_owner, *offs, object_field)
    arrived = [packs[0]] + [shifted(packs[k], "tile", tiles, k) for k in range(1, tiles)]
    prop_re, prop_im = build_propagator(chirp)
    results = pl.pallas_call(
        functools.partial(compute_kernel, tiles, pos_groups, win, modes, grad_scale),
        out_shape=[jax.ShapeDtypeStruct(pack_shape, jnp.float32)] * tiles
        + [jax.ShapeDtypeStruct((modes, 2, win // pos_groups, win), jnp.float32)] * pos_groups,
        in_specs=[smem] * 3 + [anywhere] * tiles + [vmem] * 6 + [smem],
        out_specs=[anywhere] * (tiles + pos_groups),
        scratch_shapes=[
            pltpu.VMEM((tiles,) + pack_shape, jnp.bfloat16),
            pltpu.VMEM((2, 3 * win, win), jnp.float32),
            pltpu.VMEM((2, 2, win, win), jnp.float32),
            pltpu.VMEM((2 * modes, 2 * win, win), jnp.float32),
            pltpu.VMEM((2, win, win), jnp.float32),
            pltpu.VMEM((2, 4 * win, 2 * win), jnp.bfloat16),
            pltpu.VMEM((2, 2 * win, 2 * win), jnp.bfloat16),
            pltpu.VMEM((2, 2 * win, 4 * win), jnp.bfloat16),
            pltpu.VMEM((2, 2 * win, 2 * win), jnp.bfloat16),
            pltpu.VMEM((2, 2, win, win), jnp.float32),
            pltpu.VMEM((modes, 2, win, win), jnp.float32),
            pltpu.VMEM((2, 3 * win, win), jnp.float32),
            pltpu.VMEM((2, win, half), jnp.float32),
            pltpu.VMEM((3,) + pack_shape, jnp.float32),
            pltpu.SemaphoreType.DMA((tiles,)),
            pltpu.SemaphoreType.DMA((tiles,)),
            pltpu.SemaphoreType.DMA((pos_groups,)),
        ],
        name="propagate",
    )(me, strip_owner, offsets, *arrived, probe, amplitude, prop_re, prop_im, prop_re.T, prop_im.T, spot)
    grads, pieces = results[:tiles], list(results[tiles:])

    column = [grads[0]] + [shifted(grads[k], "tile", tiles, k) for k in range(1, tiles)]
    column_offs = [jnp.concatenate([offs[(tiles - k) % tiles] for k in range(tiles)], axis=0)]
    columns = [column]
    bit = pos_groups // 2
    while bit:
        columns = columns + [[swapped(x, "pos", pos_groups, bit) for x in c] for c in columns]
        column_offs = column_offs + [swapped(o, "pos", pos_groups, bit) for o in column_offs]
        bit //= 2

    bit = 1
    while len(pieces) > 1:
        pieces = [
            pieces[j] + swapped(pieces[j + 1], "pos", pos_groups, bit) for j in range(0, len(pieces), 2)
        ]
        bit *= 2
    mine = pieces[0]
    each = mine.shape[2] // tiles
    total = lax.dynamic_slice_in_dim(mine, me[0] * each, each, 2)
    for k in range(1, tiles):
        sent = lax.dynamic_slice_in_dim(mine, lax.rem(me[0] + k, tiles) * each, each, 2)
        total = total + shifted(sent, "tile", tiles, k)
    totals = [total] + [shifted(total, "tile", tiles, k) for k in range(1, tiles)]

    flat = [x for c in columns for x in c]
    count = len(flat)
    strip_part, probe_out = pl.pallas_call(
        functools.partial(place_kernel, tiles, pos_groups, win, slab),
        out_shape=[
            jax.ShapeDtypeStruct((2, win, slab), jnp.float32),
            jax.ShapeDtypeStruct((modes, 2, win // pos_groups, win), jnp.float32),
        ],
        in_specs=[smem] * (3 + pos_groups) + [anywhere] * (count + tiles),
        out_specs=[anywhere, anywhere],
        scratch_shapes=[
            pltpu.VMEM((count,) + pack_shape, jnp.float32),
            pltpu.VMEM((2, win, slab + 4 * win), jnp.float32),
            pltpu.VMEM((modes, 2, win // pos_groups, win), jnp.float32),
            pltpu.SMEM((count, 4), jnp.int32),
            pltpu.SemaphoreType.DMA((count,)),
            pltpu.SemaphoreType.DMA,
            pltpu.SemaphoreType.DMA((tiles + 1,)),
        ],
        name="place",
    )(me, spot, strip_owner, *column_offs, *flat, *totals)
    return (strip_part, probe_out)


def per_device(object_field, probe, amplitude, offsets, strip_owner, chirp):
    tiles = lax.axis_size("tile")
    pos_groups = lax.axis_size("pos")
    pos_count, win, _ = amplitude.shape
    width = object_field.shape[2]
    packed = (
        pos_count == 2
        and object_field.shape[1] == win
        and win == 256
        and pos_groups & (pos_groups - 1) == 0
        and width // pos_groups >= 2 * win
        and (width // pos_groups) % 128 == 0
        and (win // pos_groups) % (8 * tiles) == 0
    )
    plan = per_device_packed if packed else per_device_general
    return plan(object_field, probe, amplitude, offsets, strip_owner, chirp)


def solution(mesh):
    return jax.shard_map(
        per_device,
        mesh=mesh,
        in_specs=(
            P(None, ("groups", "tile"), None),
            P("groups", None, None, None),
            P(("groups", "tile", "pos"), None, None),
            P(("groups", "tile", "pos"), None),
            P("groups"),
            P(),
        ),
        out_specs=(P(None, ("groups", "tile"), "pos"), P("groups", None, "pos", None)),
        check_vma=False,
    )
```

profile of v0, /device:TPU:1, one launch (start us, length us, event | category | flops | bytes accessed | tf_op | source)
XLA Modules:
  0.0 202.0 jit_solution(222219630351779460)
XLA Ops:
  0.6 4.2 %collective-permute-start.2 = (s32[2,2]{1,0:T(2,128)}, s32[2,2]{1,0:T(2,128)S(1)}, u32[]{:S(2)}, u32[]{:S(2)}) collective-permute-start(s32[2,2]{1,0:T(2,128)} %off_ref.1), channel_id=1, source_target_pairs={{0,12},{4,0},{8,4},{12,8},{1,13},{5,1},{9,5},{13,9},{2,14},{6,2},{... | collective-permute-start | bytes 56 | tf_op jit(solution)/shard_map/ppermute | solution.py:521
  6.0 1.7 fusion.8
  7.7 1.7 convolution_subtract_fusion
  10.0 3.5 %pack.1 = (bf16[2,320,256]{2,1,0:T(8,128)(2,1)}, bf16[2,320,256]{2,1,0:T(8,128)(2,1)}, bf16[2,320,256]{2,1,0:T(8,128)(2,1)}, bf16[2,320,256]{2,1,0:T(8,128)(2,1)}) custom-call(s32[1]{0:T(128)} %bitcast.me_ref, s32[4]{0:T(128)} %owner_ref.5, s32[2,2]{1,0:T(2,128)} %off_ref.1, s32[2,2]{1,0:T(2,128)} %copy-done.30, s32[2,2]{1,0:T(2,128)} %copy-done.32, ...), custom_call_target="tpu_custom_call" | custom-call | tf_op jit(solution)/shard_map/pack/pallas_call | solution.py:546
  13.5 2.2 %collective-permute-start.6 = (bf16[2,320,256]{2,1,0:T(8,128)(2,1)}, bf16[2,320,256]{2,1,0:T(8,128)(2,1)S(1)}, u32[]{:S(2)}, u32[]{:S(2)}) collective-permute-start(bf16[2,320,256]{2,1,0:T(8,128)(2,1)} %get-tuple-element.15), channel_id=1, source_target_pairs={{0,4},{4,8},{8,12},{12,0},{1,5},{5,9},{9,13},{13,1},{2,6},{6,10},{... | collective-permute-start | bytes 983048 | tf_op jit(solution)/shard_map/ppermute | solution.py:521
  16.7 1.3 collective-permute-start.8
  18.0 1.6 fusion.10
  20.5 1.6 convolution_add_fusion
  23.0 16.3 %collective-permute-done.7.refs_2_ = bf16[2,320,256]{2,1,0:T(8,128)(2,1)S(1)} collective-permute-done((bf16[2,320,256]{2,1,0:T(8,128)(2,1)}, bf16[2,320,256]{2,1,0:T(8,128)(2,1)S(1)}, u32[]{:S(2)}, u32[]{:S(2)}) %collective-permute-start.7) | collective-permute-done | bytes 327712 | tf_op jit(solution)/shard_map/ppermute | solution.py:521
  40.2 15.5 %propagate.1 = (f32[2,320,256]{2,1,0:T(8,128)}, f32[2,320,256]{2,1,0:T(8,128)}, f32[2,320,256]{2,1,0:T(8,128)}, f32[2,320,256]{2,1,0:T(8,128)}, f32[2,2,64,256]{...) custom-call(s32[1]{0:T(128)} %bitcast.me_ref, s32[4]{0:T(128)} %owner_ref.5, ...), custom_call_target="tpu_custom_call" | custom-call | tf_op jit(solution)/shard_map/propagate/pallas_call | solution.py:562
  56.4 1.3 collective-permute-done.25
  58.7 1.3 collective-permute-start.26
  59.9 6.3 %collective-permute-done.26 = f32[2,2,64,256]{3,2,1,0:T(8,128)S(1)} collective-permute-done((f32[2,2,64,256]{3,2,1,0:T(8,128)S(1)}, f32[2,2,64,256]{3,2,1,0:T(8,128)S(1)}, u32[]{:S(2)}, u32[]{:S(2)}) %collective-permute-start.26) | collective-permute-done | bytes 262176 | tf_op jit(solution)/shard_map/ppermute | solution.py:525
  67.3 7.1 %collective-permute-start.27 = (f32[2,2,16,256]{3,2,1,0:T(8,128)S(1)}, f32[2,2,16,256]{3,2,1,0:T(8,128)S(1)}, u32[]{:S(2)}, u32[]{:S(2)}) collective-permute-start(f32[2,2,16,256]{3,2,1,0:T(8,128)S(1)} %get-tuple-element.26), channel_id=1, source_target_pairs={{0,4},{4,8},{8,12},{12,0},{1,5},{5,9},{9,13},{13,1},{2,6},{6,10},{... | collective-permute-start | bytes 196616 | tf_op jit(solution)/shard_map/ppermute | solution.py:521
  74.4 1.3 collective-permute-start.3
  75.7 1.8 collective-permute-start.4
  77.5 2.1 %collective-permute-start.5 = (s32[8,2]{1,0:T(8,128)S(1)}, s32[8,2]{1,0:T(8,128)S(1)}, u32[]{:S(2)}, u32[]{:S(2)}) collective-permute-start(s32[8,2]{1,0:T(8,128)S(1)} %collective-permute-done.3.refs_1_), channel_id=1, source_target_pairs={{0,1},{1,0},{2,3},{3,2},{4,5},{5,4},{6,7},{7,6},{8,9},{9,8},{10,11... | collective-permute-start | bytes 200 | tf_op jit(solution)/shard_map/ppermute | solution.py:525
  79.6 3.3 %collective-permute-start.29 = (f32[2,2,16,256]{3,2,1,0:T(8,128)S(1)}, f32[2,2,16,256]{3,2,1,0:T(8,128)S(1)}, u32[]{:S(2)}, u32[]{:S(2)}) collective-permute-start(f32[2,2,16,256]{3,2,1,0:T(8,128)S(1)} %get-tuple-element.27), channel_id=1, source_target_pairs={{0,12},{4,0},{8,4},{12,8},{1,13},{5,1},{9,5},{13,9},{2,14},{6,2},{... | collective-permute-start | bytes 196616 | tf_op jit(solution)/shard_map/ppermute | solution.py:521
  82.9 2.3 %collective-permute-start.10 = (f32[2,320,256]{2,1,0:T(8,128)}, f32[2,320,256]{2,1,0:T(8,128)S(1)}, u32[]{:S(2)}, u32[]{:S(2)}) collective-permute-start(f32[2,320,256]{2,1,0:T(8,128)} %get-tuple-element.20), channel_id=1, source_target_pairs={{0,8},{4,12},{8,0},{12,4},{1,9},{5,13},{9,1},{13,5},{2,10},{6,14},... | collective-permute-start | bytes 1966088 | tf_op jit(solution)/shard_map/ppermute | solution.py:521
  86.0 9.6 %collective-permute-done.29 = f32[2,2,16,256]{3,2,1,0:T(8,128)S(1)} collective-permute-done((f32[2,2,16,256]{3,2,1,0:T(8,128)S(1)}, f32[2,2,16,256]{3,2,1,0:T(8,128)S(1)}, u32[]{:S(2)}, u32[]{:S(2)}) %collective-permute-start.29) | collective-permute-done | bytes 65568 | tf_op jit(solution)/shard_map/ppermute | solution.py:521
  97.1 3.4 %collective-permute-done.28 = f32[2,2,16,256]{3,2,1,0:T(8,128)} collective-permute-done((f32[2,2,16,256]{3,2,1,0:T(8,128)S(1)}, f32[2,2,16,256]{3,2,1,0:T(8,128)}, u32[]{:S(2)}, u32[]{:S(2)}) %collective-permute-start.28) | collective-permute-done | bytes 65568 | tf_op jit(solution)/shard_map/ppermute | solution.py:521
  100.5 1.2 collective-permute-start.12
  102.7 30.1 %collective-permute-start.32 = (f32[2,2,16,256]{3,2,1,0:T(8,128)S(1)}, f32[2,2,16,256]{3,2,1,0:T(8,128)S(1)}, u32[]{:S(2)}, u32[]{:S(2)}) collective-permute-start(f32[2,2,16,256]{3,2,1,0:T(8,128)S(1)} %add_add_fusion.1.refs_20_), channel_id=1, source_target_pairs={{0,12},{4,0},{8,4},{12,8},{1,13},{5,1},{9,5},{13,9},{2,14},{6,2},{... | collective-permute-start | bytes 196616 | tf_op jit(solution)/shard_map/ppermute | solution.py:521
  132.8 14.8 %collective-permute-start.30 = (f32[2,2,16,256]{3,2,1,0:T(8,128)S(1)}, f32[2,2,16,256]{3,2,1,0:T(8,128)S(1)}, u32[]{:S(2)}, u32[]{:S(2)}) collective-permute-start(f32[2,2,16,256]{3,2,1,0:T(8,128)S(1)} %add_add_fusion.1.refs_20_), channel_id=1, source_target_pairs={{0,4},{4,8},{8,12},{12,0},{1,5},{5,9},{9,13},{13,1},{2,6},{6,10},{... | collective-permute-start | bytes 196616 | tf_op jit(solution)/shard_map/ppermute | solution.py:521
  147.6 1.4 collective-permute-start.17
  150.9 1.2 collective-permute-start.15
  153.2 12.0 %collective-permute-done.13.refs_9_ = f32[2,320,256]{2,1,0:T(8,128)S(1)} collective-permute-done((f32[2,320,256]{2,1,0:T(8,128)S(1)}, f32[2,320,256]{2,1,0:T(8,128)S(1)}, u32[]{:S(2)}, u32[]{:S(2)}) %collective-permute-start.13) | collective-permute-done | bytes 655392 | tf_op jit(solution)/shard_map/ppermute | solution.py:525
  165.2 1.5 collective-permute-start.20
  166.8 12.5 %collective-permute-done.14.refs_10_ = f32[2,320,256]{2,1,0:T(8,128)S(1)} collective-permute-done((f32[2,320,256]{2,1,0:T(8,128)S(1)}, f32[2,320,256]{2,1,0:T(8,128)S(1)}, u32[]{:S(2)}, u32[]{:S(2)}) %collective-permute-start.14) | collective-permute-done | bytes 655392 | tf_op jit(solution)/shard_map/ppermute | solution.py:525
  179.3 1.5 collective-permute-start.22
  180.7 12.6 %collective-permute-done.15.refs_11_ = f32[2,320,256]{2,1,0:T(8,128)S(1)} collective-permute-done((f32[2,320,256]{2,1,0:T(8,128)S(1)}, f32[2,320,256]{2,1,0:T(8,128)S(1)}, u32[]{:S(2)}, u32[]{:S(2)}) %collective-permute-start.15) | collective-permute-done | bytes 655392 | tf_op jit(solution)/shard_map/ppermute | solution.py:525
  196.6 5.2 %place.1 = (f32[2,256,1024]{2,1,0:T(8,128)}, f32[2,2,64,256]{3,2,1,0:T(8,128)}) custom-call(s32[1]{0:T(128)} %bitcast.me_ref, s32[1]{0:T(128)} %bitcast.1.refs_10_.spot_ref, s32[4]{0:T(128)} %owner_ref.5, s32[8,2]{1,0:T(8,128)} %copy-done.25, s32[8,2]{1,0:T(8,128)} %copy-done.27, s32[8,2]{1,0:T(8,128)} %copy-done.28, s32[8,2]{1,0:T(8,128)} %copy-done.29, ...), custom_call_target="tpu_custom_call" | custom-call | tf_op jit(solution)/shard_map/place/pallas_call | solution.py:616
  (121 shorter events, 17.4 us)
Async XLA Ops:
  0.6 8.7 %collective-permute-start.2 = (s32[2,2]{1,0:T(2,128)}, s32[2,2]{1,0:T(2,128)S(1)}, u32[]{:S(2)}, u32[]{:S(2)}) collective-permute-start(s32[2,2]{1,0:T(2,128)} %off_ref.1), channel_id=1, source_target_pairs={{0,12},{4,0},{8,4},{12,8},{1,13},{5,1},{9,5},{13,9},{2,14},{6,2},{... | collective-permute-start | bytes 56 | tf_op jit(solution)/shard_map/ppermute | solution.py:521
  4.8 4.5 %collective-permute-start.1 = (s32[2,2]{1,0:T(2,128)}, s32[2,2]{1,0:T(2,128)S(1)}, u32[]{:S(2)}, u32[]{:S(2)}) collective-permute-start(s32[2,2]{1,0:T(2,128)} %off_ref.1), channel_id=1, source_target_pairs={{0,8},{4,12},{8,0},{12,4},{1,9},{5,13},{9,1},{13,5},{2,10},{6,14},... | collective-permute-start | bytes 56 | tf_op jit(solution)/shard_map/ppermute | solution.py:521
  4.8 4.5 %collective-permute-start = (s32[2,2]{1,0:T(2,128)}, s32[2,2]{1,0:T(2,128)S(1)}, u32[]{:S(2)}, u32[]{:S(2)}) collective-permute-start(s32[2,2]{1,0:T(2,128)} %off_ref.1), channel_id=1, source_target_pairs={{0,4},{4,8},{8,12},{12,0},{1,5},{5,9},{9,13},{13,1},{2,6},{6,10},{... | collective-permute-start | bytes 56 | tf_op jit(solution)/shard_map/ppermute | solution.py:521
  13.5 9.5 %collective-permute-start.6 = (bf16[2,320,256]{2,1,0:T(8,128)(2,1)}, bf16[2,320,256]{2,1,0:T(8,128)(2,1)S(1)}, u32[]{:S(2)}, u32[]{:S(2)}) collective-permute-start(bf16[2,320,256]{2,1,0:T(8,128)(2,1)} %get-tuple-element.15), channel_id=1, source_target_pairs={{0,4},{4,8},{8,12},{12,0},{1,5},{5,9},{9,13},{13,1},{2,6},{6,10},{... | collective-permute-start | bytes 983048 | tf_op jit(solution)/shard_map/ppermute | solution.py:521
  15.8 23.5 %collective-permute-start.7 = (bf16[2,320,256]{2,1,0:T(8,128)(2,1)}, bf16[2,320,256]{2,1,0:T(8,128)(2,1)S(1)}, u32[]{:S(2)}, u32[]{:S(2)}) collective-permute-start(bf16[2,320,256]{2,1,0:T(8,128)(2,1)} %get-tuple-element.16), channel_id=1, source_target_pairs={{0,8},{4,12},{8,0},{12,4},{1,9},{5,13},{9,1},{13,5},{2,10},{6,14},... | collective-permute-start | bytes 983048 | tf_op jit(solution)/shard_map/ppermute | solution.py:521
  16.7 22.6 %collective-permute-start.8 = (bf16[2,320,256]{2,1,0:T(8,128)(2,1)}, bf16[2,320,256]{2,1,0:T(8,128)(2,1)S(1)}, u32[]{:S(2)}, u32[]{:S(2)}) collective-permute-start(bf16[2,320,256]{2,1,0:T(8,128)(2,1)} %get-tuple-element.17), channel_id=1, source_target_pairs={{0,12},{4,0},{8,4},{12,8},{1,13},{5,1},{9,5},{13,9},{2,14},{6,2},{... | collective-permute-start | bytes 983048 | tf_op jit(solution)/shard_map/ppermute | solution.py:521
  56.3 3.6 %collective-permute-start.24 = (f32[2,2,64,256]{3,2,1,0:T(8,128)}, f32[2,2,64,256]{3,2,1,0:T(8,128)S(1)}, u32[]{:S(2)}, u32[]{:S(2)}) collective-permute-start(f32[2,2,64,256]{3,2,1,0:T(8,128)} %get-tuple-element.23), channel_id=1, source_target_pairs={{0,1},{1,0},{2,3},{3,2},{4,5},{5,4},{6,7},{7,6},{8,9},{9,8},{10,11... | collective-permute-start | bytes 786440 | tf_op jit(solution)/shard_map/ppermute | solution.py:525
  58.7 7.6 %collective-permute-start.26 = (f32[2,2,64,256]{3,2,1,0:T(8,128)S(1)}, f32[2,2,64,256]{3,2,1,0:T(8,128)S(1)}, u32[]{:S(2)}, u32[]{:S(2)}) collective-permute-start(f32[2,2,64,256]{3,2,1,0:T(8,128)S(1)} %add.72), channel_id=1, source_target_pairs={{0,2},{1,3},{2,0},{3,1},{4,6},{5,7},{6,4},{7,5},{8,10},{9,11},{10,... | collective-permute-start | bytes 786440 | tf_op jit(solution)/shard_map/ppermute | solution.py:525
  67.3 18.0 %collective-permute-start.27 = (f32[2,2,16,256]{3,2,1,0:T(8,128)S(1)}, f32[2,2,16,256]{3,2,1,0:T(8,128)S(1)}, u32[]{:S(2)}, u32[]{:S(2)}) collective-permute-start(f32[2,2,16,256]{3,2,1,0:T(8,128)S(1)} %get-tuple-element.26), channel_id=1, source_target_pairs={{0,4},{4,8},{8,12},{12,0},{1,5},{5,9},{9,13},{13,1},{2,6},{6,10},{... | collective-permute-start | bytes 196616 | tf_op jit(solution)/shard_map/ppermute | solution.py:521
  74.4 3.1 %collective-permute-start.3 = (s32[8,2]{1,0:T(8,128)S(1)}, s32[8,2]{1,0:T(8,128)S(1)}, u32[]{:S(2)}, u32[]{:S(2)}) collective-permute-start(s32[8,2]{1,0:T(8,128)S(1)} %pad_add_fusion.refs_0_), channel_id=1, source_target_pairs={{0,2},{1,3},{2,0},{3,1},{4,6},{5,7},{6,4},{7,5},{8,10},{9,11},{10,... | collective-permute-start | bytes 200 | tf_op jit(solution)/shard_map/ppermute | solution.py:525
  75.7 7.2 %collective-permute-start.4 = (s32[8,2]{1,0:T(8,128)S(1)}, s32[8,2]{1,0:T(8,128)S(1)}, u32[]{:S(2)}, u32[]{:S(2)}) collective-permute-start(s32[8,2]{1,0:T(8,128)S(1)} %pad_add_fusion.refs_0_), channel_id=1, source_target_pairs={{0,1},{1,0},{2,3},{3,2},{4,5},{5,4},{6,7},{7,6},{8,9},{9,8},{10,11... | collective-permute-start | bytes 200 | tf_op jit(solution)/shard_map/ppermute | solution.py:525
  77.5 5.4 %collective-permute-start.5 = (s32[8,2]{1,0:T(8,128)S(1)}, s32[8,2]{1,0:T(8,128)S(1)}, u32[]{:S(2)}, u32[]{:S(2)}) collective-permute-start(s32[8,2]{1,0:T(8,128)S(1)} %collective-permute-done.3.refs_1_), channel_id=1, source_target_pairs={{0,1},{1,0},{2,3},{3,2},{4,5},{5,4},{6,7},{7,6},{8,9},{9,8},{10,11... | collective-permute-start | bytes 200 | tf_op jit(solution)/shard_map/ppermute | solution.py:525
  79.6 23.0 %collective-permute-start.9 = (f32[2,320,256]{2,1,0:T(8,128)}, f32[2,320,256]{2,1,0:T(8,128)S(1)}, u32[]{:S(2)}, u32[]{:S(2)}) collective-permute-start(f32[2,320,256]{2,1,0:T(8,128)} %get-tuple-element.19), channel_id=1, source_target_pairs={{0,4},{4,8},{8,12},{12,0},{1,5},{5,9},{9,13},{13,1},{2,6},{6,10},{... | collective-permute-start | bytes 1966088 | tf_op jit(solution)/shard_map/ppermute | solution.py:521
  79.6 15.9 %collective-permute-start.29 = (f32[2,2,16,256]{3,2,1,0:T(8,128)S(1)}, f32[2,2,16,256]{3,2,1,0:T(8,128)S(1)}, u32[]{:S(2)}, u32[]{:S(2)}) collective-permute-start(f32[2,2,16,256]{3,2,1,0:T(8,128)S(1)} %get-tuple-element.27), channel_id=1, source_target_pairs={{0,12},{4,0},{8,4},{12,8},{1,13},{5,1},{9,5},{13,9},{2,14},{6,2},{... | collective-permute-start | bytes 196616 | tf_op jit(solution)/shard_map/ppermute | solution.py:521
  82.9 17.6 %collective-permute-start.28 = (f32[2,2,16,256]{3,2,1,0:T(8,128)S(1)}, f32[2,2,16,256]{3,2,1,0:T(8,128)}, u32[]{:S(2)}, u32[]{:S(2)}) collective-permute-start(f32[2,2,16,256]{3,2,1,0:T(8,128)S(1)} %get-tuple-element.28), channel_id=1, source_target_pairs={{0,8},{4,12},{8,0},{12,4},{1,9},{5,13},{9,1},{13,5},{2,10},{6,14},... | collective-permute-start | bytes 196616 | tf_op jit(solution)/shard_map/ppermute | solution.py:521
  82.9 49.8 %collective-permute-start.10 = (f32[2,320,256]{2,1,0:T(8,128)}, f32[2,320,256]{2,1,0:T(8,128)S(1)}, u32[]{:S(2)}, u32[]{:S(2)}) collective-permute-start(f32[2,320,256]{2,1,0:T(8,128)} %get-tuple-element.20), channel_id=1, source_target_pairs={{0,8},{4,12},{8,0},{12,4},{1,9},{5,13},{9,1},{13,5},{2,10},{6,14},... | collective-permute-start | bytes 1966088 | tf_op jit(solution)/shard_map/ppermute | solution.py:521
  85.9 46.9 %collective-permute-start.11 = (f32[2,320,256]{2,1,0:T(8,128)}, f32[2,320,256]{2,1,0:T(8,128)S(1)}, u32[]{:S(2)}, u32[]{:S(2)}) collective-permute-start(f32[2,320,256]{2,1,0:T(8,128)} %get-tuple-element.21), channel_id=1, source_target_pairs={{0,12},{4,0},{8,4},{12,8},{1,13},{5,1},{9,5},{13,9},{2,14},{6,2},{... | collective-permute-start | bytes 1966088 | tf_op jit(solution)/shard_map/ppermute | solution.py:521
  96.2 51.4 %collective-permute-start.16 = (f32[2,320,256]{2,1,0:T(8,128)}, f32[2,320,256]{2,1,0:T(8,128)S(1)}, u32[]{:S(2)}, u32[]{:S(2)}) collective-permute-start(f32[2,320,256]{2,1,0:T(8,128)} %get-tuple-element.18.refs_4_), channel_id=1, source_target_pairs={{0,1},{1,0},{2,3},{3,2},{4,5},{5,4},{6,7},{7,6},{8,9},{9,8},{10,11... | collective-permute-start | bytes 1966088 | tf_op jit(solution)/shard_map/ppermute | solution.py:525
  100.5 48.5 %collective-permute-start.12 = (f32[2,320,256]{2,1,0:T(8,128)}, f32[2,320,256]{2,1,0:T(8,128)S(1)}, u32[]{:S(2)}, u32[]{:S(2)}) collective-permute-start(f32[2,320,256]{2,1,0:T(8,128)} %get-tuple-element.18.refs_4_), channel_id=1, source_target_pairs={{0,2},{1,3},{2,0},{3,1},{4,6},{5,7},{6,4},{7,5},{8,10},{9,11},{10,... | collective-permute-start | bytes 1966088 | tf_op jit(solution)/shard_map/ppermute | solution.py:525
  102.7 47.5 %collective-permute-start.32 = (f32[2,2,16,256]{3,2,1,0:T(8,128)S(1)}, f32[2,2,16,256]{3,2,1,0:T(8,128)S(1)}, u32[]{:S(2)}, u32[]{:S(2)}) collective-permute-start(f32[2,2,16,256]{3,2,1,0:T(8,128)S(1)} %add_add_fusion.1.refs_20_), channel_id=1, source_target_pairs={{0,12},{4,0},{8,4},{12,8},{1,13},{5,1},{9,5},{13,9},{2,14},{6,2},{... | collective-permute-start | bytes 196616 | tf_op jit(solution)/shard_map/ppermute | solution.py:521
  132.8 17.8 %collective-permute-start.31 = (f32[2,2,16,256]{3,2,1,0:T(8,128)S(1)}, f32[2,2,16,256]{3,2,1,0:T(8,128)S(1)}, u32[]{:S(2)}, u32[]{:S(2)}) collective-permute-start(f32[2,2,16,256]{3,2,1,0:T(8,128)S(1)} %add_add_fusion.1.refs_20_), channel_id=1, source_target_pairs={{0,8},{4,12},{8,0},{12,4},{1,9},{5,13},{9,1},{13,5},{2,10},{6,14},... | collective-permute-start | bytes 196616 | tf_op jit(solution)/shard_map/ppermute | solution.py:521
  132.8 18.1 %collective-permute-start.30 = (f32[2,2,16,256]{3,2,1,0:T(8,128)S(1)}, f32[2,2,16,256]{3,2,1,0:T(8,128)S(1)}, u32[]{:S(2)}, u32[]{:S(2)}) collective-permute-start(f32[2,2,16,256]{3,2,1,0:T(8,128)S(1)} %add_add_fusion.1.refs_20_), channel_id=1, source_target_pairs={{0,4},{4,8},{8,12},{12,0},{1,5},{5,9},{9,13},{13,1},{2,6},{6,10},{... | collective-permute-start | bytes 196616 | tf_op jit(solution)/shard_map/ppermute | solution.py:521
  147.6 4.5 %collective-permute-start.17 = (f32[2,320,256]{2,1,0:T(8,128)S(1)}, f32[2,320,256]{2,1,0:T(8,128)S(1)}, u32[]{:S(2)}, u32[]{:S(2)}) collective-permute-start(f32[2,320,256]{2,1,0:T(8,128)S(1)} %collective-permute-done.9.refs_5_), channel_id=1, source_target_pairs={{0,1},{1,0},{2,3},{3,2},{4,5},{5,4},{6,7},{7,6},{8,9},{9,8},{10,11... | collective-permute-start | bytes 1966088 | tf_op jit(solution)/shard_map/ppermute | solution.py:525
  149.0 16.2 %collective-permute-start.13 = (f32[2,320,256]{2,1,0:T(8,128)S(1)}, f32[2,320,256]{2,1,0:T(8,128)S(1)}, u32[]{:S(2)}, u32[]{:S(2)}) collective-permute-start(f32[2,320,256]{2,1,0:T(8,128)S(1)} %collective-permute-done.9.refs_5_), channel_id=1, source_target_pairs={{0,2},{1,3},{2,0},{3,1},{4,6},{5,7},{6,4},{7,5},{8,10},{9,11},{10,... | collective-permute-start | bytes 1966088 | tf_op jit(solution)/shard_map/ppermute | solution.py:525
  150.2 16.5 %collective-permute-start.18 = (f32[2,320,256]{2,1,0:T(8,128)S(1)}, f32[2,320,256]{2,1,0:T(8,128)S(1)}, u32[]{:S(2)}, u32[]{:S(2)}) collective-permute-start(f32[2,320,256]{2,1,0:T(8,128)S(1)} %collective-permute-done.10.refs_6_), channel_id=1, source_target_pairs={{0,1},{1,0},{2,3},{3,2},{4,5},{5,4},{6,7},{7,6},{8,9},{9,8},{10,11... | collective-permute-start | bytes 1966088 | tf_op jit(solution)/shard_map/ppermute | solution.py:525
  150.6 28.7 %collective-permute-start.14 = (f32[2,320,256]{2,1,0:T(8,128)S(1)}, f32[2,320,256]{2,1,0:T(8,128)S(1)}, u32[]{:S(2)}, u32[]{:S(2)}) collective-permute-start(f32[2,320,256]{2,1,0:T(8,128)S(1)} %collective-permute-done.10.refs_6_), channel_id=1, source_target_pairs={{0,2},{1,3},{2,0},{3,1},{4,6},{5,7},{6,4},{7,5},{8,10},{9,11},{10,... | collective-permute-start | bytes 1966088 | tf_op jit(solution)/shard_map/ppermute | solution.py:525
  150.9 42.4 %collective-permute-start.15 = (f32[2,320,256]{2,1,0:T(8,128)S(1)}, f32[2,320,256]{2,1,0:T(8,128)S(1)}, u32[]{:S(2)}, u32[]{:S(2)}) collective-permute-start(f32[2,320,256]{2,1,0:T(8,128)S(1)} %collective-permute-done.11.refs_7_), channel_id=1, source_target_pairs={{0,2},{1,3},{2,0},{3,1},{4,6},{5,7},{6,4},{7,5},{8,10},{9,11},{10,... | collective-permute-start | bytes 1966088 | tf_op jit(solution)/shard_map/ppermute | solution.py:525
  152.1 42.2 %collective-permute-start.19 = (f32[2,320,256]{2,1,0:T(8,128)S(1)}, f32[2,320,256]{2,1,0:T(8,128)S(1)}, u32[]{:S(2)}, u32[]{:S(2)}) collective-permute-start(f32[2,320,256]{2,1,0:T(8,128)S(1)} %collective-permute-done.11.refs_7_), channel_id=1, source_target_pairs={{0,1},{1,0},{2,3},{3,2},{4,5},{5,4},{6,7},{7,6},{8,9},{9,8},{10,11... | collective-permute-start | bytes 1966088 | tf_op jit(solution)/shard_map/ppermute | solution.py:525
  165.2 29.0 %collective-permute-start.20 = (f32[2,320,256]{2,1,0:T(8,128)S(1)}, f32[2,320,256]{2,1,0:T(8,128)S(1)}, u32[]{:S(2)}, u32[]{:S(2)}) collective-permute-start(f32[2,320,256]{2,1,0:T(8,128)S(1)} %collective-permute-done.12.refs_8_), channel_id=1, source_target_pairs={{0,1},{1,0},{2,3},{3,2},{4,5},{5,4},{6,7},{7,6},{8,9},{9,8},{10,11... | collective-permute-start | bytes 1966088 | tf_op jit(solution)/shard_map/ppermute | solution.py:525
  166.7 27.6 %collective-permute-start.21 = (f32[2,320,256]{2,1,0:T(8,128)S(1)}, f32[2,320,256]{2,1,0:T(8,128)S(1)}, u32[]{:S(2)}, u32[]{:S(2)}) collective-permute-start(f32[2,320,256]{2,1,0:T(8,128)S(1)} %collective-permute-done.13.refs_9_), channel_id=1, source_target_pairs={{0,1},{1,0},{2,3},{3,2},{4,5},{5,4},{6,7},{7,6},{8,9},{9,8},{10,11... | collective-permute-start | bytes 1966088 | tf_op jit(solution)/shard_map/ppermute | solution.py:525
  179.3 15.1 %collective-permute-start.22 = (f32[2,320,256]{2,1,0:T(8,128)S(1)}, f32[2,320,256]{2,1,0:T(8,128)S(1)}, u32[]{:S(2)}, u32[]{:S(2)}) collective-permute-start(f32[2,320,256]{2,1,0:T(8,128)S(1)} %collective-permute-done.14.refs_10_), channel_id=1, source_target_pairs={{0,1},{1,0},{2,3},{3,2},{4,5},{5,4},{6,7},{7,6},{8,9},{9,8},{10,11... | collective-permute-start | bytes 1966088 | tf_op jit(solution)/shard_map/ppermute | solution.py:525
  193.3 3.2 %collective-permute-start.23 = (f32[2,320,256]{2,1,0:T(8,128)S(1)}, f32[2,320,256]{2,1,0:T(8,128)}, u32[]{:S(2)}, u32[]{:S(2)}) collective-permute-start(f32[2,320,256]{2,1,0:T(8,128)S(1)} %collective-permute-done.15.refs_11_), channel_id=1, source_target_pairs={{0,1},{1,0},{2,3},{3,2},{4,5},{5,4},{6,7},{7,6},{8,9},{9,8},{10,11... | collective-permute-start | bytes 1966088 | tf_op jit(solution)/shard_map/ppermute | solution.py:525
  (37 other events, 1403.8 us)
where the time goes:
time: 204 us; the launch traced here: 202 us
  starting transfers between devices  85.6 us (42%)
  waiting for transfers between devices  74 us (36%)
  Pallas kernels  24.2 us (12%)
  matrix products  6.61 us (3%)
  local copies, waits for them, and re-layouts  6.61 us (3%)
  other arithmetic  3.64 us (2%)
    ppermute x15, starting transfers between devices, shifted(): return lax.ppermute(x, axis, [(i, (i + k) % count) for i in range(count)])  66.7 us
    ppermute x18, waiting for transfers between devices, swapped(): return lax.ppermute(x, axis, [(i, i ^ bit) for i in range(count)])  44.6 us
    ppermute x15, waiting for transfers between devices, shifted(): return lax.ppermute(x, axis, [(i, (i + k) % count) for i in range(count)])  29.4 us
    ppermute x18, starting transfers between devices, swapped(): return lax.ppermute(x, axis, [(i, i ^ bit) for i in range(count)])  18.9 us
    pallas_call x1, Pallas kernels, per_device_packed(): pl.pallas_call(functools.partial(compute_kernel, tiles, pos_groups, win,...  15.5 us
    pallas_call x1, Pallas kernels, per_device_packed(): pl.pallas_call(functools.partial(place_kernel, tiles, pos_groups, win, sl...  5.22 us
    unnamed x72, local copies, waits for them, and re-layouts  4.9 us
  transfers between devices with their start and end apart: 33, of which 8 were waited for; matrix products, arithmetic and copies ran while one was open for 5% of the time, Pallas kernels for 0%

commit v1 on v0

--- a/solution.py
+++ b/solution.py
@@ -265,15 +265,44 @@
     ref[part, pl.ds(down, rows.shape[0]), :] = pltpu.roll(rows, start - down, 0)
 
 
+LEVELS = 32600.0
+CODE_UNIT = 256.0
+
+
+def code_of(peak):
+    return jnp.ceil(jnp.log(jnp.maximum(peak, 1e-30)) * (CODE_UNIT / math.log(2.0)))
+
+
+def step_of(code):
+    return jnp.exp(code * (math.log(2.0) / CODE_UNIT)) * (1.0 / LEVELS)
+
+
+def column_peak(x):
+    return jnp.max(jnp.abs(x), axis=0, keepdims=True)
+
+
+def to_levels(x, code):
+    return jnp.floor(x * (1.0 / step_of(code)) + 0.5).astype(jnp.int32).astype(jnp.int16)
+
+
+def code_rows(codes):
+    rest = jnp.zeros((16 - len(codes), codes[0].shape[1]), jnp.float32)
+    return jnp.concatenate(codes + [rest], axis=0).astype(jnp.int32).astype(jnp.int16)
+
+
+def wide_of(x):
+    return x.astype(jnp.int32).astype(jnp.float32)
+
+
 def compute_kernel(tiles, pos_groups, win, modes, grad_scale, me_ref, owner_ref, off_ref, *refs):
     packs = refs[:tiles]
     probe, amp, prop_re, prop_im, prop_t_re, prop_t_im, spot_ref = refs[tiles : tiles + 7]
     grads = refs[tiles + 7 : 2 * tiles + 7]
-    pieces = refs[2 * tiles + 7 : 2 * tiles + 7 + pos_groups]
+    away_ref, kept_ref = refs[2 * tiles + 7 : 2 * tiles + 9]
     (
         held, cat, wins, far, factor, right_a, right_b, left_a, left_b, obj_acc, probe_acc, gcat, outer_acc, gpack,
         in_sem, out_sem, piece_sem,
-    ) = refs[2 * tiles + 7 + pos_groups :]
+    ) = refs[2 * tiles + 9 :]
     half = win // 2
     quarter = win // 4
     me = me_ref[0]
@@ -383,10 +412,9 @@
     piece_copies = []
     for j in range(pos_groups):
         start = pl.multiple_of(jnp.bitwise_xor(spot, j) * share, share)
+        home = (away_ref if j % 2 else kept_ref).at[j // 2]
         piece_copies.append(
-            pltpu.make_async_copy(
-                probe_acc.at[:, :, pl.ds(start, share), :], pieces[j], piece_sem.at[j]
-            )
+            pltpu.make_async_copy(probe_acc.at[:, :, pl.ds(start, share), :], home, piece_sem.at[j])
         )
         piece_copies[-1].start()
 
@@ -401,12 +429,20 @@
         rows_to(gcat, part, rem, [obj_acc[0, part], obj_acc[1, part, half:win, :]])
         rows_to(outer_acc, part, low_rem, [jnp.where(right, low_b, low_a)])
         outer = outer_acc[part, 0:half, :] + outer_acc[part, half:win, :]
+        outer_code = code_of(column_peak(outer))
+        outer_levels = to_levels(outer, outer_code)
         for d in range(3):
-            gpack[d, part, 0:win, :] = gcat[part, d * win : (d + 1) * win, :]
+            codes = []
+            for level in range(2):
+                rows = gcat[part, d * win + level * half : d * win + (level + 1) * half, :]
+                codes.append(code_of(column_peak(rows)))
+                gpack[d, part, level * half : (level + 1) * half, :] = to_levels(rows, codes[-1])
             for chunk in range(2):
-                gpack[d, part, win : win + quarter, half * chunk : half * (chunk + 1)] = outer[
+                gpack[d, part, win : win + quarter, half * chunk : half * (chunk + 1)] = outer_levels[
                     chunk * quarter : (chunk + 1) * quarter, :
                 ]
+            codes.append(jnp.concatenate([outer_code, outer_code], axis=1))
+            gpack[d, part, win + quarter : win + quarter + 16, :] = code_rows(codes)
     grad_copies = []
     for k in range(tiles):
         there = strip_held(owner_ref, lax.rem(me + k, tiles), tiles)
@@ -417,13 +453,24 @@
         copy.wait()
 
 
+def probe_pack_kernel(blocks, rows, kept_ref, came_ref, total_ref, pack_ref):
+    codes = []
+    for b in range(blocks):
+        total = kept_ref[b] + came_ref[b]
+        total_ref[b] = total
+        codes.append(code_of(column_peak(total)))
+        pack_ref[b * rows : (b + 1) * rows, :] = to_levels(total, codes[-1])
+    pack_ref[blocks * rows : blocks * rows + 16, :] = code_rows(codes)
+
+
 def place_kernel(tiles, pos_groups, win, slab, me_ref, spot_ref, owner_ref, *refs):
     count = tiles * pos_groups
     offs = refs[:pos_groups]
     packs = refs[pos_groups : pos_groups + count]
-    parts_in = refs[pos_groups + count : pos_groups + count + tiles]
+    probe_own = refs[pos_groups + count]
+    probe_packs = refs[pos_groups + count + 1 : pos_groups + count + tiles]
     out_ref, probe_ref = refs[pos_groups + count + tiles : pos_groups + count + tiles + 2]
-    held, acc, probe_acc, params, in_sem, out_sem, part_sem = refs[pos_groups + count + tiles + 2 :]
+    held, acc, params, in_sem, out_sem = refs[pos_groups + count + tiles + 2 :]
     half = win // 2
     quarter = win // 4
     me = me_ref[0]
@@ -432,18 +479,6 @@
     first_col = spot_ref[0] * slab
     margin = 2 * win
     span = 3 * half
-    rows_each = probe_acc.shape[2] // tiles
-    part_copies = []
-    for k in range(tiles):
-        turn = lax.rem(me + tiles - k, tiles)
-        start = pl.multiple_of(turn * rows_each, rows_each)
-        part_copies.append(
-            pltpu.make_async_copy(
-                parts_in[k], probe_acc.at[:, :, pl.ds(start, rows_each), :], part_sem.at[k]
-            )
-        )
-        part_copies[-1].start()
-
     for n in range(count):
         j, k = n // tiles, n % tiles
         off = offs[j]
@@ -464,10 +499,13 @@
         return carry
 
     lax.fori_loop(0, win // 8, clear, 0)
-    for copy in part_copies:
-        copy.wait()
-    probe_out = pltpu.make_async_copy(probe_acc, probe_ref, part_sem.at[tiles])
-    probe_out.start()
+    blocks, rows_each = probe_own.shape[0], probe_own.shape[1]
+    scales = [step_of(wide_of(pk[blocks * rows_each : blocks * rows_each + 16, :])) for pk in probe_packs]
+    for b in range(blocks):
+        total = probe_own[b]
+        for pk, scale in zip(probe_packs, scales):
+            total = total + wide_of(pk[b * rows_each : (b + 1) * rows_each, :]) * scale[b : b + 1, :]
+        probe_ref[b] = total
 
     def one(n, carry):
         @pl.when(params[n, 0] == 1)
@@ -482,15 +520,18 @@
             stay = lanes >= rem
 
             for part in range(2):
+                steps = step_of(wide_of(held[n, part, win + quarter : win + quarter + 16, :]))
                 for chunk in range(4):
                     row0 = chunk * quarter
+                    level = chunk // 2
                     rows = base + row0 + row_iota((quarter, half))
                     low_first = (rows < y_up + win).astype(jnp.int32) == right
                     in_outer = (rows >= y_up + half) & (rows < y_up + win)
-                    m0 = held[n, part, row0 : row0 + quarter, 0:half]
-                    m1 = held[n, part, row0 : row0 + quarter, half:win]
+                    main = wide_of(held[n, part, row0 : row0 + quarter, :]) * steps[level : level + 1, :]
+                    m0 = main[:, 0:half]
+                    m1 = main[:, half:win]
                     side = held[n, part, win : win + quarter, half * (chunk % 2) : half * (chunk % 2 + 1)]
-                    side = jnp.where(in_outer, side, 0.0)
+                    side = jnp.where(in_outer, wide_of(side) * steps[2:3, 0:half], 0.0)
                     cols = [
                         jnp.where(low_first, m0, jnp.where(right == 0, side, 0.0)),
                         jnp.where(low_first, m1, m0),
@@ -514,7 +555,6 @@
     out = pltpu.make_async_copy(acc.at[:, :, margin : margin + slab], out_ref, out_sem)
     out.start()
     out.wait()
-    probe_out.wait()
 
 
 def shifted(x, axis, count, k):
@@ -541,6 +581,8 @@
     vmem = pl.BlockSpec(memory_space=pltpu.VMEM)
     anywhere = pl.BlockSpec(memory_space=pl.ANY)
     pack_shape = (2, win + quarter, win)
+    grad_shape = (2, win + quarter + 16, win)
+    share = win // pos_groups
 
     offs = [offsets] + [shifted(offsets, "tile", tiles, tiles - k) for k in range(1, tiles)]
     packs = pl.pallas_call(
@@ -561,10 +603,10 @@
     prop_re, prop_im = build_propagator(chirp)
     results = pl.pallas_call(
         functools.partial(compute_kernel, tiles, pos_groups, win, modes, grad_scale),
-        out_shape=[jax.ShapeDtypeStruct(pack_shape, jnp.float32)] * tiles
-        + [jax.ShapeDtypeStruct((modes, 2, win // pos_groups, win), jnp.float32)] * pos_groups,
+        out_shape=[jax.ShapeDtypeStruct(grad_shape, jnp.int16)] * tiles
+        + [jax.ShapeDtypeStruct((pos_groups // 2, modes, 2, share, win), jnp.float32)] * 2,
         in_specs=[smem] * 3 + [anywhere] * tiles + [vmem] * 6 + [smem],
-        out_specs=[anywhere] * (tiles + pos_groups),
+        out_specs=[anywhere] * (tiles + 2),
         scratch_shapes=[
             pltpu.VMEM((tiles,) + pack_shape, jnp.bfloat16),
             pltpu.VMEM((2, 3 * win, win), jnp.float32),
@@ -579,14 +621,14 @@
             pltpu.VMEM((modes, 2, win, win), jnp.float32),
             pltpu.VMEM((2, 3 * win, win), jnp.float32),
             pltpu.VMEM((2, win, half), jnp.float32),
-            pltpu.VMEM((3,) + pack_shape, jnp.float32),
+            pltpu.VMEM((3,) + grad_shape, jnp.int16),
             pltpu.SemaphoreType.DMA((tiles,)),
             pltpu.SemaphoreType.DMA((tiles,)),
             pltpu.SemaphoreType.DMA((pos_groups,)),
         ],
         name="propagate",
     )(me, strip_owner, offsets, *arrived, probe, amplitude, prop_re, prop_im, prop_re.T, prop_im.T, spot)
-    grads, pieces = results[:tiles], list(results[tiles:])
+    grads, (away, kept) = results[:tiles], results[tiles:]
 
     column = [grads[0]] + [shifted(grads[k], "tile", tiles, k) for k in range(1, tiles)]
     column_offs = [jnp.concatenate([offs[(tiles - k) % tiles] for k in range(tiles)], axis=0)]
@@ -597,19 +639,22 @@
         column_offs = column_offs + [swapped(o, "pos", pos_groups, bit) for o in column_offs]
         bit //= 2
 
-    bit = 1
-    while len(pieces) > 1:
-        pieces = [
-            pieces[j] + swapped(pieces[j + 1], "pos", pos_groups, bit) for j in range(0, len(pieces), 2)
-        ]
+    kept = kept + swapped(away, "pos", pos_groups, 1)
+    bit = 2
+    while kept.shape[0] > 2:
+        kept = kept[0::2] + swapped(kept[1::2], "pos", pos_groups, bit)
         bit *= 2
-    mine = pieces[0]
-    each = mine.shape[2] // tiles
-    total = lax.dynamic_slice_in_dim(mine, me[0] * each, each, 2)
-    for k in range(1, tiles):
-        sent = lax.dynamic_slice_in_dim(mine, lax.rem(me[0] + k, tiles) * each, each, 2)
-        total = total + shifted(sent, "tile", tiles, k)
-    totals = [total] + [shifted(total, "tile", tiles, k) for k in range(1, tiles)]
+    blocks = modes * 2
+    came = swapped(kept[1], "pos", pos_groups, bit)
+    probe_own, probe_pack = pl.pallas_call(
+        functools.partial(probe_pack_kernel, blocks, share),
+        out_shape=[
+            jax.ShapeDtypeStruct((blocks, share, win), jnp.float32),
+            jax.ShapeDtypeStruct((blocks * share + 16, win), jnp.int16),
+        ],
+        name="probe_pack",
+    )(kept[0].reshape(blocks, share, win), came.reshape(blocks, share, win))
+    probe_packs = [shifted(probe_pack, "tile", tiles, k) for k in range(1, tiles)]
 
     flat = [x for c in columns for x in c]
     count = len(flat)
@@ -617,22 +662,20 @@
         functools.partial(place_kernel, tiles, pos_groups, win, slab),
         out_shape=[
             jax.ShapeDtypeStruct((2, win, slab), jnp.float32),
-            jax.ShapeDtypeStruct((modes, 2, win // pos_groups, win), jnp.float32),
+            jax.ShapeDtypeStruct((blocks, share, win), jnp.float32),
         ],
-        in_specs=[smem] * (3 + pos_groups) + [anywhere] * (count + tiles),
-        out_specs=[anywhere, anywhere],
+        in_specs=[smem] * (3 + pos_groups) + [anywhere] * count + [vmem] * tiles,
+        out_specs=[anywhere, vmem],
         scratch_shapes=[
-            pltpu.VMEM((count,) + pack_shape, jnp.float32),
+            pltpu.VMEM((count,) + grad_shape, jnp.int16),
             pltpu.VMEM((2, win, slab + 4 * win), jnp.float32),
-            pltpu.VMEM((modes, 2, win // pos_groups, win), jnp.float32),
             pltpu.SMEM((count, 4), jnp.int32),
             pltpu.SemaphoreType.DMA((count,)),
             pltpu.SemaphoreType.DMA,
-            pltpu.SemaphoreType.DMA((tiles + 1,)),
         ],
         name="place",
-    )(me, spot, strip_owner, *column_offs, *flat, *totals)
-    return (strip_part, probe_out)
+    )(me, spot, strip_owner, *column_offs, *flat, probe_own, *probe_packs)
+    return (strip_part, probe_out.reshape(modes, 2, share, win))
 
 
 def per_device(object_field, probe, amplitude, offsets, strip_owner, chirp):
@@ -647,7 +690,8 @@
         and pos_groups & (pos_groups - 1) == 0
         and width // pos_groups >= 2 * win
         and (width // pos_groups) % 128 == 0
-        and (win // pos_groups) % (8 * tiles) == 0
+        and pos_groups >= 4
+        and (win // pos_groups) % 16 == 0
     )
     plan = per_device_packed if packed else per_device_general
     return plan(object_field, probe, amplitude, offsets, strip_owner, chirp)

time: 204 us -> 149 us (0.73)
  starting transfers between devices: 85.6 us -> 44.5 us
  waiting for transfers between devices: 74 us -> 62.8 us
    ppermute x15 -> x12, starting transfers between devices: 66.7 us -> 27.3 us  [shifted(): return lax.ppermute(x, axis, [(i, (i + k) % count) for i in range(count)])]
    ppermute x18 -> x17, waiting for transfers between devices: 44.6 us -> 19.9 us  [swapped(): return lax.ppermute(x, axis, [(i, i ^ bit) for i in range(count)])]
    ppermute x15 -> x12, waiting for transfers between devices: 29.4 us -> 43 us  [shifted(): return lax.ppermute(x, axis, [(i, (i + k) % count) for i in range(count)])]
    unnamed x72 -> x58, local copies, waits for them, and re-layouts: 4.9 us -> 2.21 us
    ppermute x18 -> x17, starting transfers between devices: 18.9 us -> 17.2 us  [swapped(): return lax.ppermute(x, axis, [(i, i ^ bit) for i in range(count)])]
  transfers between devices with their start and end apart: 33 -> 29, of which waited for: 8 -> 10; matrix products, arithmetic and copies ran while one was open for 5% -> 7% of each run, Pallas kernels for 0% -> 1%
where the time goes in v1:
time: 149 us; the launch traced here: 147 us
  waiting for transfers between devices  62.8 us (42%)
  starting transfers between devices  44.5 us (30%)
  Pallas kernels  25.7 us (17%)
  matrix products  6.61 us (4%)
  local copies, waits for them, and re-layouts  4.61 us (3%)
  other arithmetic  1.84 us (1%)
    ppermute x12, waiting for transfers between devices, shifted(): return lax.ppermute(x, axis, [(i, (i + k) % count) for i in range(count)])  43 us
    ppermute x12, starting transfers between devices, shifted(): return lax.ppermute(x, axis, [(i, (i + k) % count) for i in range(count)])  27.3 us
    ppermute x17, waiting for transfers between devices, swapped(): return lax.ppermute(x, axis, [(i, i ^ bit) for i in range(count)])  19.9 us
    ppermute x17, starting transfers between devices, swapped(): return lax.ppermute(x, axis, [(i, i ^ bit) for i in range(count)])  17.2 us
    pallas_call x1, Pallas kernels, per_device_packed(): pl.pallas_call(functools.partial(compute_kernel, tiles, pos_groups, win,...  15.4 us
    pallas_call x1, Pallas kernels, per_device_packed(): pl.pallas_call(functools.partial(place_kernel, tiles, pos_groups, win, sl...  4.91 us
    pallas_call x1, Pallas kernels, per_device_packed(): pl.pallas_call(functools.partial(pack_kernel, tiles, win, width), out_sha...  3.54 us
  transfers between devices with their start and end apart: 29, of which 10 were waited for; matrix products, arithmetic and copies ran while one was open for 7% of the time, Pallas kernels for 1%

profile of v1, /device:TPU:1, one launch (start us, length us, event | category | flops | bytes accessed | tf_op | source)
XLA Modules:
  0.0 147.2 jit_solution(2336844399457081713)
XLA Ops:
  0.6 4.2 %collective-permute-start.2 = (s32[2,2]{1,0:T(2,128)}, s32[2,2]{1,0:T(2,128)S(1)}, u32[]{:S(2)}, u32[]{:S(2)}) collective-permute-start(s32[2,2]{1,0:T(2,128)} %off_ref.1), channel_id=1, source_target_pairs={{0,12},{4,0},{8,4},{12,8},{1,13},{5,1},{9,5},{13,9},{2,14},{6,2},{... | collective-permute-start | bytes 56 | tf_op jit(solution)/shard_map/ppermute | solution.py:561
  6.0 1.7 %fusion.8 = f32[256,256]{0,1:T(8,128)S(1)} fusion(f32[256]{0:T(256)S(1)} %get-tuple-element.33, f32[256]{0:T(256)S(1)} %get-tuple-element.32), kind=kOutput, calls=%fused_computation.17 | convolution fusion | flops 203489280 | bytes 264192 | tf_op jit(solution)/shard_map/dot_general | solution.py:33
  7.7 1.7 %convolution_subtract_fusion = f32[256,256]{0,1:T(8,128)S(1)} fusion(f32[256,256]{0,1:T(8,128)S(1)} %fusion.8, f32[256]{0:T(256)S(1)} %get-tuple-element.33, f32[256]{0:T(256)S(1)} %get-tuple-element.32), kind=kOutput, calls=%fused_computation | convolution fusion | flops 203620352 | bytes 526336 | tf_op jit(solution)/shard_map/dot_general | solution.py:33
  10.0 3.5 %pack.1 = (bf16[2,320,256]{2,1,0:T(8,128)(2,1)}, bf16[2,320,256]{2,1,0:T(8,128)(2,1)}, bf16[2,320,256]{2,1,0:T(8,128)(2,1)}, bf16[2,320,256]{2,1,0:T(8,128)(2,1)}) custom-call(s32[1]{0:T(128)} %bitcast.me_ref, s32[4]{0:T(128)} %owner_ref.5, s32[2,2]{1,0:T(2,128)} %off_ref.1, s32[2,2]{1,0:T(2,128)} %copy-done.23, s32[2,2]{1,0:T(2,128)} %copy-done.25, ...), custom_call_target="tpu_custom_call" | custom-call | tf_op jit(solution)/shard_map/pack/pallas_call | solution.py:588
  13.5 2.2 %collective-permute-start.6 = (bf16[2,320,256]{2,1,0:T(8,128)(2,1)}, bf16[2,320,256]{2,1,0:T(8,128)(2,1)S(1)}, u32[]{:S(2)}, u32[]{:S(2)}) collective-permute-start(bf16[2,320,256]{2,1,0:T(8,128)(2,1)} %get-tuple-element.17), channel_id=1, source_target_pairs={{0,4},{4,8},{8,12},{12,0},{1,5},{5,9},{9,13},{13,1},{2,6},{6,10},{... | collective-permute-start | bytes 983048 | tf_op jit(solution)/shard_map/ppermute | solution.py:561
  16.7 1.3 collective-permute-start.8
  18.0 1.7 %fusion.10 = f32[256,256]{0,1:T(8,128)S(1)} fusion(f32[256]{0:T(256)S(1)} %get-tuple-element.33, f32[256]{0:T(256)S(1)} %get-tuple-element.32), kind=kOutput, calls=%fused_computation.19 | convolution fusion | flops 203489280 | bytes 264192 | tf_op jit(solution)/shard_map/dot_general | solution.py:30
  20.5 1.6 %convolution_add_fusion = f32[256,256]{0,1:T(8,128)S(1)} fusion(f32[256,256]{0,1:T(8,128)S(1)} %fusion.10, f32[256]{0:T(256)S(1)} %get-tuple-element.33, f32[256]{0:T(256)S(1)} %get-tuple-element.32), kind=kOutput, calls=%fused_computation.1 | convolution fusion | flops 203620352 | bytes 526336 | tf_op jit(solution)/shard_map/dot_general | solution.py:30
  23.0 16.3 %collective-permute-done.7.refs_2_ = bf16[2,320,256]{2,1,0:T(8,128)(2,1)S(1)} collective-permute-done((bf16[2,320,256]{2,1,0:T(8,128)(2,1)}, bf16[2,320,256]{2,1,0:T(8,128)(2,1)S(1)}, u32[]{:S(2)}, u32[]{:S(2)}) %collective-permute-start.7) | collective-permute-done | bytes 327712 | tf_op jit(solution)/shard_map/ppermute | solution.py:561
  40.2 15.4 %propagate.1 = (s16[2,336,256]{2,1,0:T(8,128)(2,1)}, s16[2,336,256]{2,1,0:T(8,128)(2,1)}, s16[2,336,256]{2,1,0:T(8,128)(2,1)}, s16[2,336,256]{2,1,0:T(8,128)(2,1...) custom-call(s32[1]{0:T(128)} %bitcast.me_ref, s32[4]{0:T(128)} %owner_ref.5, s32[2,2]{1,0:T(2,128)} %off_ref.1, ...), custom_call_target="tpu_custom_call" | custom-call | tf_op jit(solution)/shard_map/propagate/pallas_call | solution.py:604
  55.6 7.3 %collective-permute-start.9 = (s16[2,336,256]{2,1,0:T(8,128)(2,1)}, s16[2,336,256]{2,1,0:T(8,128)(2,1)S(1)}, u32[]{:S(2)}, u32[]{:S(2)}) collective-permute-start(s16[2,336,256]{2,1,0:T(8,128)(2,1)} %get-tuple-element.21), channel_id=1, source_target_pairs={{0,4},{4,8},{8,12},{12,0},{1,5},{5,9},{9,13},{13,1},{2,6},{6,10},{... | collective-permute-start | bytes 1032200 | tf_op jit(solution)/shard_map/ppermute | solution.py:561
  62.9 2.1 %collective-permute-start.24 = (f32[2,2,2,64,256]{4,3,2,1,0:T(8,128)}, f32[2,2,2,64,256]{4,3,2,1,0:T(8,128)S(1)}, u32[]{:S(2)}, u32[]{:S(2)}) collective-permute-start(f32[2,2,2,64,256]{4,3,2,1,0:T(8,128)} %get-tuple-element.25), channel_id=1, source_target_pairs={{0,1},{1,0},{2,3},{3,2},{4,5},{5,4},{6,7},{7,6},{8,9},{9,8},{10,11... | collective-permute-start | bytes 1572872 | tf_op jit(solution)/shard_map/ppermute | solution.py:565
  65.1 1.3 collective-permute-start.3
  66.7 1.2 collective-permute-done.3.refs_1_
  70.1 1.2 collective-permute-start.12
  71.3 14.3 %collective-permute-done.10.refs_6_ = s16[2,336,256]{2,1,0:T(8,128)(2,1)S(1)} collective-permute-done((s16[2,336,256]{2,1,0:T(8,128)(2,1)}, s16[2,336,256]{2,1,0:T(8,128)(2,1)S(1)}, u32[]{:S(2)}, u32[]{:S(2)}) %collective-permute-start.10) | collective-permute-done | bytes 344096 | tf_op jit(solution)/shard_map/ppermute | solution.py:561
  86.2 1.3 collective-permute-start.13
  87.5 1.1 add.35
  89.7 1.3 collective-permute-start.15
  91.7 4.1 %collective-permute-done.13.refs_9_ = s16[2,336,256]{2,1,0:T(8,128)(2,1)S(1)} collective-permute-done((s16[2,336,256]{2,1,0:T(8,128)(2,1)S(1)}, s16[2,336,256]{2,1,0:T(8,128)(2,1)S(1)}, u32[]{:S(2)}, u32[]{:S(2)}) %collective-permute-start.13) | collective-permute-done | bytes 344096 | tf_op jit(solution)/shard_map/ppermute | solution.py:565
  95.7 1.3 collective-permute-start.25
  97.0 1.7 %collective-permute-start.20 = (s16[2,336,256]{2,1,0:T(8,128)(2,1)S(1)}, s16[2,336,256]{2,1,0:T(8,128)(2,1)}, u32[]{:S(2)}, u32[]{:S(2)}) collective-permute-start(s16[2,336,256]{2,1,0:T(8,128)(2,1)S(1)} %collective-permute-done.12.refs_8_), channel_id=1, source_target_pairs={{0,1},{1,0},{2,3},{3,2},{4,5},{5,4},{6,7},{7,6},{8,9},{9,8},{10,11... | collective-permute-start | bytes 1032200 | tf_op jit(solution)/shard_map/ppermute | solution.py:565
  98.7 4.4 %collective-permute-done.14.refs_10_ = s16[2,336,256]{2,1,0:T(8,128)(2,1)S(1)} collective-permute-done((s16[2,336,256]{2,1,0:T(8,128)(2,1)S(1)}, s16[2,336,256]{2,1,0:T(8,128)(2,1)S(1)}, u32[]{:S(2)}, u32[]{:S(2)}) %collective-permute-start.14) | collective-permute-done | bytes 344096 | tf_op jit(solution)/shard_map/ppermute | solution.py:565
  103.1 1.5 collective-permute-start.21
  104.6 6.0 %collective-permute-done.15.refs_11_ = s16[2,336,256]{2,1,0:T(8,128)(2,1)} collective-permute-done((s16[2,336,256]{2,1,0:T(8,128)(2,1)S(1)}, s16[2,336,256]{2,1,0:T(8,128)(2,1)}, u32[]{:S(2)}, u32[]{:S(2)}) %collective-permute-start.15) | collective-permute-done | bytes 344096 | tf_op jit(solution)/shard_map/ppermute | solution.py:565
  110.6 1.5 collective-permute-start.22
  112.0 4.2 %collective-permute-done.25 = f32[2,2,64,256]{3,2,1,0:T(8,128)} collective-permute-done((f32[2,2,64,256]{3,2,1,0:T(8,128)S(1)}, f32[2,2,64,256]{3,2,1,0:T(8,128)}, u32[]{:S(2)}, u32[]{:S(2)}) %collective-permute-start.25) | collective-permute-done | bytes 262176 | tf_op jit(solution)/shard_map/ppermute | solution.py:565
  117.1 1.8 %probe_pack.1 = (f32[4,64,256]{2,1,0:T(8,128)}, s16[272,256]{1,0:T(8,128)(2,1)}) custom-call(f32[4,64,256]{2,1,0:T(8,128)} %bitcast.11, f32[4,64,256]{2,1,0:T(8,128)} %bitcast.6.came_ref), custom_call_target="tpu_custom_call" | custom-call | tf_op jit(solution)/shard_map/probe_pack/pallas_call | solution.py:649
  118.9 10.2 %collective-permute-start.28 = (s16[272,256]{1,0:T(8,128)(2,1)}, s16[272,256]{1,0:T(8,128)(2,1)S(1)}, u32[]{:S(2)}, u32[]{:S(2)}) collective-permute-start(s16[272,256]{1,0:T(8,128)(2,1)} %get-tuple-element.27), channel_id=1, source_target_pairs={{0,12},{4,0},{8,4},{12,8},{1,13},{5,1},{9,5},{13,9},{2,14},{6,2},{... | collective-permute-start | bytes 417800 | tf_op jit(solution)/shard_map/ppermute | solution.py:561
  129.1 3.4 %collective-permute-done.28.refs_23_ = s16[272,256]{1,0:T(8,128)(2,1)S(1)} collective-permute-done((s16[272,256]{1,0:T(8,128)(2,1)}, s16[272,256]{1,0:T(8,128)(2,1)S(1)}, u32[]{:S(2)}, u32[]{:S(2)}) %collective-permute-start.28) | collective-permute-done | bytes 139296 | tf_op jit(solution)/shard_map/ppermute | solution.py:561
  132.5 8.8 %collective-permute-done.27.refs_22_ = s16[272,256]{1,0:T(8,128)(2,1)S(1)} collective-permute-done((s16[272,256]{1,0:T(8,128)(2,1)}, s16[272,256]{1,0:T(8,128)(2,1)S(1)}, u32[]{:S(2)}, u32[]{:S(2)}) %collective-permute-start.27) | collective-permute-done | bytes 139296 | tf_op jit(solution)/shard_map/ppermute | solution.py:561
  142.1 4.9 %place.1 = (f32[2,256,1024]{2,1,0:T(8,128)}, f32[4,64,256]{2,1,0:T(8,128)}) custom-call(s32[1]{0:T(128)} %bitcast.me_ref, s32[1]{0:T(128)} %bitcast.1.refs_10_.spot_ref, s32[4]{0:T(128)} %owner_ref.5, s32[8,2]{1,0:T(8,128)} %copy-done.18, s32[8,2]{1,0:T(8,128)} %copy-done.20, s32[8,2]{1,0:T(8,128)} %copy-done.21, s32[8,2]{1,0:T(8,128)} %copy-done.22, ...), custom_call_target="tpu_custom_call" | custom-call | tf_op jit(solution)/shard_map/place/pallas_call | solution.py:661
  (98 shorter events, 11.9 us)
Async XLA Ops:
  0.6 8.7 %collective-permute-start.2 = (s32[2,2]{1,0:T(2,128)}, s32[2,2]{1,0:T(2,128)S(1)}, u32[]{:S(2)}, u32[]{:S(2)}) collective-permute-start(s32[2,2]{1,0:T(2,128)} %off_ref.1), channel_id=1, source_target_pairs={{0,12},{4,0},{8,4},{12,8},{1,13},{5,1},{9,5},{13,9},{2,14},{6,2},{... | collective-permute-start | bytes 56 | tf_op jit(solution)/shard_map/ppermute | solution.py:561
  4.8 4.5 %collective-permute-start.1 = (s32[2,2]{1,0:T(2,128)}, s32[2,2]{1,0:T(2,128)S(1)}, u32[]{:S(2)}, u32[]{:S(2)}) collective-permute-start(s32[2,2]{1,0:T(2,128)} %off_ref.1), channel_id=1, source_target_pairs={{0,8},{4,12},{8,0},{12,4},{1,9},{5,13},{9,1},{13,5},{2,10},{6,14},... | collective-permute-start | bytes 56 | tf_op jit(solution)/shard_map/ppermute | solution.py:561
  4.8 4.5 %collective-permute-start = (s32[2,2]{1,0:T(2,128)}, s32[2,2]{1,0:T(2,128)S(1)}, u32[]{:S(2)}, u32[]{:S(2)}) collective-permute-start(s32[2,2]{1,0:T(2,128)} %off_ref.1), channel_id=1, source_target_pairs={{0,4},{4,8},{8,12},{12,0},{1,5},{5,9},{9,13},{13,1},{2,6},{6,10},{... | collective-permute-start | bytes 56 | tf_op jit(solution)/shard_map/ppermute | solution.py:561
  13.5 9.5 %collective-permute-start.6 = (bf16[2,320,256]{2,1,0:T(8,128)(2,1)}, bf16[2,320,256]{2,1,0:T(8,128)(2,1)S(1)}, u32[]{:S(2)}, u32[]{:S(2)}) collective-permute-start(bf16[2,320,256]{2,1,0:T(8,128)(2,1)} %get-tuple-element.17), channel_id=1, source_target_pairs={{0,4},{4,8},{8,12},{12,0},{1,5},{5,9},{9,13},{13,1},{2,6},{6,10},{... | collective-permute-start | bytes 983048 | tf_op jit(solution)/shard_map/ppermute | solution.py:561
  15.8 23.5 %collective-permute-start.7 = (bf16[2,320,256]{2,1,0:T(8,128)(2,1)}, bf16[2,320,256]{2,1,0:T(8,128)(2,1)S(1)}, u32[]{:S(2)}, u32[]{:S(2)}) collective-permute-start(bf16[2,320,256]{2,1,0:T(8,128)(2,1)} %get-tuple-element.18), channel_id=1, source_target_pairs={{0,8},{4,12},{8,0},{12,4},{1,9},{5,13},{9,1},{13,5},{2,10},{6,14},... | collective-permute-start | bytes 983048 | tf_op jit(solution)/shard_map/ppermute | solution.py:561
  16.7 22.6 %collective-permute-start.8 = (bf16[2,320,256]{2,1,0:T(8,128)(2,1)}, bf16[2,320,256]{2,1,0:T(8,128)(2,1)S(1)}, u32[]{:S(2)}, u32[]{:S(2)}) collective-permute-start(bf16[2,320,256]{2,1,0:T(8,128)(2,1)} %get-tuple-element.19), channel_id=1, source_target_pairs={{0,12},{4,0},{8,4},{12,8},{1,13},{5,1},{9,5},{13,9},{2,14},{6,2},{... | collective-permute-start | bytes 983048 | tf_op jit(solution)/shard_map/ppermute | solution.py:561
  55.6 14.5 %collective-permute-start.9 = (s16[2,336,256]{2,1,0:T(8,128)(2,1)}, s16[2,336,256]{2,1,0:T(8,128)(2,1)S(1)}, u32[]{:S(2)}, u32[]{:S(2)}) collective-permute-start(s16[2,336,256]{2,1,0:T(8,128)(2,1)} %get-tuple-element.21), channel_id=1, source_target_pairs={{0,4},{4,8},{8,12},{12,0},{1,5},{5,9},{9,13},{13,1},{2,6},{6,10},{... | collective-permute-start | bytes 1032200 | tf_op jit(solution)/shard_map/ppermute | solution.py:561
  62.9 22.7 %collective-permute-start.10 = (s16[2,336,256]{2,1,0:T(8,128)(2,1)}, s16[2,336,256]{2,1,0:T(8,128)(2,1)S(1)}, u32[]{:S(2)}, u32[]{:S(2)}) collective-permute-start(s16[2,336,256]{2,1,0:T(8,128)(2,1)} %get-tuple-element.22), channel_id=1, source_target_pairs={{0,8},{4,12},{8,0},{12,4},{1,9},{5,13},{9,1},{13,5},{2,10},{6,14},... | collective-permute-start | bytes 1032200 | tf_op jit(solution)/shard_map/ppermute | solution.py:561
  62.9 23.3 %collective-permute-start.24 = (f32[2,2,2,64,256]{4,3,2,1,0:T(8,128)}, f32[2,2,2,64,256]{4,3,2,1,0:T(8,128)S(1)}, u32[]{:S(2)}, u32[]{:S(2)}) collective-permute-start(f32[2,2,2,64,256]{4,3,2,1,0:T(8,128)} %get-tuple-element.25), channel_id=1, source_target_pairs={{0,1},{1,0},{2,3},{3,2},{4,5},{5,4},{6,7},{7,6},{8,9},{9,8},{10,11... | collective-permute-start | bytes 1572872 | tf_op jit(solution)/shard_map/ppermute | solution.py:565
  65.0 77.0 %copy-start.18 = (s32[8,2]{1,0:T(8,128)}, s32[8,2]{1,0:T(8,128)S(1)}, u32[]{:S(2)}) copy-start(s32[8,2]{1,0:T(8,128)S(1)} %pad_add_fusion.refs_0_) | copy-start | bytes 196
  65.1 2.8 %collective-permute-start.3 = (s32[8,2]{1,0:T(8,128)S(1)}, s32[8,2]{1,0:T(8,128)S(1)}, u32[]{:S(2)}, u32[]{:S(2)}) collective-permute-start(s32[8,2]{1,0:T(8,128)S(1)} %pad_add_fusion.refs_0_), channel_id=1, source_target_pairs={{0,2},{1,3},{2,0},{3,1},{4,6},{5,7},{6,4},{7,5},{8,10},{9,11},{10,... | collective-permute-start | bytes 200 | tf_op jit(solution)/shard_map/ppermute | solution.py:565
  66.4 2.4 %collective-permute-start.4 = (s32[8,2]{1,0:T(8,128)S(1)}, s32[8,2]{1,0:T(8,128)S(1)}, u32[]{:S(2)}, u32[]{:S(2)}) collective-permute-start(s32[8,2]{1,0:T(8,128)S(1)} %pad_add_fusion.refs_0_), channel_id=1, source_target_pairs={{0,1},{1,0},{2,3},{3,2},{4,5},{5,4},{6,7},{7,6},{8,9},{9,8},{10,11... | collective-permute-start | bytes 200 | tf_op jit(solution)/shard_map/ppermute | solution.py:565
  67.9 74.1 %copy-start.20 = (s32[8,2]{1,0:T(8,128)}, s32[8,2]{1,0:T(8,128)S(1)}, u32[]{:S(2)}) copy-start(s32[8,2]{1,0:T(8,128)S(1)} %collective-permute-done.3.refs_1_) | copy-start | bytes 196
  67.9 1.7 %collective-permute-start.5 = (s32[8,2]{1,0:T(8,128)S(1)}, s32[8,2]{1,0:T(8,128)S(1)}, u32[]{:S(2)}, u32[]{:S(2)}) collective-permute-start(s32[8,2]{1,0:T(8,128)S(1)} %collective-permute-done.3.refs_1_), channel_id=1, source_target_pairs={{0,1},{1,0},{2,3},{3,2},{4,5},{5,4},{6,7},{7,6},{8,9},{9,8},{10,11... | collective-permute-start | bytes 200 | tf_op jit(solution)/shard_map/ppermute | solution.py:565
  68.7 73.3 %copy-start.21 = (s32[8,2]{1,0:T(8,128)}, s32[8,2]{1,0:T(8,128)S(1)}, u32[]{:S(2)}) copy-start(s32[8,2]{1,0:T(8,128)S(1)} %collective-permute-done.4.refs_2_) | copy-start | bytes 196
  68.8 19.8 %collective-permute-start.11 = (s16[2,336,256]{2,1,0:T(8,128)(2,1)}, s16[2,336,256]{2,1,0:T(8,128)(2,1)S(1)}, u32[]{:S(2)}, u32[]{:S(2)}) collective-permute-start(s16[2,336,256]{2,1,0:T(8,128)(2,1)} %get-tuple-element.23), channel_id=1, source_target_pairs={{0,12},{4,0},{8,4},{12,8},{1,13},{5,1},{9,5},{13,9},{2,14},{6,2},{... | collective-permute-start | bytes 1032200 | tf_op jit(solution)/shard_map/ppermute | solution.py:561
  69.6 19.4 %collective-permute-start.16 = (s16[2,336,256]{2,1,0:T(8,128)(2,1)}, s16[2,336,256]{2,1,0:T(8,128)(2,1)S(1)}, u32[]{:S(2)}, u32[]{:S(2)}) collective-permute-start(s16[2,336,256]{2,1,0:T(8,128)(2,1)} %get-tuple-element.20.refs_4_), channel_id=1, source_target_pairs={{0,1},{1,0},{2,3},{3,2},{4,5},{5,4},{6,7},{7,6},{8,9},{9,8},{10,11... | collective-permute-start | bytes 1032200 | tf_op jit(solution)/shard_map/ppermute | solution.py:565
  70.1 19.1 %collective-permute-start.12 = (s16[2,336,256]{2,1,0:T(8,128)(2,1)}, s16[2,336,256]{2,1,0:T(8,128)(2,1)S(1)}, u32[]{:S(2)}, u32[]{:S(2)}) collective-permute-start(s16[2,336,256]{2,1,0:T(8,128)(2,1)} %get-tuple-element.20.refs_4_), channel_id=1, source_target_pairs={{0,2},{1,3},{2,0},{3,1},{4,6},{5,7},{6,4},{7,5},{8,10},{9,11},{10,... | collective-permute-start | bytes 1032200 | tf_op jit(solution)/shard_map/ppermute | solution.py:565
  85.6 4.1 %collective-permute-start.17 = (s16[2,336,256]{2,1,0:T(8,128)(2,1)S(1)}, s16[2,336,256]{2,1,0:T(8,128)(2,1)S(1)}, u32[]{:S(2)}, u32[]{:S(2)}) collective-permute-start(s16[2,336,256]{2,1,0:T(8,128)(2,1)S(1)} %collective-permute-done.9.refs_5_), channel_id=1, source_target_pairs={{0,1},{1,0},{2,3},{3,2},{4,5},{5,4},{6,7},{7,6},{8,9},{9,8},{10,11... | collective-permute-start | bytes 1032200 | tf_op jit(solution)/shard_map/ppermute | solution.py:565
  86.2 9.6 %collective-permute-start.13 = (s16[2,336,256]{2,1,0:T(8,128)(2,1)S(1)}, s16[2,336,256]{2,1,0:T(8,128)(2,1)S(1)}, u32[]{:S(2)}, u32[]{:S(2)}) collective-permute-start(s16[2,336,256]{2,1,0:T(8,128)(2,1)S(1)} %collective-permute-done.9.refs_5_), channel_id=1, source_target_pairs={{0,2},{1,3},{2,0},{3,1},{4,6},{5,7},{6,4},{7,5},{8,10},{9,11},{10,... | collective-permute-start | bytes 1032200 | tf_op jit(solution)/shard_map/ppermute | solution.py:565
  88.6 8.4 %collective-permute-start.18 = (s16[2,336,256]{2,1,0:T(8,128)(2,1)S(1)}, s16[2,336,256]{2,1,0:T(8,128)(2,1)S(1)}, u32[]{:S(2)}, u32[]{:S(2)}) collective-permute-start(s16[2,336,256]{2,1,0:T(8,128)(2,1)S(1)} %collective-permute-done.10.refs_6_), channel_id=1, source_target_pairs={{0,1},{1,0},{2,3},{3,2},{4,5},{5,4},{6,7},{7,6},{8,9},{9,8},{10,11... | collective-permute-start | bytes 1032200 | tf_op jit(solution)/shard_map/ppermute | solution.py:565
  89.0 14.1 %collective-permute-start.14 = (s16[2,336,256]{2,1,0:T(8,128)(2,1)S(1)}, s16[2,336,256]{2,1,0:T(8,128)(2,1)S(1)}, u32[]{:S(2)}, u32[]{:S(2)}) collective-permute-start(s16[2,336,256]{2,1,0:T(8,128)(2,1)S(1)} %collective-permute-done.10.refs_6_), channel_id=1, source_target_pairs={{0,2},{1,3},{2,0},{3,1},{4,6},{5,7},{6,4},{7,5},{8,10},{9,11},{10,... | collective-permute-start | bytes 1032200 | tf_op jit(solution)/shard_map/ppermute | solution.py:565
  89.2 29.7 %collective-permute-start.19 = (s16[2,336,256]{2,1,0:T(8,128)(2,1)S(1)}, s16[2,336,256]{2,1,0:T(8,128)(2,1)S(1)}, u32[]{:S(2)}, u32[]{:S(2)}) collective-permute-start(s16[2,336,256]{2,1,0:T(8,128)(2,1)S(1)} %collective-permute-done.11.refs_7_), channel_id=1, source_target_pairs={{0,1},{1,0},{2,3},{3,2},{4,5},{5,4},{6,7},{7,6},{8,9},{9,8},{10,11... | collective-permute-start | bytes 1032200 | tf_op jit(solution)/shard_map/ppermute | solution.py:565
  89.7 20.9 %collective-permute-start.15 = (s16[2,336,256]{2,1,0:T(8,128)(2,1)S(1)}, s16[2,336,256]{2,1,0:T(8,128)(2,1)}, u32[]{:S(2)}, u32[]{:S(2)}) collective-permute-start(s16[2,336,256]{2,1,0:T(8,128)(2,1)S(1)} %collective-permute-done.11.refs_7_), channel_id=1, source_target_pairs={{0,2},{1,3},{2,0},{3,1},{4,6},{5,7},{6,4},{7,5},{8,10},{9,11},{10,... | collective-permute-start | bytes 1032200 | tf_op jit(solution)/shard_map/ppermute | solution.py:565
  95.7 20.5 %collective-permute-start.25 = (f32[2,2,64,256]{3,2,1,0:T(8,128)S(1)}, f32[2,2,64,256]{3,2,1,0:T(8,128)}, u32[]{:S(2)}, u32[]{:S(2)}) collective-permute-start(f32[2,2,64,256]{3,2,1,0:T(8,128)S(1)} %get-tuple-element.30), channel_id=1, source_target_pairs={{0,2},{1,3},{2,0},{3,1},{4,6},{5,7},{6,4},{7,5},{8,10},{9,11},{10,... | collective-permute-start | bytes 786440 | tf_op jit(solution)/shard_map/ppermute | solution.py:565
  97.0 32.1 %collective-permute-start.20 = (s16[2,336,256]{2,1,0:T(8,128)(2,1)S(1)}, s16[2,336,256]{2,1,0:T(8,128)(2,1)}, u32[]{:S(2)}, u32[]{:S(2)}) collective-permute-start(s16[2,336,256]{2,1,0:T(8,128)(2,1)S(1)} %collective-permute-done.12.refs_8_), channel_id=1, source_target_pairs={{0,1},{1,0},{2,3},{3,2},{4,5},{5,4},{6,7},{7,6},{8,9},{9,8},{10,11... | collective-permute-start | bytes 1032200 | tf_op jit(solution)/shard_map/ppermute | solution.py:565
  103.1 38.2 %collective-permute-start.21 = (s16[2,336,256]{2,1,0:T(8,128)(2,1)S(1)}, s16[2,336,256]{2,1,0:T(8,128)(2,1)}, u32[]{:S(2)}, u32[]{:S(2)}) collective-permute-start(s16[2,336,256]{2,1,0:T(8,128)(2,1)S(1)} %collective-permute-done.13.refs_9_), channel_id=1, source_target_pairs={{0,1},{1,0},{2,3},{3,2},{4,5},{5,4},{6,7},{7,6},{8,9},{9,8},{10,11... | collective-permute-start | bytes 1032200 | tf_op jit(solution)/shard_map/ppermute | solution.py:565
  110.6 30.7 %collective-permute-start.22 = (s16[2,336,256]{2,1,0:T(8,128)(2,1)S(1)}, s16[2,336,256]{2,1,0:T(8,128)(2,1)}, u32[]{:S(2)}, u32[]{:S(2)}) collective-permute-start(s16[2,336,256]{2,1,0:T(8,128)(2,1)S(1)} %collective-permute-done.14.refs_10_), channel_id=1, source_target_pairs={{0,1},{1,0},{2,3},{3,2},{4,5},{5,4},{6,7},{7,6},{8,9},{9,8},{10,11... | collective-permute-start | bytes 1032200 | tf_op jit(solution)/shard_map/ppermute | solution.py:565
  116.2 25.1 %collective-permute-start.23 = (s16[2,336,256]{2,1,0:T(8,128)(2,1)}, s16[2,336,256]{2,1,0:T(8,128)(2,1)}, u32[]{:S(2)}, u32[]{:S(2)}) collective-permute-start(s16[2,336,256]{2,1,0:T(8,128)(2,1)} %collective-permute-done.15.refs_11_), channel_id=1, source_target_pairs={{0,1},{1,0},{2,3},{3,2},{4,5},{5,4},{6,7},{7,6},{8,9},{9,8},{10,11... | collective-permute-start | bytes 1032200 | tf_op jit(solution)/shard_map/ppermute | solution.py:565
  118.9 13.5 %collective-permute-start.28 = (s16[272,256]{1,0:T(8,128)(2,1)}, s16[272,256]{1,0:T(8,128)(2,1)S(1)}, u32[]{:S(2)}, u32[]{:S(2)}) collective-permute-start(s16[272,256]{1,0:T(8,128)(2,1)} %get-tuple-element.27), channel_id=1, source_target_pairs={{0,12},{4,0},{8,4},{12,8},{1,13},{5,1},{9,5},{13,9},{2,14},{6,2},{... | collective-permute-start | bytes 417800 | tf_op jit(solution)/shard_map/ppermute | solution.py:561
  129.1 12.2 %collective-permute-start.27 = (s16[272,256]{1,0:T(8,128)(2,1)}, s16[272,256]{1,0:T(8,128)(2,1)S(1)}, u32[]{:S(2)}, u32[]{:S(2)}) collective-permute-start(s16[272,256]{1,0:T(8,128)(2,1)} %get-tuple-element.27), channel_id=1, source_target_pairs={{0,8},{4,12},{8,0},{12,4},{1,9},{5,13},{9,1},{13,5},{2,10},{6,14},... | collective-permute-start | bytes 417800 | tf_op jit(solution)/shard_map/ppermute | solution.py:561
  132.5 8.8 %collective-permute-start.26 = (s16[272,256]{1,0:T(8,128)(2,1)}, s16[272,256]{1,0:T(8,128)(2,1)S(1)}, u32[]{:S(2)}, u32[]{:S(2)}) collective-permute-start(s16[272,256]{1,0:T(8,128)(2,1)} %get-tuple-element.27), channel_id=1, source_target_pairs={{0,4},{4,8},{8,12},{12,0},{1,5},{5,9},{9,13},{13,1},{2,6},{6,10},{... | collective-permute-start | bytes 417800 | tf_op jit(solution)/shard_map/ppermute | solution.py:561
  (26 other events, 807.7 us)

commit v2 on v1

--- a/solution.py
+++ b/solution.py
@@ -7,6 +7,7 @@
 from jax.experimental import pallas as pl
 from jax.experimental.pallas import tpu as pltpu
 from jax.sharding import PartitionSpec as P
+
 
 HIGHEST_PREC = lax.Precision.HIGHEST
 
@@ -178,11 +179,11 @@
     return lax.broadcasted_iota(jnp.int32, shape, 0)
 
 
-def pack_kernel(tiles, win, width, me_ref, owner_ref, *refs):
-    offs = refs[:tiles]
-    obj_ref = refs[tiles]
-    outs = refs[tiles + 1 : 2 * tiles + 1]
-    buf, pack, params, in_sem, out_sem = refs[2 * tiles + 1 :]
+def pack_kernel(tiles, asked, win, width, me_ref, owner_ref, *refs):
+    offs = refs[:asked]
+    obj_ref = refs[asked]
+    outs = refs[asked + 1 : 2 * asked + 1]
+    buf, pack, params, in_sem, out_sem = refs[2 * asked + 1 :]
     half = win // 2
     quarter = win // 4
     strip = strip_held(owner_ref, me_ref[0], tiles)
@@ -193,7 +194,7 @@
             obj_ref.at[:, :, pl.ds(start, 2 * win)], buf.at[k], in_sem.at[k]
         )
 
-    for k in range(tiles):
+    for k in range(asked):
         y_up, x_up, x_low, _ = geometry(offs[k][0, 0], offs[k][0, 1], offs[k][1, 0], offs[k][1, 1])
         left = jnp.minimum(x_up, x_low)
         params[k, 0] = y_up
@@ -237,10 +238,10 @@
                 ).astype(pack.dtype)
         return carry
 
-    for k in range(tiles):
+    for k in range(asked):
         one(k, 0)
         pltpu.make_async_copy(pack.at[k], outs[k], out_sem.at[k]).start()
-    for k in range(tiles):
+    for k in range(asked):
         pltpu.make_async_copy(pack.at[k], outs[k], out_sem.at[k]).wait()
 
 
@@ -453,6 +454,43 @@
         copy.wait()
 
 
+def propagate_call(tiles, pos_groups, win, modes, grad_scale):
+    half = win // 2
+    share = win // pos_groups
+    pack_shape = (2, win + win // 4, win)
+    grad_shape = (2, win + win // 4 + 16, win)
+    smem = pl.BlockSpec(memory_space=pltpu.SMEM)
+    vmem = pl.BlockSpec(memory_space=pltpu.VMEM)
+    anywhere = pl.BlockSpec(memory_space=pl.ANY)
+    return pl.pallas_call(
+        functools.partial(compute_kernel, tiles, pos_groups, win, modes, grad_scale),
+        out_shape=[jax.ShapeDtypeStruct(grad_shape, jnp.int16)] * tiles
+        + [jax.ShapeDtypeStruct((pos_groups // 2, modes, 2, share, win), jnp.float32)] * 2,
+        in_specs=[smem] * 3 + [anywhere] * tiles + [vmem] * 6 + [smem],
+        out_specs=[anywhere] * (tiles + 2),
+        scratch_shapes=[
+            pltpu.VMEM((tiles,) + pack_shape, jnp.bfloat16),
+            pltpu.VMEM((2, 3 * win, win), jnp.float32),
+            pltpu.VMEM((2, 2, win, win), jnp.float32),
+            pltpu.VMEM((2 * modes, 2 * win, win), jnp.float32),
+            pltpu.VMEM((2, win, win), jnp.float32),
+            pltpu.VMEM((2, 4 * win, 2 * win), jnp.bfloat16),
+            pltpu.VMEM((2, 2 * win, 2 * win), jnp.bfloat16),
+            pltpu.VMEM((2, 2 * win, 4 * win), jnp.bfloat16),
+            pltpu.VMEM((2, 2 * win, 2 * win), jnp.bfloat16),
+            pltpu.VMEM((2, 2, win, win), jnp.float32),
+            pltpu.VMEM((modes, 2, win, win), jnp.float32),
+            pltpu.VMEM((2, 3 * win, win), jnp.float32),
+            pltpu.VMEM((2, win, half), jnp.float32),
+            pltpu.VMEM((3,) + grad_shape, jnp.int16),
+            pltpu.SemaphoreType.DMA((tiles,)),
+            pltpu.SemaphoreType.DMA((tiles,)),
+            pltpu.SemaphoreType.DMA((pos_groups,)),
+        ],
+        name="propagate",
+    )
+
+
 def probe_pack_kernel(blocks, rows, kept_ref, came_ref, total_ref, pack_ref):
     codes = []
     for b in range(blocks):
@@ -463,14 +501,24 @@
     pack_ref[blocks * rows : blocks * rows + 16, :] = code_rows(codes)
 
 
-def place_kernel(tiles, pos_groups, win, slab, me_ref, spot_ref, owner_ref, *refs):
-    count = tiles * pos_groups
-    offs = refs[:pos_groups]
-    packs = refs[pos_groups : pos_groups + count]
-    probe_own = refs[pos_groups + count]
-    probe_packs = refs[pos_groups + count + 1 : pos_groups + count + tiles]
-    out_ref, probe_ref = refs[pos_groups + count + tiles : pos_groups + count + tiles + 2]
-    held, acc, params, in_sem, out_sem = refs[pos_groups + count + tiles + 2 :]
+def probe_sum_kernel(blocks, rows, own_ref, *refs):
+    packs, total_ref = refs[:-1], refs[-1]
+    scales = [step_of(wide_of(pack[blocks * rows : blocks * rows + 16, :])) for pack in packs]
+    for b in range(blocks):
+        total = own_ref[b]
+        for pack, scale in zip(packs, scales):
+            total = total + wide_of(pack[b * rows : (b + 1) * rows, :]) * scale[b : b + 1, :]
+        total_ref[b] = total
+
+
+def place_kernel(tiles, spots, steps_back, first, win, slab, me_ref, spot_ref, owner_ref, *refs):
+    picks = [(j, k) for k in steps_back for j in range(spots)]
+    count = len(picks)
+    offs, refs = refs[:spots], refs[spots:]
+    packs, refs = refs[:count], refs[count:]
+    if not first:
+        before, refs = refs[0], refs[1:]
+    out_ref, held, acc, params, in_sem, out_sem = refs
     half = win // 2
     quarter = win // 4
     me = me_ref[0]
@@ -479,8 +527,10 @@
     first_col = spot_ref[0] * slab
     margin = 2 * win
     span = 3 * half
-    for n in range(count):
-        j, k = n // tiles, n % tiles
+    if not first:
+        resume = pltpu.make_async_copy(before, acc.at[:, :, margin : margin + slab], out_sem)
+        resume.start()
+    for n, (j, k) in enumerate(picks):
         off = offs[j]
         y_up, x_up, x_low, _ = geometry(off[2 * k, 0], off[2 * k, 1], off[2 * k + 1, 0], off[2 * k + 1, 1])
         left = jnp.minimum(x_up, x_low)
@@ -498,14 +548,10 @@
         acc[:, pl.ds(pl.multiple_of(i * 8, 8), 8), :] = jnp.zeros((2, 8, acc.shape[2]), jnp.float32)
         return carry
 
-    lax.fori_loop(0, win // 8, clear, 0)
-    blocks, rows_each = probe_own.shape[0], probe_own.shape[1]
-    scales = [step_of(wide_of(pk[blocks * rows_each : blocks * rows_each + 16, :])) for pk in probe_packs]
-    for b in range(blocks):
-        total = probe_own[b]
-        for pk, scale in zip(probe_packs, scales):
-            total = total + wide_of(pk[b * rows_each : (b + 1) * rows_each, :]) * scale[b : b + 1, :]
-        probe_ref[b] = total
+    if first:
+        lax.fori_loop(0, win // 8, clear, 0)
+    else:
+        resume.wait()
 
     def one(n, carry):
         @pl.when(params[n, 0] == 1)
@@ -572,7 +618,6 @@
     modes = probe.shape[0]
     width = object_field.shape[2]
     slab = width // pos_groups
-    half = win // 2
     quarter = win // 4
     grad_scale = 1.0 / math.sqrt(pos_count * tiles * pos_groups)
     me = lax.axis_index("tile").astype(jnp.int32).reshape(1)
@@ -585,58 +630,45 @@
     share = win // pos_groups
 
     offs = [offsets] + [shifted(offsets, "tile", tiles, tiles - k) for k in range(1, tiles)]
-    packs = pl.pallas_call(
-        functools.partial(pack_kernel, tiles, win, width),
-        out_shape=[jax.ShapeDtypeStruct(pack_shape, jnp.bfloat16)] * tiles,
-        in_specs=[smem] * (2 + tiles) + [anywhere],
-        out_specs=[anywhere] * tiles,
-        scratch_shapes=[
-            pltpu.VMEM((tiles, 2, win, 2 * win), jnp.bfloat16),
-            pltpu.VMEM((tiles,) + pack_shape, jnp.bfloat16),
-            pltpu.SMEM((tiles, 4), jnp.int32),
-            pltpu.SemaphoreType.DMA((tiles,)),
-            pltpu.SemaphoreType.DMA((tiles,)),
-        ],
-        name="pack",
-    )(me, strip_owner, *offs, object_field)
+
+    def pack_for(asking, field):
+        asked = len(asking)
+        return pl.pallas_call(
+            functools.partial(pack_kernel, tiles, asked, win, width),
+            out_shape=[jax.ShapeDtypeStruct(pack_shape, jnp.bfloat16)] * asked,
+            in_specs=[smem] * (2 + asked) + [anywhere],
+            out_specs=[anywhere] * asked,
+            scratch_shapes=[
+                pltpu.VMEM((asked, 2, win, 2 * win), jnp.bfloat16),
+                pltpu.VMEM((asked,) + pack_shape, jnp.bfloat16),
+                pltpu.SMEM((asked, 4), jnp.int32),
+                pltpu.SemaphoreType.DMA((asked,)),
+                pltpu.SemaphoreType.DMA((asked,)),
+            ],
+            name="pack",
+        )(me, strip_owner, *asking, field)
+
+    packs = pack_for(offs[1:], object_field)
+    packs, chirp, own_off = lax.optimization_barrier((packs, chirp, offsets))
+    packs = pack_for([own_off], object_field) + packs
+    column_offs = [jnp.concatenate([own_off] + [offs[tiles - k] for k in range(1, tiles)], axis=0)]
+    bit = pos_groups // 2
+    while bit:
+        column_offs = column_offs + [swapped(o, "pos", pos_groups, bit) for o in column_offs]
+        bit //= 2
     arrived = [packs[0]] + [shifted(packs[k], "tile", tiles, k) for k in range(1, tiles)]
     prop_re, prop_im = build_propagator(chirp)
-    results = pl.pallas_call(
-        functools.partial(compute_kernel, tiles, pos_groups, win, modes, grad_scale),
-        out_shape=[jax.ShapeDtypeStruct(grad_shape, jnp.int16)] * tiles
-        + [jax.ShapeDtypeStruct((pos_groups // 2, modes, 2, share, win), jnp.float32)] * 2,
-        in_specs=[smem] * 3 + [anywhere] * tiles + [vmem] * 6 + [smem],
-        out_specs=[anywhere] * (tiles + 2),
-        scratch_shapes=[
-            pltpu.VMEM((tiles,) + pack_shape, jnp.bfloat16),
-            pltpu.VMEM((2, 3 * win, win), jnp.float32),
-            pltpu.VMEM((2, 2, win, win), jnp.float32),
-            pltpu.VMEM((2 * modes, 2 * win, win), jnp.float32),
-            pltpu.VMEM((2, win, win), jnp.float32),
-            pltpu.VMEM((2, 4 * win, 2 * win), jnp.bfloat16),
-            pltpu.VMEM((2, 2 * win, 2 * win), jnp.bfloat16),
-            pltpu.VMEM((2, 2 * win, 4 * win), jnp.bfloat16),
-            pltpu.VMEM((2, 2 * win, 2 * win), jnp.bfloat16),
-            pltpu.VMEM((2, 2, win, win), jnp.float32),
-            pltpu.VMEM((modes, 2, win, win), jnp.float32),
-            pltpu.VMEM((2, 3 * win, win), jnp.float32),
-            pltpu.VMEM((2, win, half), jnp.float32),
-            pltpu.VMEM((3,) + grad_shape, jnp.int16),
-            pltpu.SemaphoreType.DMA((tiles,)),
-            pltpu.SemaphoreType.DMA((tiles,)),
-            pltpu.SemaphoreType.DMA((pos_groups,)),
-        ],
-        name="propagate",
-    )(me, strip_owner, offsets, *arrived, probe, amplitude, prop_re, prop_im, prop_re.T, prop_im.T, spot)
+    arrived, column_offs = lax.optimization_barrier((arrived, column_offs))
+    results = propagate_call(tiles, pos_groups, win, modes, grad_scale)(
+        me, strip_owner, offsets, *arrived, probe, amplitude, prop_re, prop_im, prop_re.T, prop_im.T, spot
+    )
     grads, (away, kept) = results[:tiles], results[tiles:]
 
     column = [grads[0]] + [shifted(grads[k], "tile", tiles, k) for k in range(1, tiles)]
-    column_offs = [jnp.concatenate([offs[(tiles - k) % tiles] for k in range(tiles)], axis=0)]
     columns = [column]
     bit = pos_groups // 2
     while bit:
-        columns = columns + [[swapped(x, "pos", pos_groups, bit) for x in c] for c in columns]
-        column_offs = column_offs + [swapped(o, "pos", pos_groups, bit) for o in column_offs]
+        columns = columns + [[swapped(x, "pos", pos_groups, bit) for x in column] for column in columns]
         bit //= 2
 
     kept = kept + swapped(away, "pos", pos_groups, 1)
@@ -656,30 +688,36 @@
     )(kept[0].reshape(blocks, share, win), came.reshape(blocks, share, win))
     probe_packs = [shifted(probe_pack, "tile", tiles, k) for k in range(1, tiles)]
 
-    flat = [x for c in columns for x in c]
-    count = len(flat)
-    strip_part, probe_out = pl.pallas_call(
-        functools.partial(place_kernel, tiles, pos_groups, win, slab),
-        out_shape=[
-            jax.ShapeDtypeStruct((2, win, slab), jnp.float32),
-            jax.ShapeDtypeStruct((blocks, share, win), jnp.float32),
-        ],
-        in_specs=[smem] * (3 + pos_groups) + [anywhere] * count + [vmem] * tiles,
-        out_specs=[anywhere, vmem],
-        scratch_shapes=[
-            pltpu.VMEM((count,) + grad_shape, jnp.int16),
-            pltpu.VMEM((2, win, slab + 4 * win), jnp.float32),
-            pltpu.SMEM((count, 4), jnp.int32),
-            pltpu.SemaphoreType.DMA((count,)),
-            pltpu.SemaphoreType.DMA,
-        ],
-        name="place",
-    )(me, spot, strip_owner, *column_offs, *flat, probe_own, *probe_packs)
-    return (strip_part, probe_out.reshape(modes, 2, share, win))
+    probe_out = pl.pallas_call(
+        functools.partial(probe_sum_kernel, blocks, share),
+        out_shape=jax.ShapeDtypeStruct((blocks, share, win), jnp.float32),
+        name="probe_sum",
+    )(probe_own, *probe_packs)
+
+    spots = len(columns)
+    placed = None
+    near_first = near_to_far(tiles)
+    for steps_back in ([0], near_first[:-1], near_first[-1:]):
+        arrays = [columns[j][k] for k in steps_back for j in range(spots)]
+        count = len(arrays)
+        first = placed is None
+        placed = pl.pallas_call(
+            functools.partial(place_kernel, tiles, spots, steps_back, first, win, slab),
+            out_shape=jax.ShapeDtypeStruct((2, win, slab), jnp.float32),
+            in_specs=[smem] * (3 + spots) + [anywhere] * (count + (not first)),
+            out_specs=anywhere,
+            scratch_shapes=[
+                pltpu.VMEM((count,) + grad_shape, jnp.int16),
+                pltpu.VMEM((2, win, slab + 4 * win), jnp.float32),
+                pltpu.SMEM((count, 4), jnp.int32),
+                pltpu.SemaphoreType.DMA((count,)),
+                pltpu.SemaphoreType.DMA,
+            ],
+        )(me, spot, strip_owner, *column_offs, *arrays, *([] if first else [placed]))
+    return (placed, probe_out.reshape(modes, 2, share, win))
 
 
 def per_device(object_field, probe, amplitude, offsets, strip_owner, chirp):
-    tiles = lax.axis_size("tile")
     pos_groups = lax.axis_size("pos")
     pos_count, win, _ = amplitude.shape
     width = object_field.shape[2]
@@ -693,8 +731,13 @@
         and pos_groups >= 4
         and (win // pos_groups) % 16 == 0
     )
-    plan = per_device_packed if packed else per_device_general
-    return plan(object_field, probe, amplitude, offsets, strip_owner, chirp)
+    if not packed:
+        return per_device_general(object_field, probe, amplitude, offsets, strip_owner, chirp)
+    return per_device_packed(object_field, probe, amplitude, offsets, strip_owner, chirp)
+
+
+def near_to_far(tiles):
+    return sorted(range(1, tiles), key=lambda k: (min(k, tiles - k), k))
 
 
 def solution(mesh):

time: 149 us -> 140 us (0.940)
  waiting for transfers between devices: 62.8 us -> 48.2 us
  Pallas kernels: 25.7 us -> 38.5 us
  starting transfers between devices: 44.5 us -> 38 us
    ppermute x17, waiting for transfers between devices: 19.9 us -> 3.08 us  [swapped(): return lax.ppermute(x, axis, [(i, i ^ bit) for i in range(count)])]
    pallas_call x3 -> x7, Pallas kernels: 23.9 us -> 36.7 us  [the longest x1 15.7 us: per_device_packed(): propagate_call(tiles, pos_groups, win, modes, grad_scale)]
    ppermute x12, starting transfers between devices: 27.3 us -> 19.4 us  [shifted(): return lax.ppermute(x, axis, [(i, (i + k) % count) for i in range(count)])]
    ppermute x12, waiting for transfers between devices: 43 us -> 45.1 us  [shifted(): return lax.ppermute(x, axis, [(i, (i + k) % count) for i in range(count)])]
  transfers between devices with their start and end apart: 29 -> 29, of which waited for: 10 -> 11; matrix products, arithmetic and copies ran while one was open for 7% -> 5% of each run, Pallas kernels for 1% -> 9%
where the time goes in v2:
time: 140 us; the launch traced here: 138 us
  waiting for transfers between devices  48.2 us (34%)
  Pallas kernels  38.5 us (28%)
  starting transfers between devices  38 us (27%)
  matrix products  6.61 us (5%)
  local copies, waits for them, and re-layouts  4.57 us (3%)
    ppermute x12, waiting for transfers between devices, shifted(): return lax.ppermute(x, axis, [(i, (i + k) % count) for i in range(count)])  45.1 us
    ppermute x12, starting transfers between devices, shifted(): return lax.ppermute(x, axis, [(i, (i + k) % count) for i in range(count)])  19.4 us
    ppermute x17, starting transfers between devices, swapped(): return lax.ppermute(x, axis, [(i, i ^ bit) for i in range(count)])  18.6 us
    pallas_call x1, Pallas kernels, per_device_packed(): propagate_call(tiles, pos_groups, win, modes, grad_scale)  15.7 us
    pallas_call x3, Pallas kernels, per_device_packed(): pl.pallas_call(functools.partial(place_kernel, tiles, spots, steps_back,...  12.7 us
    pallas_call x2, Pallas kernels, pack_for(): pl.pallas_call(functools.partial(pack_kernel, tiles, asked, win, width),...  6.29 us
    ppermute x17, waiting for transfers between devices, swapped(): return lax.ppermute(x, axis, [(i, i ^ bit) for i in range(count)])  3.08 us
  transfers between devices with their start and end apart: 29, of which 11 were waited for; matrix products, arithmetic and copies ran while one was open for 5% of the time, Pallas kernels for 9%

profile of v2, /device:TPU:1, one launch (start us, length us, event | category | flops | bytes accessed | tf_op | source)
XLA Modules:
  0.0 138.3 jit_solution(8423423201154341572)
XLA Ops:
  0.6 4.2 %collective-permute-start = (s32[2,2]{1,0:T(2,128)}, s32[2,2]{1,0:T(2,128)S(1)}, u32[]{:S(2)}, u32[]{:S(2)}) collective-permute-start(s32[2,2]{1,0:T(2,128)} %off_ref.1), channel_id=1, source_target_pairs={{0,12},{4,0},{8,4},{12,8},{1,13},{5,1},{9,5},{13,9},{2,14},{6,2},{... | collective-permute-start | bytes 56 | tf_op jit(solution)/shard_map/ppermute | solution.py:607
  5.8 2.6 %collective-permute-done.1.refs_1_ = s32[2,2]{1,0:T(2,128)S(1)} collective-permute-done((s32[2,2]{1,0:T(2,128)}, s32[2,2]{1,0:T(2,128)S(1)}, u32[]{:S(2)}, u32[]{:S(2)}) %collective-permute-start.1) | collective-permute-done | bytes 48 | tf_op jit(solution)/shard_map/ppermute | solution.py:607
  9.8 3.4 %pack.2 = (bf16[2,320,256]{2,1,0:T(8,128)(2,1)}, bf16[2,320,256]{2,1,0:T(8,128)(2,1)}, bf16[2,320,256]{2,1,0:T(8,128)(2,1)}) custom-call(s32[1]{0:T(128)} %bitcast.me_ref, s32[4]{0:T(128)} %owner_ref.11, s32[2,2]{1,0:T(2,128)} %copy-done.23, s32[2,2]{1,0:T(2,128)} %copy-done.25, s32[2,2]{1,0:T(2,128)} %copy-done.27, bf16[2,256,4096]{2,1,0:T(8,128)(2,1)} %refs_1_.1), custom_call_target="tpu_custom_call" | custom-call | tf_op jit(solution)/shard_map/pack/pallas_call | solution.py:636
  13.3 1.7 %fusion.8 = f32[256,256]{0,1:T(8,128)S(1)} fusion(f32[256]{0:T(256)S(1)} %get-tuple-element.53, f32[256]{0:T(256)S(1)} %get-tuple-element.52), kind=kOutput, calls=%fused_computation.17 | convolution fusion | flops 203489280 | bytes 264192 | tf_op jit(solution)/shard_map/dot_general | solution.py:34
  15.0 1.7 %fusion.10 = f32[256,256]{0,1:T(8,128)S(1)} fusion(f32[256]{0:T(256)S(1)} %get-tuple-element.53, f32[256]{0:T(256)S(1)} %get-tuple-element.52), kind=kOutput, calls=%fused_computation.19 | convolution fusion | flops 203489280 | bytes 264192 | tf_op jit(solution)/shard_map/dot_general | solution.py:31
  16.7 2.9 %pack.3.refs_0_ = bf16[2,320,256]{2,1,0:T(8,128)(2,1)} custom-call(s32[1]{0:T(128)} %bitcast.me_ref, s32[4]{0:T(128)} %owner_ref.11, s32[2,2]{1,0:T(2,128)} %off_ref.1, bf16[2,256,4096]{2,1,0:T(8,128)(2,1)} %refs_1_.1), custom_call_target="tpu_custom_call" | custom-call | tf_op jit(solution)/shard_map/pack/pallas_call | solution.py:636
  19.7 1.3 collective-permute-start.6
  20.9 2.4 %collective-permute-start.7 = (s32[8,2]{1,0:T(8,128)S(1)}, s32[8,2]{1,0:T(8,128)S(1)}, u32[]{:S(2)}, u32[]{:S(2)}) collective-permute-start(s32[8,2]{1,0:T(8,128)S(1)} %pad_add_fusion.refs_0_), channel_id=1, source_target_pairs={{0,1},{1,0},{2,3},{3,2},{4,5},{5,4},{6,7},{7,6},{8,9},{9,8},{10,11... | collective-permute-start | bytes 200 | tf_op jit(solution)/shard_map/ppermute | solution.py:611
  24.2 2.6 %collective-permute-start.5 = (bf16[2,320,256]{2,1,0:T(8,128)(2,1)S(1)}, bf16[2,320,256]{2,1,0:T(8,128)(2,1)S(1)}, u32[]{:S(2)}, u32[]{:S(2)}) collective-permute-start(bf16[2,320,256]{2,1,0:T(8,128)(2,1)S(1)} %copy-done.30), channel_id=1, source_target_pairs={{0,12},{4,0},{8,4},{12,8},{1,13},{5,1},{9,5},{13,9},{2,14},{6,2},{... | collective-permute-start | bytes 983048 | tf_op jit(solution)/shard_map/ppermute | solution.py:607
  26.8 1.6 %convolution_subtract_fusion = f32[256,256]{0,1:T(8,128)S(1)} fusion(f32[256,256]{0,1:T(8,128)S(1)} %fusion.8, f32[256]{0:T(256)S(1)} %get-tuple-element.53, f32[256]{0:T(256)S(1)} %get-tuple-element.52), kind=kOutput, calls=%fused_computation | convolution fusion | flops 203620352 | bytes 526336 | tf_op jit(solution)/shard_map/dot_general | solution.py:34
  29.4 1.6 %convolution_add_fusion = f32[256,256]{0,1:T(8,128)S(1)} fusion(f32[256,256]{0,1:T(8,128)S(1)} %fusion.10, f32[256]{0:T(256)S(1)} %get-tuple-element.53, f32[256]{0:T(256)S(1)} %get-tuple-element.52), kind=kOutput, calls=%fused_computation.1 | convolution fusion | flops 203620352 | bytes 526336 | tf_op jit(solution)/shard_map/dot_general | solution.py:31
  34.5 13.2 %collective-permute-done.4.refs_2_ = bf16[2,320,256]{2,1,0:T(8,128)(2,1)S(1)} collective-permute-done((bf16[2,320,256]{2,1,0:T(8,128)(2,1)S(1)}, bf16[2,320,256]{2,1,0:T(8,128)(2,1)S(1)}, u32[]{:S(2)}, u32[]{:S(2)}) %collective-permute-start.4) | collective-permute-done | bytes 327712 | tf_op jit(solution)/shard_map/ppermute | solution.py:607
  48.5 15.7 %propagate.1 = (s16[2,336,256]{2,1,0:T(8,128)(2,1)}, s16[2,336,256]{2,1,0:T(8,128)(2,1)}, s16[2,336,256]{2,1,0:T(8,128)(2,1)}, s16[2,336,256]{2,1,0:T(8,128)(2,1...) custom-call(s32[1]{0:T(128)} %bitcast.me_ref, s32[4]{0:T(128)} %owner_ref.11, s32[2,2]{1,0:T(2,128)} %off_ref.1, ...), custom_call_target="tpu_custom_call" | custom-call | tf_op jit(solution)/shard_map/propagate/pallas_call | solution.py:662
  64.2 1.4 %collective-permute-start.24 = (f32[2,2,2,64,256]{4,3,2,1,0:T(8,128)}, f32[2,2,2,64,256]{4,3,2,1,0:T(8,128)S(1)}, u32[]{:S(2)}, u32[]{:S(2)}) collective-permute-start(f32[2,2,2,64,256]{4,3,2,1,0:T(8,128)} %get-tuple-element.47), channel_id=1, source_target_pairs={{0,1},{1,0},{2,3},{3,2},{4,5},{5,4},{6,7},{7,6},{8,9},{9,8},{10,11... | collective-permute-start | bytes 1572872 | tf_op jit(solution)/shard_map/ppermute | solution.py:611
  66.2 6.7 %collective-permute-start.13 = (s16[2,336,256]{2,1,0:T(8,128)(2,1)}, s16[2,336,256]{2,1,0:T(8,128)(2,1)S(1)}, u32[]{:S(2)}, u32[]{:S(2)}) collective-permute-start(s16[2,336,256]{2,1,0:T(8,128)(2,1)} %get-tuple-element.43), channel_id=1, source_target_pairs={{0,4},{4,8},{8,12},{12,0},{1,5},{5,9},{9,13},{13,1},{2,6},{6,10},{... | collective-permute-start | bytes 1032200 | tf_op jit(solution)/shard_map/ppermute | solution.py:607
  78.2 3.8 %collective-permute-done.13.refs_4_ = s16[2,336,256]{2,1,0:T(8,128)(2,1)S(1)} collective-permute-done((s16[2,336,256]{2,1,0:T(8,128)(2,1)}, s16[2,336,256]{2,1,0:T(8,128)(2,1)S(1)}, u32[]{:S(2)}, u32[]{:S(2)}) %collective-permute-start.13) | collective-permute-done | bytes 344096 | tf_op jit(solution)/shard_map/ppermute | solution.py:607
  82.0 1.2 collective-permute-start.14
  83.2 6.4 %collective-permute-done.17.refs_8_ = s16[2,336,256]{2,1,0:T(8,128)(2,1)S(1)} collective-permute-done((s16[2,336,256]{2,1,0:T(8,128)(2,1)}, s16[2,336,256]{2,1,0:T(8,128)(2,1)S(1)}, u32[]{:S(2)}, u32[]{:S(2)}) %collective-permute-start.17) | collective-permute-done | bytes 344096 | tf_op jit(solution)/shard_map/ppermute | solution.py:607
  89.6 1.2 collective-permute-start.18
  90.8 13.5 %collective-permute-done.9.refs_4_ = s16[2,336,256]{2,1,0:T(8,128)(2,1)S(1)} collective-permute-done((s16[2,336,256]{2,1,0:T(8,128)(2,1)}, s16[2,336,256]{2,1,0:T(8,128)(2,1)S(1)}, u32[]{:S(2)}, u32[]{:S(2)}) %collective-permute-start.9) | collective-permute-done | bytes 344096 | tf_op jit(solution)/shard_map/ppermute | solution.py:607
  104.8 1.2 collective-permute-start.10
  106.1 1.8 %probe_pack.1 = (f32[4,64,256]{2,1,0:T(8,128)}, s16[272,256]{1,0:T(8,128)(2,1)}) custom-call(f32[4,64,256]{2,1,0:T(8,128)} %bitcast.11, f32[4,64,256]{2,1,0:T(8,128)} %bitcast.6.came_ref), custom_call_target="tpu_custom_call" | custom-call | tf_op jit(solution)/shard_map/probe_pack/pallas_call | solution.py:681
  107.9 1.8 %collective-permute-start.27 = (s16[272,256]{1,0:T(8,128)(2,1)}, s16[272,256]{1,0:T(8,128)(2,1)S(1)}, u32[]{:S(2)}, u32[]{:S(2)}) collective-permute-start(s16[272,256]{1,0:T(8,128)(2,1)} %get-tuple-element.49), channel_id=1, source_target_pairs={{0,8},{4,12},{8,0},{12,4},{1,9},{5,13},{9,1},{13,5},{2,10},{6,14},... | collective-permute-start | bytes 417800 | tf_op jit(solution)/shard_map/ppermute | solution.py:607
  109.7 1.5 %collective-permute-start.28 = (s16[272,256]{1,0:T(8,128)(2,1)}, s16[272,256]{1,0:T(8,128)(2,1)S(1)}, u32[]{:S(2)}, u32[]{:S(2)}) collective-permute-start(s16[272,256]{1,0:T(8,128)(2,1)} %get-tuple-element.49), channel_id=1, source_target_pairs={{0,12},{4,0},{8,4},{12,8},{1,13},{5,1},{9,5},{13,9},{2,14},{6,2},{... | collective-permute-start | bytes 417800 | tf_op jit(solution)/shard_map/ppermute | solution.py:607
  112.2 2.2 %collective-permute-done.10.refs_5_ = s16[2,336,256]{2,1,0:T(8,128)(2,1)S(1)} collective-permute-done((s16[2,336,256]{2,1,0:T(8,128)(2,1)S(1)}, s16[2,336,256]{2,1,0:T(8,128)(2,1)S(1)}, u32[]{:S(2)}, u32[]{:S(2)}) %collective-permute-start.10) | collective-permute-done | bytes 344096 | tf_op jit(solution)/shard_map/ppermute | solution.py:611
  115.3 1.6 %collective-permute-start.20 = (s16[2,336,256]{2,1,0:T(8,128)(2,1)S(1)}, s16[2,336,256]{2,1,0:T(8,128)(2,1)}, u32[]{:S(2)}, u32[]{:S(2)}) collective-permute-start(s16[2,336,256]{2,1,0:T(8,128)(2,1)S(1)} %collective-permute-done.18.refs_9_), channel_id=1, source_target_pairs={{0,1},{1,0},{2,3},{3,2},{4,5},{5,4},{6,7},{7,6},{8,9},{9,8},{10,11... | collective-permute-start | bytes 1032200 | tf_op jit(solution)/shard_map/ppermute | solution.py:611
  116.9 3.1 %collective-permute-done.27.refs_1_ = s16[272,256]{1,0:T(8,128)(2,1)S(1)} collective-permute-done((s16[272,256]{1,0:T(8,128)(2,1)}, s16[272,256]{1,0:T(8,128)(2,1)S(1)}, u32[]{:S(2)}, u32[]{:S(2)}) %collective-permute-start.27) | collective-permute-done | bytes 139296 | tf_op jit(solution)/shard_map/ppermute | solution.py:607
  120.0 2.0 %collective-permute-start.11 = (s16[2,336,256]{2,1,0:T(8,128)(2,1)S(1)}, s16[2,336,256]{2,1,0:T(8,128)(2,1)}, u32[]{:S(2)}, u32[]{:S(2)}) collective-permute-start(s16[2,336,256]{2,1,0:T(8,128)(2,1)S(1)} %collective-permute-done.9.refs_4_), channel_id=1, source_target_pairs={{0,1},{1,0},{2,3},{3,2},{4,5},{5,4},{6,7},{7,6},{8,9},{9,8},{10,11... | collective-permute-start | bytes 1032200 | tf_op jit(solution)/shard_map/ppermute | solution.py:611
  123.3 3.7 %shard_map.77.refs_12_ = f32[2,256,1024]{2,1,0:T(8,128)} custom-call(s32[1]{0:T(128)} %bitcast.me_ref, s32[1]{0:T(128)} %bitcast.1.refs_10_.spot_ref, s32[4]{0:T(128)} %owner_ref.11, s32[8,2]{1,0:T(8,128)} %copy-done.18, s32[8,2]{1,0:T(8,128)} %copy-done.19, s32[8,2]{1,0:T(8,128)} %copy-done.20, s32[8,2]{1,0:T(8,128)} %copy-done.21, ...), custom_call_target="tpu_custom_call" | custom-call | tf_op jit(solution)/shard_map/pallas_call | solution.py:704
  127.1 1.9 %probe_sum.1 = f32[4,64,256]{2,1,0:T(8,128)} custom-call(f32[4,64,256]{2,1,0:T(8,128)} %get-tuple-element.48.own_ref, s16[272,256]{1,0:T(8,128)(2,1)} %copy-done.15, s16[272,256]{1,0:T(8,128)(2,1)} %copy-done.16, s16[272,256]{1,0:T(8,128)(2,1)} %copy-done.17), custom_call_target="tpu_custom_call" | custom-call | tf_op jit(solution)/shard_map/probe_sum/pallas_call | solution.py:691
  129.1 4.6 %shard_map.78.refs_8_ = f32[2,256,1024]{2,1,0:T(8,128)} custom-call(s32[1]{0:T(128)} %bitcast.me_ref, s32[1]{0:T(128)} %bitcast.1.refs_10_.spot_ref, s32[4]{0:T(128)} %owner_ref.11, s32[8,2]{1,0:T(8,128)} %copy-done.18, s32[8,2]{1,0:T(8,128)} %copy-done.19, s32[8,2]{1,0:T(8,128)} %copy-done.20, s32[8,2]{1,0:T(8,128)} %copy-done.21, ...), custom_call_target="tpu_custom_call" | custom-call | tf_op jit(solution)/shard_map/pallas_call | solution.py:704
  133.7 4.5 %shard_map.79 = f32[2,256,1024]{2,1,0:T(8,128)} custom-call(s32[1]{0:T(128)} %bitcast.me_ref, s32[1]{0:T(128)} %bitcast.1.refs_10_.spot_ref, s32[4]{0:T(128)} %owner_ref.11, s32[8,2]{1,0:T(8,128)} %copy-done.18, s32[8,2]{1,0:T(8,128)} %copy-done.19, s32[8,2]{1,0:T(8,128)} %copy-done.20, s32[8,2]{1,0:T(8,128)} %copy-done.21, s16[2,336,256]{2,1,0:T(8,128)(2,1)} %copy-done.2, ...), custom_call_target="tpu_custom_call" | custom-call | tf_op jit(solution)/shard_map/pallas_call | solution.py:704
  (110 shorter events, 18.1 us)
Async XLA Ops:
  0.6 5.1 %collective-permute-start = (s32[2,2]{1,0:T(2,128)}, s32[2,2]{1,0:T(2,128)S(1)}, u32[]{:S(2)}, u32[]{:S(2)}) collective-permute-start(s32[2,2]{1,0:T(2,128)} %off_ref.1), channel_id=1, source_target_pairs={{0,12},{4,0},{8,4},{12,8},{1,13},{5,1},{9,5},{13,9},{2,14},{6,2},{... | collective-permute-start | bytes 56 | tf_op jit(solution)/shard_map/ppermute | solution.py:607
  4.8 3.5 %collective-permute-start.1 = (s32[2,2]{1,0:T(2,128)}, s32[2,2]{1,0:T(2,128)S(1)}, u32[]{:S(2)}, u32[]{:S(2)}) collective-permute-start(s32[2,2]{1,0:T(2,128)} %off_ref.1), channel_id=1, source_target_pairs={{0,8},{4,12},{8,0},{12,4},{1,9},{5,13},{9,1},{13,5},{2,10},{6,14},... | collective-permute-start | bytes 56 | tf_op jit(solution)/shard_map/ppermute | solution.py:607
  4.8 4.4 %collective-permute-start.2 = (s32[2,2]{1,0:T(2,128)}, s32[2,2]{1,0:T(2,128)S(1)}, u32[]{:S(2)}, u32[]{:S(2)}) collective-permute-start(s32[2,2]{1,0:T(2,128)} %off_ref.1), channel_id=1, source_target_pairs={{0,4},{4,8},{8,12},{12,0},{1,5},{5,9},{9,13},{13,1},{2,6},{6,10},{... | collective-permute-start | bytes 56 | tf_op jit(solution)/shard_map/ppermute | solution.py:607
  19.7 12.2 %collective-permute-start.6 = (s32[8,2]{1,0:T(8,128)S(1)}, s32[8,2]{1,0:T(8,128)S(1)}, u32[]{:S(2)}, u32[]{:S(2)}) collective-permute-start(s32[8,2]{1,0:T(8,128)S(1)} %pad_add_fusion.refs_0_), channel_id=1, source_target_pairs={{0,2},{1,3},{2,0},{3,1},{4,6},{5,7},{6,4},{7,5},{8,10},{9,11},{10,... | collective-permute-start | bytes 200 | tf_op jit(solution)/shard_map/ppermute | solution.py:611
  20.9 11.5 %collective-permute-start.7 = (s32[8,2]{1,0:T(8,128)S(1)}, s32[8,2]{1,0:T(8,128)S(1)}, u32[]{:S(2)}, u32[]{:S(2)}) collective-permute-start(s32[8,2]{1,0:T(8,128)S(1)} %pad_add_fusion.refs_0_), channel_id=1, source_target_pairs={{0,1},{1,0},{2,3},{3,2},{4,5},{5,4},{6,7},{7,6},{8,9},{9,8},{10,11... | collective-permute-start | bytes 200 | tf_op jit(solution)/shard_map/ppermute | solution.py:611
  23.3 11.2 %collective-permute-start.3 = (bf16[2,320,256]{2,1,0:T(8,128)(2,1)S(1)}, bf16[2,320,256]{2,1,0:T(8,128)(2,1)S(1)}, u32[]{:S(2)}, u32[]{:S(2)}) collective-permute-start(bf16[2,320,256]{2,1,0:T(8,128)(2,1)S(1)} %copy-done.32), channel_id=1, source_target_pairs={{0,4},{4,8},{8,12},{12,0},{1,5},{5,9},{9,13},{13,1},{2,6},{6,10},{... | collective-permute-start | bytes 983048 | tf_op jit(solution)/shard_map/ppermute | solution.py:607
  23.3 24.3 %collective-permute-start.4 = (bf16[2,320,256]{2,1,0:T(8,128)(2,1)S(1)}, bf16[2,320,256]{2,1,0:T(8,128)(2,1)S(1)}, u32[]{:S(2)}, u32[]{:S(2)}) collective-permute-start(bf16[2,320,256]{2,1,0:T(8,128)(2,1)S(1)} %copy-done.31), channel_id=1, source_target_pairs={{0,8},{4,12},{8,0},{12,4},{1,9},{5,13},{9,1},{13,5},{2,10},{6,14},... | collective-permute-start | bytes 983048 | tf_op jit(solution)/shard_map/ppermute | solution.py:607
  24.2 23.4 %collective-permute-start.5 = (bf16[2,320,256]{2,1,0:T(8,128)(2,1)S(1)}, bf16[2,320,256]{2,1,0:T(8,128)(2,1)S(1)}, u32[]{:S(2)}, u32[]{:S(2)}) collective-permute-start(bf16[2,320,256]{2,1,0:T(8,128)(2,1)S(1)} %copy-done.30), channel_id=1, source_target_pairs={{0,12},{4,0},{8,4},{12,8},{1,13},{5,1},{9,5},{13,9},{2,14},{6,2},{... | collective-permute-start | bytes 983048 | tf_op jit(solution)/shard_map/ppermute | solution.py:607
  31.9 1.4 %collective-permute-start.8 = (s32[8,2]{1,0:T(8,128)S(1)}, s32[8,2]{1,0:T(8,128)S(1)}, u32[]{:S(2)}, u32[]{:S(2)}) collective-permute-start(s32[8,2]{1,0:T(8,128)S(1)} %collective-permute-done.6.refs_1_), channel_id=1, source_target_pairs={{0,1},{1,0},{2,3},{3,2},{4,5},{5,4},{6,7},{7,6},{8,9},{9,8},{10,11... | collective-permute-start | bytes 200 | tf_op jit(solution)/shard_map/ppermute | solution.py:611
  32.4 90.9 %copy-start.20 = (s32[8,2]{1,0:T(8,128)}, s32[8,2]{1,0:T(8,128)S(1)}, u32[]{:S(2)}) copy-start(s32[8,2]{1,0:T(8,128)S(1)} %collective-permute-done.7.refs_2_) | copy-start | bytes 196
  33.3 90.0 %copy-start.21 = (s32[8,2]{1,0:T(8,128)}, s32[8,2]{1,0:T(8,128)S(1)}, u32[]{:S(2)}) copy-start(s32[8,2]{1,0:T(8,128)S(1)} %collective-permute-done.8.refs_3_) | copy-start | bytes 196
  64.2 9.3 %collective-permute-start.24 = (f32[2,2,2,64,256]{4,3,2,1,0:T(8,128)}, f32[2,2,2,64,256]{4,3,2,1,0:T(8,128)S(1)}, u32[]{:S(2)}, u32[]{:S(2)}) collective-permute-start(f32[2,2,2,64,256]{4,3,2,1,0:T(8,128)} %get-tuple-element.47), channel_id=1, source_target_pairs={{0,1},{1,0},{2,3},{3,2},{4,5},{5,4},{6,7},{7,6},{8,9},{9,8},{10,11... | collective-permute-start | bytes 1572872 | tf_op jit(solution)/shard_map/ppermute | solution.py:611
  65.6 10.4 %collective-permute-start.21 = (s16[2,336,256]{2,1,0:T(8,128)(2,1)}, s16[2,336,256]{2,1,0:T(8,128)(2,1)S(1)}, u32[]{:S(2)}, u32[]{:S(2)}) collective-permute-start(s16[2,336,256]{2,1,0:T(8,128)(2,1)} %get-tuple-element.45.refs_4_), channel_id=1, source_target_pairs={{0,2},{1,3},{2,0},{3,1},{4,6},{5,7},{6,4},{7,5},{8,10},{9,11},{10,... | collective-permute-start | bytes 1032200 | tf_op jit(solution)/shard_map/ppermute | solution.py:611
  65.9 11.4 %collective-permute-start.22 = (s16[2,336,256]{2,1,0:T(8,128)(2,1)}, s16[2,336,256]{2,1,0:T(8,128)(2,1)S(1)}, u32[]{:S(2)}, u32[]{:S(2)}) collective-permute-start(s16[2,336,256]{2,1,0:T(8,128)(2,1)} %get-tuple-element.45.refs_4_), channel_id=1, source_target_pairs={{0,1},{1,0},{2,3},{3,2},{4,5},{5,4},{6,7},{7,6},{8,9},{9,8},{10,11... | collective-permute-start | bytes 1032200 | tf_op jit(solution)/shard_map/ppermute | solution.py:611
  66.2 15.8 %collective-permute-start.13 = (s16[2,336,256]{2,1,0:T(8,128)(2,1)}, s16[2,336,256]{2,1,0:T(8,128)(2,1)S(1)}, u32[]{:S(2)}, u32[]{:S(2)}) collective-permute-start(s16[2,336,256]{2,1,0:T(8,128)(2,1)} %get-tuple-element.43), channel_id=1, source_target_pairs={{0,4},{4,8},{8,12},{12,0},{1,5},{5,9},{9,13},{13,1},{2,6},{6,10},{... | collective-permute-start | bytes 1032200 | tf_op jit(solution)/shard_map/ppermute | solution.py:607
  73.0 16.7 %collective-permute-start.17 = (s16[2,336,256]{2,1,0:T(8,128)(2,1)}, s16[2,336,256]{2,1,0:T(8,128)(2,1)S(1)}, u32[]{:S(2)}, u32[]{:S(2)}) collective-permute-start(s16[2,336,256]{2,1,0:T(8,128)(2,1)} %get-tuple-element.44), channel_id=1, source_target_pairs={{0,12},{4,0},{8,4},{12,8},{1,13},{5,1},{9,5},{13,9},{2,14},{6,2},{... | collective-permute-start | bytes 1032200 | tf_op jit(solution)/shard_map/ppermute | solution.py:607
  73.5 30.9 %collective-permute-start.9 = (s16[2,336,256]{2,1,0:T(8,128)(2,1)}, s16[2,336,256]{2,1,0:T(8,128)(2,1)S(1)}, u32[]{:S(2)}, u32[]{:S(2)}) collective-permute-start(s16[2,336,256]{2,1,0:T(8,128)(2,1)} %get-tuple-element.42), channel_id=1, source_target_pairs={{0,8},{4,12},{8,0},{12,4},{1,9},{5,13},{9,1},{13,5},{2,10},{6,14},... | collective-permute-start | bytes 1032200 | tf_op jit(solution)/shard_map/ppermute | solution.py:607
  76.0 47.3 %copy-start.5 = (s16[2,336,256]{2,1,0:T(8,128)(2,1)}, s16[2,336,256]{2,1,0:T(8,128)(2,1)S(1)}, u32[]{:S(2)}) copy-start(s16[2,336,256]{2,1,0:T(8,128)(2,1)S(1)} %collective-permute-done.21.refs_5_) | copy-start | bytes 1032196
  76.0 28.8 %collective-permute-start.25 = (f32[2,2,64,256]{3,2,1,0:T(8,128)S(1)}, f32[2,2,64,256]{3,2,1,0:T(8,128)}, u32[]{:S(2)}, u32[]{:S(2)}) collective-permute-start(f32[2,2,64,256]{3,2,1,0:T(8,128)S(1)} %get-tuple-element.50), channel_id=1, source_target_pairs={{0,2},{1,3},{2,0},{3,1},{4,6},{5,7},{6,4},{7,5},{8,10},{9,11},{10,... | collective-permute-start | bytes 786440 | tf_op jit(solution)/shard_map/ppermute | solution.py:611
  77.2 30.6 %collective-permute-start.23 = (s16[2,336,256]{2,1,0:T(8,128)(2,1)S(1)}, s16[2,336,256]{2,1,0:T(8,128)(2,1)S(1)}, u32[]{:S(2)}, u32[]{:S(2)}) collective-permute-start(s16[2,336,256]{2,1,0:T(8,128)(2,1)S(1)} %collective-permute-done.21.refs_5_), channel_id=1, source_target_pairs={{0,1},{1,0},{2,3},{3,2},{4,5},{5,4},{6,7},{7,6},{8,9},{9,8},{10,11... | collective-permute-start | bytes 1032200 | tf_op jit(solution)/shard_map/ppermute | solution.py:611
  82.0 25.9 %collective-permute-start.14 = (s16[2,336,256]{2,1,0:T(8,128)(2,1)S(1)}, s16[2,336,256]{2,1,0:T(8,128)(2,1)S(1)}, u32[]{:S(2)}, u32[]{:S(2)}) collective-permute-start(s16[2,336,256]{2,1,0:T(8,128)(2,1)S(1)} %collective-permute-done.13.refs_4_), channel_id=1, source_target_pairs={{0,2},{1,3},{2,0},{3,1},{4,6},{5,7},{6,4},{7,5},{8,10},{9,11},{10,... | collective-permute-start | bytes 1032200 | tf_op jit(solution)/shard_map/ppermute | solution.py:611
  89.6 20.1 %collective-permute-start.18 = (s16[2,336,256]{2,1,0:T(8,128)(2,1)S(1)}, s16[2,336,256]{2,1,0:T(8,128)(2,1)S(1)}, u32[]{:S(2)}, u32[]{:S(2)}) collective-permute-start(s16[2,336,256]{2,1,0:T(8,128)(2,1)S(1)} %collective-permute-done.17.refs_8_), channel_id=1, source_target_pairs={{0,2},{1,3},{2,0},{3,1},{4,6},{5,7},{6,4},{7,5},{8,10},{9,11},{10,... | collective-permute-start | bytes 1032200 | tf_op jit(solution)/shard_map/ppermute | solution.py:611
  104.4 6.9 %collective-permute-start.15 = (s16[2,336,256]{2,1,0:T(8,128)(2,1)S(1)}, s16[2,336,256]{2,1,0:T(8,128)(2,1)S(1)}, u32[]{:S(2)}, u32[]{:S(2)}) collective-permute-start(s16[2,336,256]{2,1,0:T(8,128)(2,1)S(1)} %collective-permute-done.13.refs_4_), channel_id=1, source_target_pairs={{0,1},{1,0},{2,3},{3,2},{4,5},{5,4},{6,7},{7,6},{8,9},{9,8},{10,11... | collective-permute-start | bytes 1032200 | tf_op jit(solution)/shard_map/ppermute | solution.py:611
  104.8 9.6 %collective-permute-start.10 = (s16[2,336,256]{2,1,0:T(8,128)(2,1)S(1)}, s16[2,336,256]{2,1,0:T(8,128)(2,1)S(1)}, u32[]{:S(2)}, u32[]{:S(2)}) collective-permute-start(s16[2,336,256]{2,1,0:T(8,128)(2,1)S(1)} %collective-permute-done.9.refs_4_), channel_id=1, source_target_pairs={{0,2},{1,3},{2,0},{3,1},{4,6},{5,7},{6,4},{7,5},{8,10},{9,11},{10,... | collective-permute-start | bytes 1032200 | tf_op jit(solution)/shard_map/ppermute | solution.py:611
  107.9 7.5 %collective-permute-start.26 = (s16[272,256]{1,0:T(8,128)(2,1)}, s16[272,256]{1,0:T(8,128)(2,1)S(1)}, u32[]{:S(2)}, u32[]{:S(2)}) collective-permute-start(s16[272,256]{1,0:T(8,128)(2,1)} %get-tuple-element.49), channel_id=1, source_target_pairs={{0,4},{4,8},{8,12},{12,0},{1,5},{5,9},{9,13},{13,1},{2,6},{6,10},{... | collective-permute-start | bytes 417800 | tf_op jit(solution)/shard_map/ppermute | solution.py:607
  107.9 12.1 %collective-permute-start.27 = (s16[272,256]{1,0:T(8,128)(2,1)}, s16[272,256]{1,0:T(8,128)(2,1)S(1)}, u32[]{:S(2)}, u32[]{:S(2)}) collective-permute-start(s16[272,256]{1,0:T(8,128)(2,1)} %get-tuple-element.49), channel_id=1, source_target_pairs={{0,8},{4,12},{8,0},{12,4},{1,9},{5,13},{9,1},{13,5},{2,10},{6,14},... | collective-permute-start | bytes 417800 | tf_op jit(solution)/shard_map/ppermute | solution.py:607
  109.7 12.3 %collective-permute-start.28 = (s16[272,256]{1,0:T(8,128)(2,1)}, s16[272,256]{1,0:T(8,128)(2,1)S(1)}, u32[]{:S(2)}, u32[]{:S(2)}) collective-permute-start(s16[272,256]{1,0:T(8,128)(2,1)} %get-tuple-element.49), channel_id=1, source_target_pairs={{0,12},{4,0},{8,4},{12,8},{1,13},{5,1},{9,5},{13,9},{2,14},{6,2},{... | collective-permute-start | bytes 417800 | tf_op jit(solution)/shard_map/ppermute | solution.py:607
  111.3 17.8 %collective-permute-start.19 = (s16[2,336,256]{2,1,0:T(8,128)(2,1)S(1)}, s16[2,336,256]{2,1,0:T(8,128)(2,1)}, u32[]{:S(2)}, u32[]{:S(2)}) collective-permute-start(s16[2,336,256]{2,1,0:T(8,128)(2,1)S(1)} %collective-permute-done.17.refs_8_), channel_id=1, source_target_pairs={{0,1},{1,0},{2,3},{3,2},{4,5},{5,4},{6,7},{7,6},{8,9},{9,8},{10,11... | collective-permute-start | bytes 1032200 | tf_op jit(solution)/shard_map/ppermute | solution.py:611
  114.4 14.7 %collective-permute-start.16 = (s16[2,336,256]{2,1,0:T(8,128)(2,1)S(1)}, s16[2,336,256]{2,1,0:T(8,128)(2,1)}, u32[]{:S(2)}, u32[]{:S(2)}) collective-permute-start(s16[2,336,256]{2,1,0:T(8,128)(2,1)S(1)} %collective-permute-done.14.refs_5_), channel_id=1, source_target_pairs={{0,1},{1,0},{2,3},{3,2},{4,5},{5,4},{6,7},{7,6},{8,9},{9,8},{10,11... | collective-permute-start | bytes 1032200 | tf_op jit(solution)/shard_map/ppermute | solution.py:611
  115.3 13.7 %collective-permute-start.20 = (s16[2,336,256]{2,1,0:T(8,128)(2,1)S(1)}, s16[2,336,256]{2,1,0:T(8,128)(2,1)}, u32[]{:S(2)}, u32[]{:S(2)}) collective-permute-start(s16[2,336,256]{2,1,0:T(8,128)(2,1)S(1)} %collective-permute-done.18.refs_9_), channel_id=1, source_target_pairs={{0,1},{1,0},{2,3},{3,2},{4,5},{5,4},{6,7},{7,6},{8,9},{9,8},{10,11... | collective-permute-start | bytes 1032200 | tf_op jit(solution)/shard_map/ppermute | solution.py:611
  120.0 13.7 %collective-permute-start.11 = (s16[2,336,256]{2,1,0:T(8,128)(2,1)S(1)}, s16[2,336,256]{2,1,0:T(8,128)(2,1)}, u32[]{:S(2)}, u32[]{:S(2)}) collective-permute-start(s16[2,336,256]{2,1,0:T(8,128)(2,1)S(1)} %collective-permute-done.9.refs_4_), channel_id=1, source_target_pairs={{0,1},{1,0},{2,3},{3,2},{4,5},{5,4},{6,7},{7,6},{8,9},{9,8},{10,11... | collective-permute-start | bytes 1032200 | tf_op jit(solution)/shard_map/ppermute | solution.py:611
  122.7 11.0 %collective-permute-start.12 = (s16[2,336,256]{2,1,0:T(8,128)(2,1)S(1)}, s16[2,336,256]{2,1,0:T(8,128)(2,1)}, u32[]{:S(2)}, u32[]{:S(2)}) collective-permute-start(s16[2,336,256]{2,1,0:T(8,128)(2,1)S(1)} %collective-permute-done.10.refs_5_), channel_id=1, source_target_pairs={{0,1},{1,0},{2,3},{3,2},{4,5},{5,4},{6,7},{7,6},{8,9},{9,8},{10,11... | collective-permute-start | bytes 1032200 | tf_op jit(solution)/shard_map/ppermute | solution.py:611
  (30 other events, 401.1 us)

commit v3 on v2

--- a/solution.py
+++ b/solution.py
@@ -152,6 +152,10 @@
         probe_total, lax.axis_index("pos") * row_share, row_share, 2
     )
     return (strip_part, probe_out)
+
+
+def grant(mib):
+    return pltpu.CompilerParams(vmem_limit_bytes=mib << 20)
 
 
 def strip_held(owner_ref, me, count):
@@ -301,7 +305,7 @@
     grads = refs[tiles + 7 : 2 * tiles + 7]
     away_ref, kept_ref = refs[2 * tiles + 7 : 2 * tiles + 9]
     (
-        held, cat, wins, far, factor, right_a, right_b, left_a, left_b, obj_acc, probe_acc, gcat, outer_acc, gpack,
+        held, cat, wins, far, factor, right_m, left_m, obj_acc, probe_acc, gcat, outer_acc, gpack,
         in_sem, out_sem, piece_sem,
     ) = refs[2 * tiles + 9 :]
     half = win // 2
@@ -313,25 +317,15 @@
 
     for way in range(2):
         if way == 0:
-            r_re, r_im = prop_t_re[...], prop_t_im[...]
-            l_re, l_im = prop_re[...], prop_im[...]
+            right, left = (prop_t_re[...], prop_t_im[...]), (prop_re[...], prop_im[...])
         else:
-            r_re, r_im = prop_re[...], -prop_im[...]
-            l_re, l_im = prop_t_re[...], -prop_t_im[...]
-        (rr, rr_low), (ri, ri_low) = halves(r_re), halves(r_im)
-        for row, (a, b) in enumerate([(rr, ri), (rr, ri), (-ri, rr), (-ri, rr)]):
-            right_a[way, row * win : (row + 1) * win, 0:win] = a
-            right_a[way, row * win : (row + 1) * win, win : 2 * win] = b
-        for row, (a, b) in enumerate([(rr_low, ri_low), (-ri_low, rr_low)]):
-            right_b[way, row * win : (row + 1) * win, 0:win] = a
-            right_b[way, row * win : (row + 1) * win, win : 2 * win] = b
-        (lr, lr_low), (li, li_low) = halves(l_re), halves(l_im)
-        for col, (a, b) in enumerate([(lr, li), (lr, li), (-li, lr), (-li, lr)]):
-            left_a[way, 0:win, col * win : (col + 1) * win] = a
-            left_a[way, win : 2 * win, col * win : (col + 1) * win] = b
-        for col, (a, b) in enumerate([(lr_low, li_low), (-li_low, lr_low)]):
-            left_b[way, 0:win, col * win : (col + 1) * win] = a
-            left_b[way, win : 2 * win, col * win : (col + 1) * win] = b
+            right, left = (prop_re[...], -prop_im[...]), (prop_t_re[...], -prop_t_im[...])
+        for at, (r, l) in enumerate(zip(right + (right[0] + right[1],), left + (left[0] + left[1],))):
+            r_h, r_l = halves(r)
+            l_h, l_l = halves(l)
+            for third, (rr, ll) in enumerate([(r_h, l_h), (r_h, l_h), (r_l, l_l)]):
+                right_m[way, at, third * win : (third + 1) * win, :] = rr
+                left_m[way, at, :, third * win : (third + 1) * win] = ll
 
     y_up, x_up, x_low, first = geometry(off_ref[0, 0], off_ref[0, 1], off_ref[1, 0], off_ref[1, 1])
     right = x_low > x_up
@@ -363,33 +357,38 @@
         wins[1, part, 0:half, 0:half] = jnp.where(right, upper[half:win, half:win], outer)
         wins[1, part, 0:half, half:win] = jnp.where(right, outer, upper[half:win, 0:half])
 
+    def three(re, im, side):
+        both_re, both_im, both_sum = side(re, 0), side(im, 1), side(re + im, 2)
+        return both_re - both_im, both_sum - both_re - both_im
+
     def both(way, re, im):
-        (re_h, re_l), (im_h, im_l) = halves(re), halves(im)
-        mid = dot(jnp.concatenate([re_h, re_l, im_h, im_l], axis=1), right_a[way]) + dot(
-            jnp.concatenate([re_h, im_h], axis=1), right_b[way]
-        )
-        (re_h, re_l), (im_h, im_l) = halves(mid[:, 0:win]), halves(mid[:, win : 2 * win])
-        return dot(left_a[way], jnp.concatenate([re_h, re_l, im_h, im_l], axis=0)) + dot(
-            left_b[way], jnp.concatenate([re_h, im_h], axis=0)
-        )
+        def from_right(x, at):
+            high, low = halves(x)
+            return dot(jnp.concatenate([high, low, high], axis=1), right_m[way, at])
+
+        def from_left(x, at):
+            high, low = halves(x)
+            return dot(left_m[way, at], jnp.concatenate([high, low, high], axis=0))
+
+        return three(*three(re, im, from_right), from_left)
 
     def forward(n, carry):
         q = n // modes
         m = lax.rem(n, modes)
         p_re, p_im = probe[m, 0], probe[m, 1]
         w_re, w_im = wins[q, 0], wins[q, 1]
-        far[n] = both(0, p_re * w_re - p_im * w_im, p_re * w_im + p_im * w_re)
+        far[n, 0:win, :], far[n, win : 2 * win, :] = both(0, p_re * w_re - p_im * w_im, p_re * w_im + p_im * w_re)
         return carry
 
-    lax.fori_loop(0, 2 * modes, forward, 0)
+    lax.fori_loop(0, 2 * modes, forward, 0, unroll=2)
     for q in range(2):
         total = jnp.zeros((win, win), jnp.float32)
         for m in range(modes):
             f_re, f_im = far[q * modes + m, 0:win, :], far[q * modes + m, win : 2 * win, :]
             total = total + (f_re * f_re + f_im * f_im)
         frame = jnp.where(first, q, 1 - q)
-        measured = amp[frame].astype(jnp.float32)
-        factor[q] = (1.0 - measured / jnp.maximum(jnp.sqrt(total), 1.0)) * grad_scale
+        measured = amp[frame]
+        factor[q] = (1.0 - measured * lax.rsqrt(jnp.maximum(total, 1.0))) * grad_scale
     obj_acc[...] = jnp.zeros_like(obj_acc)
     probe_acc[...] = jnp.zeros_like(probe_acc)
 
@@ -397,8 +396,7 @@
         q = n // modes
         m = lax.rem(n, modes)
         scale = factor[q]
-        back = both(1, far[n, 0:win, :] * scale, far[n, win : 2 * win, :] * scale)
-        b_re, b_im = back[0:win, :], back[win : 2 * win, :]
+        b_re, b_im = both(1, far[n, 0:win, :] * scale, far[n, win : 2 * win, :] * scale)
         p_re, p_im = probe[m, 0], probe[m, 1]
         w_re, w_im = wins[q, 0], wins[q, 1]
         obj_acc[q, 0] = obj_acc[q, 0] + (p_re * b_re + p_im * b_im)
@@ -407,7 +405,7 @@
         probe_acc[m, 1] = probe_acc[m, 1] + (w_re * b_im - w_im * b_re)
         return carry
 
-    lax.fori_loop(0, 2 * modes, backward, 0)
+    lax.fori_loop(0, 2 * modes, backward, 0, unroll=2)
     share = win // pos_groups
     spot = spot_ref[0]
     piece_copies = []
@@ -474,10 +472,8 @@
             pltpu.VMEM((2, 2, win, win), jnp.float32),
             pltpu.VMEM((2 * modes, 2 * win, win), jnp.float32),
             pltpu.VMEM((2, win, win), jnp.float32),
-            pltpu.VMEM((2, 4 * win, 2 * win), jnp.bfloat16),
-            pltpu.VMEM((2, 2 * win, 2 * win), jnp.bfloat16),
-            pltpu.VMEM((2, 2 * win, 4 * win), jnp.bfloat16),
-            pltpu.VMEM((2, 2 * win, 2 * win), jnp.bfloat16),
+            pltpu.VMEM((2, 3, 3 * win, win), jnp.bfloat16),
+            pltpu.VMEM((2, 3, win, 3 * win), jnp.bfloat16),
             pltpu.VMEM((2, 2, win, win), jnp.float32),
             pltpu.VMEM((modes, 2, win, win), jnp.float32),
             pltpu.VMEM((2, 3 * win, win), jnp.float32),
@@ -487,17 +483,32 @@
             pltpu.SemaphoreType.DMA((tiles,)),
             pltpu.SemaphoreType.DMA((pos_groups,)),
         ],
+        compiler_params=grant(40),
         name="propagate",
     )
 
 
-def probe_pack_kernel(blocks, rows, kept_ref, came_ref, total_ref, pack_ref):
+def packed(total, pack_ref, b, rows):
+    code = code_of(column_peak(total))
+    pack_ref[b * rows : (b + 1) * rows, :] = to_levels(total, code)
+    return code
+
+
+def probe_cross_kernel(blocks, rows, kept_ref, came_ref, total_ref, pack_ref):
     codes = []
     for b in range(blocks):
-        total = kept_ref[b] + came_ref[b]
+        total_ref[b] = kept_ref[0, b] + came_ref[0, b]
+        codes.append(packed(kept_ref[1, b] + came_ref[1, b], pack_ref, b, rows))
+    pack_ref[blocks * rows : blocks * rows + 16, :] = code_rows(codes)
+
+
+def probe_close_kernel(blocks, rows, kept_ref, came_ref, total_ref, pack_ref):
+    scale = step_of(wide_of(came_ref[blocks * rows : blocks * rows + 16, :]))
+    codes = []
+    for b in range(blocks):
+        total = kept_ref[b] + wide_of(came_ref[b * rows : (b + 1) * rows, :]) * scale[b : b + 1, :]
         total_ref[b] = total
-        codes.append(code_of(column_peak(total)))
-        pack_ref[b * rows : (b + 1) * rows, :] = to_levels(total, codes[-1])
+        codes.append(packed(total, pack_ref, b, rows))
     pack_ref[blocks * rows : blocks * rows + 16, :] = code_rows(codes)
 
 
@@ -565,35 +576,42 @@
             lanes = lane_iota((quarter, half))
             stay = lanes >= rem
 
-            for part in range(2):
-                steps = step_of(wide_of(held[n, part, win + quarter : win + quarter + 16, :]))
-                for chunk in range(4):
-                    row0 = chunk * quarter
-                    level = chunk // 2
-                    rows = base + row0 + row_iota((quarter, half))
-                    low_first = (rows < y_up + win).astype(jnp.int32) == right
-                    in_outer = (rows >= y_up + half) & (rows < y_up + win)
-                    main = wide_of(held[n, part, row0 : row0 + quarter, :]) * steps[level : level + 1, :]
-                    m0 = main[:, 0:half]
-                    m1 = main[:, half:win]
-                    side = held[n, part, win : win + quarter, half * (chunk % 2) : half * (chunk % 2 + 1)]
-                    side = jnp.where(in_outer, wide_of(side) * steps[2:3, 0:half], 0.0)
-                    cols = [
-                        jnp.where(low_first, m0, jnp.where(right == 0, side, 0.0)),
-                        jnp.where(low_first, m1, m0),
-                        jnp.where(low_first, jnp.where(right == 1, side, 0.0), m1),
-                    ]
-                    spun = [pltpu.roll(c, rem, 1) for c in cols]
-                    zero = jnp.zeros_like(m0)
-                    shifted = [
-                        jnp.where(stay, spun[0], zero),
-                        jnp.where(stay, spun[1], spun[0]),
-                        jnp.where(stay, spun[2], spun[1]),
-                        jnp.where(stay, zero, spun[2]),
-                    ]
-                    for b in range(4):
-                        at = pl.ds(pl.multiple_of(start + b * half, 128), half)
-                        acc[part, row0 : row0 + quarter, at] += shifted[b]
+            def strip_piece(part, chunk, steps):
+                row0 = chunk * quarter
+                level = chunk // 2
+                rows = base + row0 + row_iota((quarter, half))
+                low_first = (rows < y_up + win).astype(jnp.int32) == right
+                in_outer = (rows >= y_up + half) & (rows < y_up + win)
+                main = wide_of(held[n, part, row0 : row0 + quarter, :]) * steps[level : level + 1, :]
+                m0 = main[:, 0:half]
+                m1 = main[:, half:win]
+                side = held[n, part, win : win + quarter, half * (chunk % 2) : half * (chunk % 2 + 1)]
+                side = jnp.where(in_outer, wide_of(side) * steps[2:3, 0:half], 0.0)
+                cols = [
+                    jnp.where(low_first, m0, jnp.where(right == 0, side, 0.0)),
+                    jnp.where(low_first, m1, m0),
+                    jnp.where(low_first, jnp.where(right == 1, side, 0.0), m1),
+                ]
+                spun = [pltpu.roll(c, rem, 1) for c in cols]
+                zero = jnp.zeros_like(m0)
+                moved = [
+                    jnp.where(stay, spun[0], zero),
+                    jnp.where(stay, spun[1], spun[0]),
+                    jnp.where(stay, spun[2], spun[1]),
+                    jnp.where(stay, zero, spun[2]),
+                ]
+                for b in range(4):
+                    at = pl.ds(pl.multiple_of(start + b * half, 128), half)
+                    acc[part, row0 : row0 + quarter, at] += moved[b]
+
+            steps = [step_of(wide_of(held[n, part, win + quarter : win + quarter + 16, :])) for part in range(2)]
+            for chunk in range(4):
+                low = base + chunk * quarter
+
+                @pl.when((low < y_up + span) & (low + quarter > y_up))
+                def _():
+                    for part in range(2):
+                        strip_piece(part, chunk, steps[part])
 
         return carry
 
@@ -645,6 +663,7 @@
                 pltpu.SemaphoreType.DMA((asked,)),
                 pltpu.SemaphoreType.DMA((asked,)),
             ],
+            compiler_params=grant(60),
             name="pack",
         )(me, strip_owner, *asking, field)
 
@@ -658,9 +677,10 @@
         bit //= 2
     arrived = [packs[0]] + [shifted(packs[k], "tile", tiles, k) for k in range(1, tiles)]
     prop_re, prop_im = build_propagator(chirp)
+    measured = lax.optimization_barrier((amplitude, chirp))[0].astype(jnp.float32)
     arrived, column_offs = lax.optimization_barrier((arrived, column_offs))
     results = propagate_call(tiles, pos_groups, win, modes, grad_scale)(
-        me, strip_owner, offsets, *arrived, probe, amplitude, prop_re, prop_im, prop_re.T, prop_im.T, spot
+        me, strip_owner, offsets, *arrived, probe, measured, prop_re, prop_im, prop_re.T, prop_im.T, spot
     )
     grads, (away, kept) = results[:tiles], results[tiles:]
 
@@ -671,26 +691,29 @@
         columns = columns + [[swapped(x, "pos", pos_groups, bit) for x in column] for column in columns]
         bit //= 2
 
-    kept = kept + swapped(away, "pos", pos_groups, 1)
-    bit = 2
-    while kept.shape[0] > 2:
-        kept = kept[0::2] + swapped(kept[1::2], "pos", pos_groups, bit)
-        bit *= 2
     blocks = modes * 2
-    came = swapped(kept[1], "pos", pos_groups, bit)
-    probe_own, probe_pack = pl.pallas_call(
-        functools.partial(probe_pack_kernel, blocks, share),
-        out_shape=[
-            jax.ShapeDtypeStruct((blocks, share, win), jnp.float32),
-            jax.ShapeDtypeStruct((blocks * share + 16, win), jnp.int16),
-        ],
-        name="probe_pack",
-    )(kept[0].reshape(blocks, share, win), came.reshape(blocks, share, win))
+
+    def probe_step(kernel, *parts):
+        return pl.pallas_call(
+            functools.partial(kernel, blocks, share),
+            out_shape=[
+                jax.ShapeDtypeStruct((blocks, share, win), jnp.float32),
+                jax.ShapeDtypeStruct((blocks * share + 16, win), jnp.int16),
+            ],
+            compiler_params=grant(8),
+        )(*parts)
+
+    pair = (2, blocks, share, win)
+    came = swapped(away, "pos", pos_groups, 1).reshape(pair)
+    probe_own, probe_pack = probe_step(probe_cross_kernel, kept.reshape(pair), came)
+    came = swapped(probe_pack, "pos", pos_groups, 2)
+    probe_own, probe_pack = probe_step(probe_close_kernel, probe_own, came)
     probe_packs = [shifted(probe_pack, "tile", tiles, k) for k in range(1, tiles)]
 
     probe_out = pl.pallas_call(
         functools.partial(probe_sum_kernel, blocks, share),
         out_shape=jax.ShapeDtypeStruct((blocks, share, win), jnp.float32),
+        compiler_params=grant(4),
         name="probe_sum",
     )(probe_own, *probe_packs)
 
@@ -713,6 +736,7 @@
                 pltpu.SemaphoreType.DMA((count,)),
                 pltpu.SemaphoreType.DMA,
             ],
+            compiler_params=grant(16),
         )(me, spot, strip_owner, *column_offs, *arrays, *([] if first else [placed]))
     return (placed, probe_out.reshape(modes, 2, share, win))
 
@@ -725,10 +749,9 @@
         pos_count == 2
         and object_field.shape[1] == win
         and win == 256
-        and pos_groups & (pos_groups - 1) == 0
         and width // pos_groups >= 2 * win
         and (width // pos_groups) % 128 == 0
-        and pos_groups >= 4
+        and pos_groups == 4
         and (win // pos_groups) % 16 == 0
     )
     if not packed:

time: 140 us -> 127 us (0.907)
  the two profiles are of different devices: /device:TPU:1 before, /device:TPU:9 now
where the time goes in v3:
time: 127 us
  waiting for transfers between devices  56 us (44%)
  starting transfers between devices  31.9 us (25%)
  Pallas kernels  28.9 us (23%)
  matrix products  6.61 us (5%)
    ppermute x12, waiting for transfers between devices, shifted(): return lax.ppermute(x, axis, [(i, (i + k) % count) for i in range(count)])  46.3 us
    ppermute x12, starting transfers between devices, shifted(): return lax.ppermute(x, axis, [(i, (i + k) % count) for i in range(count)])  16.2 us
    ppermute x17, starting transfers between devices, swapped(): return lax.ppermute(x, axis, [(i, i ^ bit) for i in range(count)])  15.7 us
    pallas_call x1, Pallas kernels, per_device_packed(): propagate_call(tiles, pos_groups, win, modes, grad_scale)  11.6 us
    pallas_call x3, Pallas kernels, per_device_packed(): pl.pallas_call(functools.partial(place_kernel, tiles, spots, steps_back,...  10 us
    ppermute x17, waiting for transfers between devices, swapped(): return lax.ppermute(x, axis, [(i, i ^ bit) for i in range(count)])  9.78 us
    pallas_call x2, Pallas kernels, pack_for(): pl.pallas_call(functools.partial(pack_kernel, tiles, asked, win, width),...  6.18 us
  transfers between devices with their start and end apart: 29, of which 11 were waited for; matrix products, arithmetic and copies ran while one was open for 4% of the time, Pallas kernels for 6%

profile of v3, /device:TPU:9, one launch (start us, length us, event | category | flops | bytes accessed | tf_op | source)
XLA Modules:
  0.0 126.5 jit_solution(6457259222640978790)
XLA Ops:
  0.7 2.5 %collective-permute-start.1 = (s32[2,2]{1,0:T(2,128)}, s32[2,2]{1,0:T(2,128)S(1)}, u32[]{:S(2)}, u32[]{:S(2)}) collective-permute-start(s32[2,2]{1,0:T(2,128)} %off_ref.1), channel_id=1, source_target_pairs={{0,8},{4,12},{8,0},{12,4},{1,9},{5,13},{9,1},{13,5},{2,10},{6,14},... | collective-permute-start | bytes 56 | tf_op jit(solution)/shard_map/ppermute | solution.py:625
  3.2 2.2 %collective-permute-start.2 = (s32[2,2]{1,0:T(2,128)}, s32[2,2]{1,0:T(2,128)S(1)}, u32[]{:S(2)}, u32[]{:S(2)}) collective-permute-start(s32[2,2]{1,0:T(2,128)} %off_ref.1), channel_id=1, source_target_pairs={{0,4},{4,8},{8,12},{12,0},{1,5},{5,9},{9,13},{13,1},{2,6},{6,10},{... | collective-permute-start | bytes 56 | tf_op jit(solution)/shard_map/ppermute | solution.py:625
  6.9 3.4 %pack.2 = (bf16[2,320,256]{2,1,0:T(8,128)(2,1)}, bf16[2,320,256]{2,1,0:T(8,128)(2,1)}, bf16[2,320,256]{2,1,0:T(8,128)(2,1)}) custom-call(s32[1]{0:T(128)} %bitcast.me_ref, s32[4]{0:T(128)} %owner_ref.11, s32[2,2]{1,0:T(2,128)} %copy-done.4, s32[2,2]{1,0:T(2,128)} %copy-done.6, s32[2,2]{1,0:T(2,128)} %copy-done.8, bf16[2,256,4096]{2,1,0:T(8,128)(2,1)} %refs_1_.1), custom_call_target="tpu_custom_call" | custom-call | tf_op jit(solution)/shard_map/pack/pallas_call | solution.py:654
  10.4 1.7 %fusion.8 = f32[256,256]{0,1:T(8,128)S(1)} fusion(f32[256]{0:T(256)S(1)} %get-tuple-element.57, f32[256]{0:T(256)S(1)} %get-tuple-element.56), kind=kOutput, calls=%fused_computation.16 | convolution fusion | flops 203489280 | bytes 264192 | tf_op jit(solution)/shard_map/dot_general | solution.py:34
  12.0 1.7 %fusion.10 = f32[256,256]{0,1:T(8,128)S(1)} fusion(f32[256]{0:T(256)S(1)} %get-tuple-element.57, f32[256]{0:T(256)S(1)} %get-tuple-element.56), kind=kOutput, calls=%fused_computation.18 | convolution fusion | flops 203489280 | bytes 264192 | tf_op jit(solution)/shard_map/dot_general | solution.py:31
  13.7 2.8 %pack.3.refs_0_ = bf16[2,320,256]{2,1,0:T(8,128)(2,1)} custom-call(s32[1]{0:T(128)} %bitcast.me_ref, s32[4]{0:T(128)} %owner_ref.11, s32[2,2]{1,0:T(2,128)} %off_ref.1, bf16[2,256,4096]{2,1,0:T(8,128)(2,1)} %refs_1_.1), custom_call_target="tpu_custom_call" | custom-call | tf_op jit(solution)/shard_map/pack/pallas_call | solution.py:654
  16.6 1.3 %collective-permute-start.6 = (s32[8,2]{1,0:T(8,128)S(1)}, s32[8,2]{1,0:T(8,128)S(1)}, u32[]{:S(2)}, u32[]{:S(2)}) collective-permute-start(s32[8,2]{1,0:T(8,128)S(1)} %pad_add_fusion.refs_0_), channel_id=1, source_target_pairs={{0,2},{1,3},{2,0},{3,1},{4,6},{5,7},{6,4},{7,5},{8,10},{9,11},{10,... | collective-permute-start | bytes 200 | tf_op jit(solution)/shard_map/ppermute | solution.py:629
  17.8 2.4 %collective-permute-start.7 = (s32[8,2]{1,0:T(8,128)S(1)}, s32[8,2]{1,0:T(8,128)S(1)}, u32[]{:S(2)}, u32[]{:S(2)}) collective-permute-start(s32[8,2]{1,0:T(8,128)S(1)} %pad_add_fusion.refs_0_), channel_id=1, source_target_pairs={{0,1},{1,0},{2,3},{3,2},{4,5},{5,4},{6,7},{7,6},{8,9},{9,8},{10,11... | collective-permute-start | bytes 200 | tf_op jit(solution)/shard_map/ppermute | solution.py:629
  20.2 2.0 %collective-permute-start.3 = (bf16[2,320,256]{2,1,0:T(8,128)(2,1)}, bf16[2,320,256]{2,1,0:T(8,128)(2,1)S(1)}, u32[]{:S(2)}, u32[]{:S(2)}) collective-permute-start(bf16[2,320,256]{2,1,0:T(8,128)(2,1)} %get-tuple-element.33), channel_id=1, source_target_pairs={{0,4},{4,8},{8,12},{12,0},{1,5},{5,9},{9,13},{13,1},{2,6},{6,10},{... | collective-permute-start | bytes 983048 | tf_op jit(solution)/shard_map/ppermute | solution.py:625
  22.2 2.4 %collective-permute-start.4 = (bf16[2,320,256]{2,1,0:T(8,128)(2,1)}, bf16[2,320,256]{2,1,0:T(8,128)(2,1)S(1)}, u32[]{:S(2)}, u32[]{:S(2)}) collective-permute-start(bf16[2,320,256]{2,1,0:T(8,128)(2,1)} %get-tuple-element.34), channel_id=1, source_target_pairs={{0,8},{4,12},{8,0},{12,4},{1,9},{5,13},{9,1},{13,5},{2,10},{6,14},... | collective-permute-start | bytes 983048 | tf_op jit(solution)/shard_map/ppermute | solution.py:625
  24.6 1.6 %convolution_subtract_fusion = f32[256,256]{0,1:T(8,128)S(1)} fusion(f32[256,256]{0,1:T(8,128)S(1)} %fusion.8, f32[256]{0:T(256)S(1)} %get-tuple-element.57, f32[256]{0:T(256)S(1)} %get-tuple-element.56), kind=kOutput, calls=%fused_computation | convolution fusion | flops 203620352 | bytes 526336 | tf_op jit(solution)/shard_map/dot_general | solution.py:34
  26.5 1.7 %convolution_add_fusion = f32[256,256]{0,1:T(8,128)S(1)} fusion(f32[256,256]{0,1:T(8,128)S(1)} %fusion.10, f32[256]{0:T(256)S(1)} %get-tuple-element.57, f32[256]{0:T(256)S(1)} %get-tuple-element.56), kind=kOutput, calls=%fused_computation.1 | convolution fusion | flops 203620352 | bytes 526336 | tf_op jit(solution)/shard_map/dot_general | solution.py:31
  28.2 1.0 convert_element_type.20.refs_5_
  30.8 19.8 %collective-permute-done.4.refs_2_ = bf16[2,320,256]{2,1,0:T(8,128)(2,1)S(1)} collective-permute-done((bf16[2,320,256]{2,1,0:T(8,128)(2,1)}, bf16[2,320,256]{2,1,0:T(8,128)(2,1)S(1)}, u32[]{:S(2)}, u32[]{:S(2)}) %collective-permute-start.4) | collective-permute-done | bytes 327712 | tf_op jit(solution)/shard_map/ppermute | solution.py:625
  50.6 2.2 %collective-permute-done.5.refs_3_ = bf16[2,320,256]{2,1,0:T(8,128)(2,1)S(1)} collective-permute-done((bf16[2,320,256]{2,1,0:T(8,128)(2,1)}, bf16[2,320,256]{2,1,0:T(8,128)(2,1)S(1)}, u32[]{:S(2)}, u32[]{:S(2)}) %collective-permute-start.5) | collective-permute-done | bytes 327712 | tf_op jit(solution)/shard_map/ppermute | solution.py:625
  52.9 11.6 %propagate.1 = (s16[2,336,256]{2,1,0:T(8,128)(2,1)S(1)}, s16[2,336,256]{2,1,0:T(8,128)(2,1)S(1)}, s16[2,336,256]{2,1,0:T(8,128)(2,1)S(1)}, s16[2,336,256]{2,1,0:...) custom-call(s32[1]{0:T(128)} %bitcast.me_ref, s32[4]{0:T(128)S(1)} %copy-done.2, ...), custom_call_target="tpu_custom_call" | custom-call | tf_op jit(solution)/shard_map/propagate/pallas_call | solution.py:682
  66.1 1.5 %collective-permute-start.17 = (s16[2,336,256]{2,1,0:T(8,128)(2,1)S(1)}, s16[2,336,256]{2,1,0:T(8,128)(2,1)S(1)}, u32[]{:S(2)}, u32[]{:S(2)}) collective-permute-start(s16[2,336,256]{2,1,0:T(8,128)(2,1)S(1)} %get-tuple-element.48), channel_id=1, source_target_pairs={{0,12},{4,0},{8,4},{12,8},{1,13},{5,1},{9,5},{13,9},{2,14},{6,2},{... | collective-permute-start | bytes 1032200 | tf_op jit(solution)/shard_map/ppermute | solution.py:625
  68.5 6.5 %collective-permute-done.21.refs_5_ = s16[2,336,256]{2,1,0:T(8,128)(2,1)S(1)} collective-permute-done((s16[2,336,256]{2,1,0:T(8,128)(2,1)S(1)}, s16[2,336,256]{2,1,0:T(8,128)(2,1)S(1)}, u32[]{:S(2)}, u32[]{:S(2)}) %collective-permute-start.21) | collective-permute-done | bytes 344096 | tf_op jit(solution)/shard_map/ppermute | solution.py:629
  75.2 1.2 collective-permute-start.23
  76.5 1.2 collective-permute-start.14
  77.7 5.3 %collective-permute-done.17.refs_8_ = s16[2,336,256]{2,1,0:T(8,128)(2,1)S(1)} collective-permute-done((s16[2,336,256]{2,1,0:T(8,128)(2,1)S(1)}, s16[2,336,256]{2,1,0:T(8,128)(2,1)S(1)}, u32[]{:S(2)}, u32[]{:S(2)}) %collective-permute-start.17) | collective-permute-done | bytes 344096 | tf_op jit(solution)/shard_map/ppermute | solution.py:625
  83.0 1.2 collective-permute-start.18
  84.2 11.5 %collective-permute-done.9.refs_4_ = s16[2,336,256]{2,1,0:T(8,128)(2,1)S(1)} collective-permute-done((s16[2,336,256]{2,1,0:T(8,128)(2,1)S(1)}, s16[2,336,256]{2,1,0:T(8,128)(2,1)S(1)}, u32[]{:S(2)}, u32[]{:S(2)}) %collective-permute-start.9) | collective-permute-done | bytes 344096 | tf_op jit(solution)/shard_map/ppermute | solution.py:625
  96.5 1.2 collective-permute-start.10
  98.7 4.0 %collective-permute-start.27 = (s16[272,256]{1,0:T(8,128)(2,1)S(1)}, s16[272,256]{1,0:T(8,128)(2,1)S(1)}, u32[]{:S(2)}, u32[]{:S(2)}) collective-permute-start(s16[272,256]{1,0:T(8,128)(2,1)S(1)} %get-tuple-element.55), channel_id=1, source_target_pairs={{0,8},{4,12},{8,0},{12,4},{1,9},{5,13},{9,1},{13,5},{2,10},{6,14},... | collective-permute-start | bytes 417800 | tf_op jit(solution)/shard_map/ppermute | solution.py:625
  103.7 2.4 %collective-permute-done.10.refs_5_ = s16[2,336,256]{2,1,0:T(8,128)(2,1)S(1)} collective-permute-done((s16[2,336,256]{2,1,0:T(8,128)(2,1)S(1)}, s16[2,336,256]{2,1,0:T(8,128)(2,1)S(1)}, u32[]{:S(2)}, u32[]{:S(2)}) %collective-permute-start.10) | collective-permute-done | bytes 344096 | tf_op jit(solution)/shard_map/ppermute | solution.py:629
  106.9 4.6 %collective-permute-done.27.refs_1_ = s16[272,256]{1,0:T(8,128)(2,1)S(1)} collective-permute-done((s16[272,256]{1,0:T(8,128)(2,1)S(1)}, s16[272,256]{1,0:T(8,128)(2,1)S(1)}, u32[]{:S(2)}, u32[]{:S(2)}) %collective-permute-start.27) | collective-permute-done | bytes 139296 | tf_op jit(solution)/shard_map/ppermute | solution.py:625
  112.5 1.8 %collective-permute-done.28.refs_2_ = s16[272,256]{1,0:T(8,128)(2,1)S(1)} collective-permute-done((s16[272,256]{1,0:T(8,128)(2,1)S(1)}, s16[272,256]{1,0:T(8,128)(2,1)S(1)}, u32[]{:S(2)}, u32[]{:S(2)}) %collective-permute-start.28) | collective-permute-done | bytes 139296 | tf_op jit(solution)/shard_map/ppermute | solution.py:625
  114.3 1.2 collective-permute-start.12
  115.5 2.3 %shard_map.77.refs_12_ = f32[2,256,1024]{2,1,0:T(8,128)S(1)} custom-call(s32[1]{0:T(128)} %bitcast.me_ref, s32[1]{0:T(128)} %bitcast.1.refs_10_.spot_ref, s32[4]{0:T(128)S(1)} %copy-done.2, s32[8,2]{1,0:T(8,128)S(1)} %pad_add_fusion.refs_0_, s32[8,2]{1,0:T(8,128)S(1)} %collective-permute-done.6.refs_1_, s32[8,2]{1,0:T(8,128)S(1)} %collective-permute-done.7.refs_2_, ...), custom_call_target="tpu_custom_call" | custom-call | tf_op jit(solution)/shard_map/pallas_call | solution.py:727
  118.6 4.4 %shard_map.78.refs_8_ = f32[2,256,1024]{2,1,0:T(8,128)S(1)} custom-call(s32[1]{0:T(128)} %bitcast.me_ref, s32[1]{0:T(128)} %bitcast.1.refs_10_.spot_ref, s32[4]{0:T(128)S(1)} %copy-done.2, s32[8,2]{1,0:T(8,128)S(1)} %pad_add_fusion.refs_0_, s32[8,2]{1,0:T(8,128)S(1)} %collective-permute-done.6.refs_1_, s32[8,2]{1,0:T(8,128)S(1)} %collective-permute-done.7.refs_2_, ...), custom_call_target="tpu_custom_call" | custom-call | tf_op jit(solution)/shard_map/pallas_call | solution.py:727
  123.1 3.3 %shard_map.79 = f32[2,256,1024]{2,1,0:T(8,128)} custom-call(s32[1]{0:T(128)} %bitcast.me_ref, s32[1]{0:T(128)} %bitcast.1.refs_10_.spot_ref, s32[4]{0:T(128)S(1)} %copy-done.2, s32[8,2]{1,0:T(8,128)S(1)} %pad_add_fusion.refs_0_, s32[8,2]{1,0:T(8,128)S(1)} %collective-permute-done.6.refs_1_, s32[8,2]{1,0:T(8,128)S(1)} %collective-permute-done.7.refs_2_, ...), custom_call_target="tpu_custom_call" | custom-call | tf_op jit(solution)/shard_map/pallas_call | solution.py:727
  (66 shorter events, 11.7 us)
Async XLA Ops:
  0.6 4.7 %collective-permute-start = (s32[2,2]{1,0:T(2,128)}, s32[2,2]{1,0:T(2,128)S(1)}, u32[]{:S(2)}, u32[]{:S(2)}) collective-permute-start(s32[2,2]{1,0:T(2,128)} %off_ref.1), channel_id=1, source_target_pairs={{0,12},{4,0},{8,4},{12,8},{1,13},{5,1},{9,5},{13,9},{2,14},{6,2},{... | collective-permute-start | bytes 56 | tf_op jit(solution)/shard_map/ppermute | solution.py:625
  0.7 4.7 %collective-permute-start.1 = (s32[2,2]{1,0:T(2,128)}, s32[2,2]{1,0:T(2,128)S(1)}, u32[]{:S(2)}, u32[]{:S(2)}) collective-permute-start(s32[2,2]{1,0:T(2,128)} %off_ref.1), channel_id=1, source_target_pairs={{0,8},{4,12},{8,0},{12,4},{1,9},{5,13},{9,1},{13,5},{2,10},{6,14},... | collective-permute-start | bytes 56 | tf_op jit(solution)/shard_map/ppermute | solution.py:625
  3.2 3.1 %collective-permute-start.2 = (s32[2,2]{1,0:T(2,128)}, s32[2,2]{1,0:T(2,128)S(1)}, u32[]{:S(2)}, u32[]{:S(2)}) collective-permute-start(s32[2,2]{1,0:T(2,128)} %off_ref.1), channel_id=1, source_target_pairs={{0,4},{4,8},{8,12},{12,0},{1,5},{5,9},{9,13},{13,1},{2,6},{6,10},{... | collective-permute-start | bytes 56 | tf_op jit(solution)/shard_map/ppermute | solution.py:625
  16.6 12.7 %collective-permute-start.6 = (s32[8,2]{1,0:T(8,128)S(1)}, s32[8,2]{1,0:T(8,128)S(1)}, u32[]{:S(2)}, u32[]{:S(2)}) collective-permute-start(s32[8,2]{1,0:T(8,128)S(1)} %pad_add_fusion.refs_0_), channel_id=1, source_target_pairs={{0,2},{1,3},{2,0},{3,1},{4,6},{5,7},{6,4},{7,5},{8,10},{9,11},{10,... | collective-permute-start | bytes 200 | tf_op jit(solution)/shard_map/ppermute | solution.py:629
  17.8 12.0 %collective-permute-start.7 = (s32[8,2]{1,0:T(8,128)S(1)}, s32[8,2]{1,0:T(8,128)S(1)}, u32[]{:S(2)}, u32[]{:S(2)}) collective-permute-start(s32[8,2]{1,0:T(8,128)S(1)} %pad_add_fusion.refs_0_), channel_id=1, source_target_pairs={{0,1},{1,0},{2,3},{3,2},{4,5},{5,4},{6,7},{7,6},{8,9},{9,8},{10,11... | collective-permute-start | bytes 200 | tf_op jit(solution)/shard_map/ppermute | solution.py:629
  20.2 10.6 %collective-permute-start.3 = (bf16[2,320,256]{2,1,0:T(8,128)(2,1)}, bf16[2,320,256]{2,1,0:T(8,128)(2,1)S(1)}, u32[]{:S(2)}, u32[]{:S(2)}) collective-permute-start(bf16[2,320,256]{2,1,0:T(8,128)(2,1)} %get-tuple-element.33), channel_id=1, source_target_pairs={{0,4},{4,8},{8,12},{12,0},{1,5},{5,9},{9,13},{13,1},{2,6},{6,10},{... | collective-permute-start | bytes 983048 | tf_op jit(solution)/shard_map/ppermute | solution.py:625
  22.2 28.4 %collective-permute-start.4 = (bf16[2,320,256]{2,1,0:T(8,128)(2,1)}, bf16[2,320,256]{2,1,0:T(8,128)(2,1)S(1)}, u32[]{:S(2)}, u32[]{:S(2)}) collective-permute-start(bf16[2,320,256]{2,1,0:T(8,128)(2,1)} %get-tuple-element.34), channel_id=1, source_target_pairs={{0,8},{4,12},{8,0},{12,4},{1,9},{5,13},{9,1},{13,5},{2,10},{6,14},... | collective-permute-start | bytes 983048 | tf_op jit(solution)/shard_map/ppermute | solution.py:625
  24.6 28.2 %collective-permute-start.5 = (bf16[2,320,256]{2,1,0:T(8,128)(2,1)}, bf16[2,320,256]{2,1,0:T(8,128)(2,1)S(1)}, u32[]{:S(2)}, u32[]{:S(2)}) collective-permute-start(bf16[2,320,256]{2,1,0:T(8,128)(2,1)} %get-tuple-element.35), channel_id=1, source_target_pairs={{0,12},{4,0},{8,4},{12,8},{1,13},{5,1},{9,5},{13,9},{2,14},{6,2},{... | collective-permute-start | bytes 983048 | tf_op jit(solution)/shard_map/ppermute | solution.py:625
  26.4 26.4 %copy-start = (bf16[2,320,256]{2,1,0:T(8,128)(2,1)S(1)}, bf16[2,320,256]{2,1,0:T(8,128)(2,1)}, u32[]{:S(2)}) copy-start(bf16[2,320,256]{2,1,0:T(8,128)(2,1)} %pack.3.refs_0_) | copy-start | bytes 983044
  26.4 26.4 %copy-start.1 = (f32[2,2,256,256]{3,2,1,0:T(8,128)S(1)}, f32[2,2,256,256]{3,2,1,0:T(8,128)}, u32[]{:S(2)}) copy-start(f32[2,2,256,256]{3,2,1,0:T(8,128)} %refs_4_.1) | copy-start | bytes 3145732
  26.4 26.4 %copy-start.2 = (s32[4]{0:T(128)S(1)}, s32[4]{0:T(128)}, u32[]{:S(2)}) copy-start(s32[4]{0:T(128)} %owner_ref.11) | copy-start | bytes 52
  29.3 1.5 %collective-permute-start.8 = (s32[8,2]{1,0:T(8,128)S(1)}, s32[8,2]{1,0:T(8,128)S(1)}, u32[]{:S(2)}, u32[]{:S(2)}) collective-permute-start(s32[8,2]{1,0:T(8,128)S(1)} %collective-permute-done.6.refs_1_), channel_id=1, source_target_pairs={{0,1},{1,0},{2,3},{3,2},{4,5},{5,4},{6,7},{7,6},{8,9},{9,8},{10,11... | collective-permute-start | bytes 200 | tf_op jit(solution)/shard_map/ppermute | solution.py:629
  64.5 3.0 %collective-permute-start.24 = (f32[2,2,2,64,256]{4,3,2,1,0:T(8,128)S(1)}, f32[2,2,2,64,256]{4,3,2,1,0:T(8,128)S(1)}, u32[]{:S(2)}, u32[]{:S(2)}) collective-permute-start(f32[2,2,2,64,256]{4,3,2,1,0:T(8,128)S(1)} %get-tuple-element.51), channel_id=1, source_target_pairs={{0,1},{1,0},{2,3},{3,2},{4,5},{5,4},{6,7},{7,6},{8,9},{9,8},{10,11... | collective-permute-start | bytes 1572872 | tf_op jit(solution)/shard_map/ppermute | solution.py:629
  65.4 9.5 %collective-permute-start.21 = (s16[2,336,256]{2,1,0:T(8,128)(2,1)S(1)}, s16[2,336,256]{2,1,0:T(8,128)(2,1)S(1)}, u32[]{:S(2)}, u32[]{:S(2)}) collective-permute-start(s16[2,336,256]{2,1,0:T(8,128)(2,1)S(1)} %get-tuple-element.49.refs_4_), channel_id=1, source_target_pairs={{0,2},{1,3},{2,0},{3,1},{4,6},{5,7},{6,4},{7,5},{8,10},{9,11},{10,... | collective-permute-start | bytes 1032200 | tf_op jit(solution)/shard_map/ppermute | solution.py:629
  65.7 9.5 %collective-permute-start.22 = (s16[2,336,256]{2,1,0:T(8,128)(2,1)S(1)}, s16[2,336,256]{2,1,0:T(8,128)(2,1)S(1)}, u32[]{:S(2)}, u32[]{:S(2)}) collective-permute-start(s16[2,336,256]{2,1,0:T(8,128)(2,1)S(1)} %get-tuple-element.49.refs_4_), channel_id=1, source_target_pairs={{0,1},{1,0},{2,3},{3,2},{4,5},{5,4},{6,7},{7,6},{8,9},{9,8},{10,11... | collective-permute-start | bytes 1032200 | tf_op jit(solution)/shard_map/ppermute | solution.py:629
  66.1 10.4 %collective-permute-start.13 = (s16[2,336,256]{2,1,0:T(8,128)(2,1)S(1)}, s16[2,336,256]{2,1,0:T(8,128)(2,1)S(1)}, u32[]{:S(2)}, u32[]{:S(2)}) collective-permute-start(s16[2,336,256]{2,1,0:T(8,128)(2,1)S(1)} %get-tuple-element.47), channel_id=1, source_target_pairs={{0,4},{4,8},{8,12},{12,0},{1,5},{5,9},{9,13},{13,1},{2,6},{6,10},{... | collective-permute-start | bytes 1032200 | tf_op jit(solution)/shard_map/ppermute | solution.py:625
  66.1 17.0 %collective-permute-start.17 = (s16[2,336,256]{2,1,0:T(8,128)(2,1)S(1)}, s16[2,336,256]{2,1,0:T(8,128)(2,1)S(1)}, u32[]{:S(2)}, u32[]{:S(2)}) collective-permute-start(s16[2,336,256]{2,1,0:T(8,128)(2,1)S(1)} %get-tuple-element.48), channel_id=1, source_target_pairs={{0,12},{4,0},{8,4},{12,8},{1,13},{5,1},{9,5},{13,9},{2,14},{6,2},{... | collective-permute-start | bytes 1032200 | tf_op jit(solution)/shard_map/ppermute | solution.py:625
  67.5 28.2 %collective-permute-start.9 = (s16[2,336,256]{2,1,0:T(8,128)(2,1)S(1)}, s16[2,336,256]{2,1,0:T(8,128)(2,1)S(1)}, u32[]{:S(2)}, u32[]{:S(2)}) collective-permute-start(s16[2,336,256]{2,1,0:T(8,128)(2,1)S(1)} %get-tuple-element.46), channel_id=1, source_target_pairs={{0,8},{4,12},{8,0},{12,4},{1,9},{5,13},{9,1},{13,5},{2,10},{6,14},... | collective-permute-start | bytes 1032200 | tf_op jit(solution)/shard_map/ppermute | solution.py:625
  75.0 21.5 %collective-permute-start.25 = (s16[272,256]{1,0:T(8,128)(2,1)S(1)}, s16[272,256]{1,0:T(8,128)(2,1)S(1)}, u32[]{:S(2)}, u32[]{:S(2)}) collective-permute-start(s16[272,256]{1,0:T(8,128)(2,1)S(1)} %get-tuple-element.53), channel_id=1, source_target_pairs={{0,2},{1,3},{2,0},{3,1},{4,6},{5,7},{6,4},{7,5},{8,10},{9,11},{10,... | collective-permute-start | bytes 417800 | tf_op jit(solution)/shard_map/ppermute | solution.py:629
  75.2 22.6 %collective-permute-start.23 = (s16[2,336,256]{2,1,0:T(8,128)(2,1)S(1)}, s16[2,336,256]{2,1,0:T(8,128)(2,1)S(1)}, u32[]{:S(2)}, u32[]{:S(2)}) collective-permute-start(s16[2,336,256]{2,1,0:T(8,128)(2,1)S(1)} %collective-permute-done.21.refs_5_), channel_id=1, source_target_pairs={{0,1},{1,0},{2,3},{3,2},{4,5},{5,4},{6,7},{7,6},{8,9},{9,8},{10,11... | collective-permute-start | bytes 1032200 | tf_op jit(solution)/shard_map/ppermute | solution.py:629
  76.5 22.2 %collective-permute-start.14 = (s16[2,336,256]{2,1,0:T(8,128)(2,1)S(1)}, s16[2,336,256]{2,1,0:T(8,128)(2,1)S(1)}, u32[]{:S(2)}, u32[]{:S(2)}) collective-permute-start(s16[2,336,256]{2,1,0:T(8,128)(2,1)S(1)} %collective-permute-done.13.refs_4_), channel_id=1, source_target_pairs={{0,2},{1,3},{2,0},{3,1},{4,6},{5,7},{6,4},{7,5},{8,10},{9,11},{10,... | collective-permute-start | bytes 1032200 | tf_op jit(solution)/shard_map/ppermute | solution.py:629
  83.0 19.7 %collective-permute-start.18 = (s16[2,336,256]{2,1,0:T(8,128)(2,1)S(1)}, s16[2,336,256]{2,1,0:T(8,128)(2,1)S(1)}, u32[]{:S(2)}, u32[]{:S(2)}) collective-permute-start(s16[2,336,256]{2,1,0:T(8,128)(2,1)S(1)} %collective-permute-done.17.refs_8_), channel_id=1, source_target_pairs={{0,2},{1,3},{2,0},{3,1},{4,6},{5,7},{6,4},{7,5},{8,10},{9,11},{10,... | collective-permute-start | bytes 1032200 | tf_op jit(solution)/shard_map/ppermute | solution.py:629
  95.7 7.0 %collective-permute-start.15 = (s16[2,336,256]{2,1,0:T(8,128)(2,1)S(1)}, s16[2,336,256]{2,1,0:T(8,128)(2,1)S(1)}, u32[]{:S(2)}, u32[]{:S(2)}) collective-permute-start(s16[2,336,256]{2,1,0:T(8,128)(2,1)S(1)} %collective-permute-done.13.refs_4_), channel_id=1, source_target_pairs={{0,1},{1,0},{2,3},{3,2},{4,5},{5,4},{6,7},{7,6},{8,9},{9,8},{10,11... | collective-permute-start | bytes 1032200 | tf_op jit(solution)/shard_map/ppermute | solution.py:629
  96.5 9.6 %collective-permute-start.10 = (s16[2,336,256]{2,1,0:T(8,128)(2,1)S(1)}, s16[2,336,256]{2,1,0:T(8,128)(2,1)S(1)}, u32[]{:S(2)}, u32[]{:S(2)}) collective-permute-start(s16[2,336,256]{2,1,0:T(8,128)(2,1)S(1)} %collective-permute-done.9.refs_4_), channel_id=1, source_target_pairs={{0,2},{1,3},{2,0},{3,1},{4,6},{5,7},{6,4},{7,5},{8,10},{9,11},{10,... | collective-permute-start | bytes 1032200 | tf_op jit(solution)/shard_map/ppermute | solution.py:629
  97.8 9.1 %collective-permute-start.26 = (s16[272,256]{1,0:T(8,128)(2,1)S(1)}, s16[272,256]{1,0:T(8,128)(2,1)S(1)}, u32[]{:S(2)}, u32[]{:S(2)}) collective-permute-start(s16[272,256]{1,0:T(8,128)(2,1)S(1)} %get-tuple-element.55), channel_id=1, source_target_pairs={{0,4},{4,8},{8,12},{12,0},{1,5},{5,9},{9,13},{13,1},{2,6},{6,10},{... | collective-permute-start | bytes 417800 | tf_op jit(solution)/shard_map/ppermute | solution.py:625
  98.7 12.8 %collective-permute-start.27 = (s16[272,256]{1,0:T(8,128)(2,1)S(1)}, s16[272,256]{1,0:T(8,128)(2,1)S(1)}, u32[]{:S(2)}, u32[]{:S(2)}) collective-permute-start(s16[272,256]{1,0:T(8,128)(2,1)S(1)} %get-tuple-element.55), channel_id=1, source_target_pairs={{0,8},{4,12},{8,0},{12,4},{1,9},{5,13},{9,1},{13,5},{2,10},{6,14},... | collective-permute-start | bytes 417800 | tf_op jit(solution)/shard_map/ppermute | solution.py:625
  102.7 11.6 %collective-permute-start.28 = (s16[272,256]{1,0:T(8,128)(2,1)S(1)}, s16[272,256]{1,0:T(8,128)(2,1)S(1)}, u32[]{:S(2)}, u32[]{:S(2)}) collective-permute-start(s16[272,256]{1,0:T(8,128)(2,1)S(1)} %get-tuple-element.55), channel_id=1, source_target_pairs={{0,12},{4,0},{8,4},{12,8},{1,13},{5,1},{9,5},{13,9},{2,14},{6,2},{... | collective-permute-start | bytes 417800 | tf_op jit(solution)/shard_map/ppermute | solution.py:625
  102.7 15.9 %collective-permute-start.19 = (s16[2,336,256]{2,1,0:T(8,128)(2,1)S(1)}, s16[2,336,256]{2,1,0:T(8,128)(2,1)S(1)}, u32[]{:S(2)}, u32[]{:S(2)}) collective-permute-start(s16[2,336,256]{2,1,0:T(8,128)(2,1)S(1)} %collective-permute-done.17.refs_8_), channel_id=1, source_target_pairs={{0,1},{1,0},{2,3},{3,2},{4,5},{5,4},{6,7},{7,6},{8,9},{9,8},{10,11... | collective-permute-start | bytes 1032200 | tf_op jit(solution)/shard_map/ppermute | solution.py:629
  106.1 12.6 %collective-permute-start.16 = (s16[2,336,256]{2,1,0:T(8,128)(2,1)S(1)}, s16[2,336,256]{2,1,0:T(8,128)(2,1)S(1)}, u32[]{:S(2)}, u32[]{:S(2)}) collective-permute-start(s16[2,336,256]{2,1,0:T(8,128)(2,1)S(1)} %collective-permute-done.14.refs_5_), channel_id=1, source_target_pairs={{0,1},{1,0},{2,3},{3,2},{4,5},{5,4},{6,7},{7,6},{8,9},{9,8},{10,11... | collective-permute-start | bytes 1032200 | tf_op jit(solution)/shard_map/ppermute | solution.py:629
  106.9 11.7 %collective-permute-start.20 = (s16[2,336,256]{2,1,0:T(8,128)(2,1)S(1)}, s16[2,336,256]{2,1,0:T(8,128)(2,1)S(1)}, u32[]{:S(2)}, u32[]{:S(2)}) collective-permute-start(s16[2,336,256]{2,1,0:T(8,128)(2,1)S(1)} %collective-permute-done.18.refs_9_), channel_id=1, source_target_pairs={{0,1},{1,0},{2,3},{3,2},{4,5},{5,4},{6,7},{7,6},{8,9},{9,8},{10,11... | collective-permute-start | bytes 1032200 | tf_op jit(solution)/shard_map/ppermute | solution.py:629
  111.5 11.5 %collective-permute-start.11 = (s16[2,336,256]{2,1,0:T(8,128)(2,1)S(1)}, s16[2,336,256]{2,1,0:T(8,128)(2,1)S(1)}, u32[]{:S(2)}, u32[]{:S(2)}) collective-permute-start(s16[2,336,256]{2,1,0:T(8,128)(2,1)S(1)} %collective-permute-done.9.refs_4_), channel_id=1, source_target_pairs={{0,1},{1,0},{2,3},{3,2},{4,5},{5,4},{6,7},{7,6},{8,9},{9,8},{10,11... | collective-permute-start | bytes 1032200 | tf_op jit(solution)/shard_map/ppermute | solution.py:629
  114.3 8.8 %collective-permute-start.12 = (s16[2,336,256]{2,1,0:T(8,128)(2,1)S(1)}, s16[2,336,256]{2,1,0:T(8,128)(2,1)S(1)}, u32[]{:S(2)}, u32[]{:S(2)}) collective-permute-start(s16[2,336,256]{2,1,0:T(8,128)(2,1)S(1)} %collective-permute-done.10.refs_5_), channel_id=1, source_target_pairs={{0,1},{1,0},{2,3},{3,2},{4,5},{5,4},{6,7},{7,6},{8,9},{9,8},{10,11... | collective-permute-start | bytes 1032200 | tf_op jit(solution)/shard_map/ppermute | solution.py:629
  (8 other events, 17.1 us)

commit v4 on v3

--- a/solution.py
+++ b/solution.py
@@ -502,24 +502,35 @@
     pack_ref[blocks * rows : blocks * rows + 16, :] = code_rows(codes)
 
 
-def probe_close_kernel(blocks, rows, kept_ref, came_ref, total_ref, pack_ref):
-    scale = step_of(wide_of(came_ref[blocks * rows : blocks * rows + 16, :]))
-    codes = []
+def unpacked(pack_ref, scale, b, rows):
+    return wide_of(pack_ref[b * rows : (b + 1) * rows, :]) * scale[b : b + 1, :]
+
+
+def probe_scale(pack_ref, blocks, rows):
+    return step_of(wide_of(pack_ref[blocks * rows : blocks * rows + 16, :]))
+
+
+def probe_close_kernel(blocks, rows, kept_ref, came_ref, pack_ref):
+    scale = probe_scale(came_ref, blocks, rows)
+    codes = [
+        packed(kept_ref[b] + unpacked(came_ref, scale, b, rows), pack_ref, b, rows) for b in range(blocks)
+    ]
+    pack_ref[blocks * rows : blocks * rows + 16, :] = code_rows(codes)
+
+
+def probe_merge_kernel(blocks, rows, own_ref, came_ref, pack_ref):
+    own, came = probe_scale(own_ref, blocks, rows), probe_scale(came_ref, blocks, rows)
+    codes = [
+        packed(unpacked(own_ref, own, b, rows) + unpacked(came_ref, came, b, rows), pack_ref, b, rows)
+        for b in range(blocks)
+    ]
+    pack_ref[blocks * rows : blocks * rows + 16, :] = code_rows(codes)
+
+
+def probe_sum_kernel(blocks, rows, own_ref, came_ref, total_ref):
+    own, came = probe_scale(own_ref, blocks, rows), probe_scale(came_ref, blocks, rows)
     for b in range(blocks):
-        total = kept_ref[b] + wide_of(came_ref[b * rows : (b + 1) * rows, :]) * scale[b : b + 1, :]
-        total_ref[b] = total
-        codes.append(packed(total, pack_ref, b, rows))
-    pack_ref[blocks * rows : blocks * rows + 16, :] = code_rows(codes)
-
-
-def probe_sum_kernel(blocks, rows, own_ref, *refs):
-    packs, total_ref = refs[:-1], refs[-1]
-    scales = [step_of(wide_of(pack[blocks * rows : blocks * rows + 16, :])) for pack in packs]
-    for b in range(blocks):
-        total = own_ref[b]
-        for pack, scale in zip(packs, scales):
-            total = total + wide_of(pack[b * rows : (b + 1) * rows, :]) * scale[b : b + 1, :]
-        total_ref[b] = total
+        total_ref[b] = unpacked(own_ref, own, b, rows) + unpacked(came_ref, came, b, rows)
 
 
 def place_kernel(tiles, spots, steps_back, first, win, slab, me_ref, spot_ref, owner_ref, *refs):
@@ -654,7 +665,7 @@
         return pl.pallas_call(
             functools.partial(pack_kernel, tiles, asked, win, width),
             out_shape=[jax.ShapeDtypeStruct(pack_shape, jnp.bfloat16)] * asked,
-            in_specs=[smem] * (2 + asked) + [anywhere],
+            in_specs=[smem] * (2 + asked) + [pl.BlockSpec(memory_space=pltpu.HBM)],
             out_specs=[anywhere] * asked,
             scratch_shapes=[
                 pltpu.VMEM((asked, 2, win, 2 * win), jnp.bfloat16),
@@ -663,13 +674,16 @@
                 pltpu.SemaphoreType.DMA((asked,)),
                 pltpu.SemaphoreType.DMA((asked,)),
             ],
-            compiler_params=grant(60),
+            compiler_params=grant(8),
             name="pack",
-        )(me, strip_owner, *asking, field)
-
-    packs = pack_for(offs[1:], object_field)
-    packs, chirp, own_off = lax.optimization_barrier((packs, chirp, offsets))
-    packs = pack_for([own_off], object_field) + packs
+        )(me, strip_owner, *asking, pltpu.with_memory_space_constraint(field, pltpu.HBM))
+
+    near_first = near_to_far(tiles)
+    packs = [None] * tiles
+    for k in near_first:
+        packs[k] = pack_for(offs[k : k + 1], object_field)[0]
+    own_off, chirp, _ = lax.optimization_barrier((offsets, chirp, packs[near_first[-1]]))
+    packs[0] = pack_for([own_off], object_field)[0]
     column_offs = [jnp.concatenate([own_off] + [offs[tiles - k] for k in range(1, tiles)], axis=0)]
     bit = pos_groups // 2
     while bit:
@@ -693,29 +707,26 @@
 
     blocks = modes * 2
 
-    def probe_step(kernel, *parts):
+    whole = jax.ShapeDtypeStruct((blocks, share, win), jnp.float32)
+    coded = jax.ShapeDtypeStruct((blocks * share + 16, win), jnp.int16)
+
+    def probe_step(kernel, out_shape, *parts):
         return pl.pallas_call(
-            functools.partial(kernel, blocks, share),
-            out_shape=[
-                jax.ShapeDtypeStruct((blocks, share, win), jnp.float32),
-                jax.ShapeDtypeStruct((blocks * share + 16, win), jnp.int16),
-            ],
-            compiler_params=grant(8),
+            functools.partial(kernel, blocks, share), out_shape=out_shape, compiler_params=grant(8)
         )(*parts)
 
     pair = (2, blocks, share, win)
     came = swapped(away, "pos", pos_groups, 1).reshape(pair)
-    probe_own, probe_pack = probe_step(probe_cross_kernel, kept.reshape(pair), came)
+    probe_own, probe_pack = probe_step(probe_cross_kernel, [whole, coded], kept.reshape(pair), came)
     came = swapped(probe_pack, "pos", pos_groups, 2)
-    probe_own, probe_pack = probe_step(probe_close_kernel, probe_own, came)
-    probe_packs = [shifted(probe_pack, "tile", tiles, k) for k in range(1, tiles)]
-
-    probe_out = pl.pallas_call(
-        functools.partial(probe_sum_kernel, blocks, share),
-        out_shape=jax.ShapeDtypeStruct((blocks, share, win), jnp.float32),
-        compiler_params=grant(4),
-        name="probe_sum",
-    )(probe_own, *probe_packs)
+    probe_pack = probe_step(probe_close_kernel, coded, probe_own, came)
+    bit = 1
+    while 2 * bit < tiles:
+        came = swapped(probe_pack, "tile", tiles, bit)
+        probe_pack = probe_step(probe_merge_kernel, coded, probe_pack, came)
+        bit *= 2
+    came = swapped(probe_pack, "tile", tiles, bit)
+    probe_out = probe_step(probe_sum_kernel, whole, probe_pack, came)
 
     spots = len(columns)
     placed = None
@@ -742,6 +753,7 @@
 
 
 def per_device(object_field, probe, amplitude, offsets, strip_owner, chirp):
+    tiles = lax.axis_size("tile")
     pos_groups = lax.axis_size("pos")
     pos_count, win, _ = amplitude.shape
     width = object_field.shape[2]
@@ -752,6 +764,8 @@
         and width // pos_groups >= 2 * win
         and (width // pos_groups) % 128 == 0
         and pos_groups == 4
+        and tiles & (tiles - 1) == 0
+        and tiles >= 4
         and (win // pos_groups) % 16 == 0
     )
     if not packed:

time: 127 us -> 121 us (0.953)
  the two profiles are of different devices: /device:TPU:9 before, /device:TPU:20 now
where the time goes in v4:
time: 121 us; the launch traced here: 120 us
  waiting for transfers between devices  60.5 us (50%)
  Pallas kernels  30.2 us (25%)
  starting transfers between devices  19.9 us (16%)
  matrix products  6.6 us (5%)
    ppermute x9, waiting for transfers between devices, shifted(): return lax.ppermute(x, axis, [(i, (i + k) % count) for i in range(count)])  35.8 us
    ppermute x19, waiting for transfers between devices, swapped(): return lax.ppermute(x, axis, [(i, i ^ bit) for i in range(count)])  24.8 us
    pallas_call x1, Pallas kernels, per_device_packed(): propagate_call(tiles, pos_groups, win, modes, grad_scale)  11.9 us
    ppermute x19, starting transfers between devices, swapped(): return lax.ppermute(x, axis, [(i, i ^ bit) for i in range(count)])  10.9 us
    pallas_call x3, Pallas kernels, per_device_packed(): pl.pallas_call(functools.partial(place_kernel, tiles, spots, steps_back,...  9.29 us
    ppermute x9, starting transfers between devices, shifted(): return lax.ppermute(x, axis, [(i, (i + k) % count) for i in range(count)])  8.94 us
    pallas_call x4, Pallas kernels, pack_for(): pl.pallas_call(functools.partial(pack_kernel, tiles, asked, win, width),...  7.87 us
  transfers between devices with their start and end apart: 28, of which 12 were waited for; matrix products, arithmetic and copies ran while one was open for 7% of the time, Pallas kernels for 13%

profile of v4, /device:TPU:20, one launch (start us, length us, event | category | flops | bytes accessed | tf_op | source)
XLA Modules:
  0.0 120.2 jit_solution(5612732496665810286)
XLA Ops:
  1.0 2.7 %collective-permute-start.1 = (s32[2,2]{1,0:T(2,128)}, s32[2,2]{1,0:T(2,128)S(1)}, u32[]{:S(2)}, u32[]{:S(2)}) collective-permute-start(s32[2,2]{1,0:T(2,128)} %off_ref.1), channel_id=1, source_target_pairs={{0,12},{4,0},{8,4},{12,8},{1,13},{5,1},{9,5},{13,9},{2,14},{6,2},{... | collective-permute-start | bytes 56 | tf_op jit(solution)/shard_map/ppermute | solution.py:636
  3.7 1.6 %collective-permute-done.refs_0_ = s32[2,2]{1,0:T(2,128)S(1)} collective-permute-done((s32[2,2]{1,0:T(2,128)}, s32[2,2]{1,0:T(2,128)S(1)}, u32[]{:S(2)}, u32[]{:S(2)}) %collective-permute-start) | collective-permute-done | bytes 48 | tf_op jit(solution)/shard_map/ppermute | solution.py:636
  6.0 2.0 %pack.4 = bf16[2,320,256]{2,1,0:T(8,128)(2,1)S(1)} custom-call(s32[1]{0:T(128)} %bitcast.me_ref, s32[4]{0:T(128)S(1)} %copy-done.1, s32[2,2]{1,0:T(2,128)S(1)} %collective-permute-done.refs_0_, bf16[2,256,4096]{2,1,0:T(8,128)(2,1)} %refs_1_.7), custom_call_target="tpu_custom_call" | custom-call | tf_op jit(solution)/shard_map/pack/pallas_call | solution.py:665
  8.0 2.0 %pack.5.refs_0_ = bf16[2,320,256]{2,1,0:T(8,128)(2,1)S(1)} custom-call(s32[1]{0:T(128)} %bitcast.me_ref, s32[4]{0:T(128)S(1)} %copy-done.1, s32[2,2]{1,0:T(2,128)S(1)} %copy-done.3, bf16[2,256,4096]{2,1,0:T(8,128)(2,1)} %refs_1_.7), custom_call_target="tpu_custom_call" | custom-call | tf_op jit(solution)/shard_map/pack/pallas_call | solution.py:665
  10.0 1.6 %collective-permute-start.6 = (s32[8,2]{1,0:T(8,128)S(1)}, s32[8,2]{1,0:T(8,128)S(1)}, u32[]{:S(2)}, u32[]{:S(2)}) collective-permute-start(s32[8,2]{1,0:T(8,128)S(1)} %pad_add_fusion.refs_0_), channel_id=1, source_target_pairs={{0,2},{1,3},{2,0},{3,1},{4,6},{5,7},{6,4},{7,5},{8,10},{9,11},{10,... | collective-permute-start | bytes 200 | tf_op jit(solution)/shard_map/ppermute | solution.py:640
  12.2 1.7 %fusion.10 = f32[256,256]{0,1:T(8,128)S(1)} fusion(f32[256]{0:T(256)S(1)} %get-tuple-element.41, f32[256]{0:T(256)S(1)} %get-tuple-element.40), kind=kOutput, calls=%fused_computation.18 | convolution fusion | flops 203489280 | bytes 264192 | tf_op jit(solution)/shard_map/dot_general | solution.py:31
  13.8 1.7 %fusion.8 = f32[256,256]{0,1:T(8,128)S(1)} fusion(f32[256]{0:T(256)S(1)} %get-tuple-element.41, f32[256]{0:T(256)S(1)} %get-tuple-element.40), kind=kOutput, calls=%fused_computation.16 | convolution fusion | flops 203489280 | bytes 264192 | tf_op jit(solution)/shard_map/dot_general | solution.py:34
  15.5 2.0 %pack.6 = bf16[2,320,256]{2,1,0:T(8,128)(2,1)S(1)} custom-call(s32[1]{0:T(128)} %bitcast.me_ref, s32[4]{0:T(128)S(1)} %copy-done.2, s32[2,2]{1,0:T(2,128)S(1)} %collective-permute-done.1.refs_0_, bf16[2,256,4096]{2,1,0:T(8,128)(2,1)} %refs_1_.7), custom_call_target="tpu_custom_call" | custom-call | tf_op jit(solution)/shard_map/pack/pallas_call | solution.py:665
  17.5 1.4 %collective-permute-start.2 = (bf16[2,320,256]{2,1,0:T(8,128)(2,1)S(1)}, bf16[2,320,256]{2,1,0:T(8,128)(2,1)}, u32[]{:S(2)}, u32[]{:S(2)}) collective-permute-start(bf16[2,320,256]{2,1,0:T(8,128)(2,1)S(1)} %pack.6), channel_id=1, source_target_pairs={{0,4},{4,8},{8,12},{12,0},{1,5},{5,9},{9,13},{13,1},{2,6},{6,10},{... | collective-permute-start | bytes 983048 | tf_op jit(solution)/shard_map/ppermute | solution.py:636
  18.9 2.0 %pack.7 = bf16[2,320,256]{2,1,0:T(8,128)(2,1)S(1)} custom-call(s32[1]{0:T(128)} %bitcast.me_ref, s32[4]{0:T(128)S(1)} %copy-done.2, s32[2,2]{1,0:T(2,128)S(1)} %collective-permute-done.4.refs_0_, bf16[2,256,4096]{2,1,0:T(8,128)(2,1)} %refs_1_.7), custom_call_target="tpu_custom_call" | custom-call | tf_op jit(solution)/shard_map/pack/pallas_call | solution.py:665
  20.9 1.4 %collective-permute-start.5 = (bf16[2,320,256]{2,1,0:T(8,128)(2,1)S(1)}, bf16[2,320,256]{2,1,0:T(8,128)(2,1)}, u32[]{:S(2)}, u32[]{:S(2)}) collective-permute-start(bf16[2,320,256]{2,1,0:T(8,128)(2,1)S(1)} %pack.7), channel_id=1, source_target_pairs={{0,12},{4,0},{8,4},{12,8},{1,13},{5,1},{9,5},{13,9},{2,14},{6,2},{... | collective-permute-start | bytes 983048 | tf_op jit(solution)/shard_map/ppermute | solution.py:636
  22.3 1.6 %convolution_add_fusion = f32[256,256]{0,1:T(8,128)S(1)} fusion(f32[256,256]{0,1:T(8,128)S(1)} %fusion.10, f32[256]{0:T(256)S(1)} %get-tuple-element.41, f32[256]{0:T(256)S(1)} %get-tuple-element.40), kind=kOutput, calls=%fused_computation.1 | convolution fusion | flops 203620352 | bytes 526336 | tf_op jit(solution)/shard_map/dot_general | solution.py:31
  24.1 1.7 %convolution_subtract_fusion = f32[256,256]{0,1:T(8,128)S(1)} fusion(f32[256,256]{0,1:T(8,128)S(1)} %fusion.8, f32[256]{0:T(256)S(1)} %get-tuple-element.41, f32[256]{0:T(256)S(1)} %get-tuple-element.40), kind=kOutput, calls=%fused_computation | convolution fusion | flops 203620352 | bytes 526336 | tf_op jit(solution)/shard_map/dot_general | solution.py:34
  25.9 1.0 convert_element_type.20.refs_5_
  27.0 1.1 collective-permute-done.8.refs_3_
  28.1 6.2 %collective-permute-done.3.refs_2_ = bf16[2,320,256]{2,1,0:T(8,128)(2,1)} collective-permute-done((bf16[2,320,256]{2,1,0:T(8,128)(2,1)S(1)}, bf16[2,320,256]{2,1,0:T(8,128)(2,1)}, u32[]{:S(2)}, u32[]{:S(2)}) %collective-permute-start.3) | collective-permute-done | bytes 327712 | tf_op jit(solution)/shard_map/ppermute | solution.py:636
  34.3 9.5 %collective-permute-done.2.refs_1_ = bf16[2,320,256]{2,1,0:T(8,128)(2,1)} collective-permute-done((bf16[2,320,256]{2,1,0:T(8,128)(2,1)S(1)}, bf16[2,320,256]{2,1,0:T(8,128)(2,1)}, u32[]{:S(2)}, u32[]{:S(2)}) %collective-permute-start.2) | collective-permute-done | bytes 327712 | tf_op jit(solution)/shard_map/ppermute | solution.py:636
  43.9 11.9 %propagate.1 = (s16[2,336,256]{2,1,0:T(8,128)(2,1)S(1)}, s16[2,336,256]{2,1,0:T(8,128)(2,1)S(1)}, s16[2,336,256]{2,1,0:T(8,128)(2,1)S(1)}, s16[2,336,256]{2,1,0:...) custom-call(s32[1]{0:T(128)} %bitcast.me_ref, s32[4]{0:T(128)S(1)} %copy-done.2, ...), custom_call_target="tpu_custom_call" | custom-call | tf_op jit(solution)/shard_map/propagate/pallas_call | solution.py:696
  55.9 1.8 %collective-permute-done.24 = f32[2,2,2,64,256]{4,3,2,1,0:T(8,128)S(1)} collective-permute-done((f32[2,2,2,64,256]{4,3,2,1,0:T(8,128)S(1)}, f32[2,2,2,64,256]{4,3,2,1,0:T(8,128)S(1)}, u32[]{:S(2)}, u32[]{:S(2)}) %collective-permute-start.24) | collective-permute-done | bytes 524320 | tf_op jit(solution)/shard_map/ppermute | solution.py:640
  58.4 1.5 %collective-permute-start.21 = (s16[2,336,256]{2,1,0:T(8,128)(2,1)S(1)}, s16[2,336,256]{2,1,0:T(8,128)(2,1)S(1)}, u32[]{:S(2)}, u32[]{:S(2)}) collective-permute-start(s16[2,336,256]{2,1,0:T(8,128)(2,1)S(1)} %get-tuple-element.35.refs_4_), channel_id=1, source_target_pairs={{0,2},{1,3},{2,0},{3,1},{4,6},{5,7},{6,4},{7,5},{8,10},{9,11},{10,... | collective-permute-start | bytes 1032200 | tf_op jit(solution)/shard_map/ppermute | solution.py:640
  59.9 2.0 %collective-permute-start.17 = (s16[2,336,256]{2,1,0:T(8,128)(2,1)S(1)}, s16[2,336,256]{2,1,0:T(8,128)(2,1)S(1)}, u32[]{:S(2)}, u32[]{:S(2)}) collective-permute-start(s16[2,336,256]{2,1,0:T(8,128)(2,1)S(1)} %get-tuple-element.34), channel_id=1, source_target_pairs={{0,12},{4,0},{8,4},{12,8},{1,13},{5,1},{9,5},{13,9},{2,14},{6,2},{... | collective-permute-start | bytes 1032200 | tf_op jit(solution)/shard_map/ppermute | solution.py:636
  62.0 2.5 %collective-permute-done.25.came_ref = s16[272,256]{1,0:T(8,128)(2,1)S(1)} collective-permute-done((s16[272,256]{1,0:T(8,128)(2,1)S(1)}, s16[272,256]{1,0:T(8,128)(2,1)S(1)}, u32[]{:S(2)}, u32[]{:S(2)}) %collective-permute-start.25) | collective-permute-done | bytes 139296 | tf_op jit(solution)/shard_map/ppermute | solution.py:640
  65.0 5.9 %collective-permute-done.21.refs_5_ = s16[2,336,256]{2,1,0:T(8,128)(2,1)S(1)} collective-permute-done((s16[2,336,256]{2,1,0:T(8,128)(2,1)S(1)}, s16[2,336,256]{2,1,0:T(8,128)(2,1)S(1)}, u32[]{:S(2)}, u32[]{:S(2)}) %collective-permute-start.21) | collective-permute-done | bytes 344096 | tf_op jit(solution)/shard_map/ppermute | solution.py:640
  71.0 14.6 %collective-permute-done.13.refs_4_ = s16[2,336,256]{2,1,0:T(8,128)(2,1)S(1)} collective-permute-done((s16[2,336,256]{2,1,0:T(8,128)(2,1)S(1)}, s16[2,336,256]{2,1,0:T(8,128)(2,1)S(1)}, u32[]{:S(2)}, u32[]{:S(2)}) %collective-permute-start.13) | collective-permute-done | bytes 344096 | tf_op jit(solution)/shard_map/ppermute | solution.py:636
  86.1 1.5 %collective-permute-start.18 = (s16[2,336,256]{2,1,0:T(8,128)(2,1)S(1)}, s16[2,336,256]{2,1,0:T(8,128)(2,1)S(1)}, u32[]{:S(2)}, u32[]{:S(2)}) collective-permute-start(s16[2,336,256]{2,1,0:T(8,128)(2,1)S(1)} %collective-permute-done.17.refs_8_), channel_id=1, source_target_pairs={{0,2},{1,3},{2,0},{3,1},{4,6},{5,7},{6,4},{7,5},{8,10},{9,11},{10,... | collective-permute-start | bytes 1032200 | tf_op jit(solution)/shard_map/ppermute | solution.py:640
  87.6 3.8 %collective-permute-done.9.refs_4_ = s16[2,336,256]{2,1,0:T(8,128)(2,1)S(1)} collective-permute-done((s16[2,336,256]{2,1,0:T(8,128)(2,1)S(1)}, s16[2,336,256]{2,1,0:T(8,128)(2,1)S(1)}, u32[]{:S(2)}, u32[]{:S(2)}) %collective-permute-start.9) | collective-permute-done | bytes 344096 | tf_op jit(solution)/shard_map/ppermute | solution.py:636
  92.2 3.4 %collective-permute-start.27 = (s16[272,256]{1,0:T(8,128)(2,1)S(1)}, s16[272,256]{1,0:T(8,128)(2,1)S(1)}, u32[]{:S(2)}, u32[]{:S(2)}) collective-permute-start(s16[272,256]{1,0:T(8,128)(2,1)S(1)} %shard_map.82.own_ref), channel_id=1, source_target_pairs={{0,8},{4,12},{8,0},{12,4},{1,9},{5,13},{9,1},{13,5},{2,10},{6,14},... | collective-permute-start | bytes 417800 | tf_op jit(solution)/shard_map/ppermute | solution.py:640
  96.5 7.4 %collective-permute-done.18.refs_9_ = s16[2,336,256]{2,1,0:T(8,128)(2,1)S(1)} collective-permute-done((s16[2,336,256]{2,1,0:T(8,128)(2,1)S(1)}, s16[2,336,256]{2,1,0:T(8,128)(2,1)S(1)}, u32[]{:S(2)}, u32[]{:S(2)}) %collective-permute-start.18) | collective-permute-done | bytes 344096 | tf_op jit(solution)/shard_map/ppermute | solution.py:640
  104.4 5.0 %collective-permute-done.10.refs_5_ = s16[2,336,256]{2,1,0:T(8,128)(2,1)S(1)} collective-permute-done((s16[2,336,256]{2,1,0:T(8,128)(2,1)S(1)}, s16[2,336,256]{2,1,0:T(8,128)(2,1)S(1)}, u32[]{:S(2)}, u32[]{:S(2)}) %collective-permute-start.10) | collective-permute-done | bytes 344096 | tf_op jit(solution)/shard_map/ppermute | solution.py:640
  110.0 2.3 %shard_map.77.refs_12_ = f32[2,256,1024]{2,1,0:T(8,128)S(1)} custom-call(s32[1]{0:T(128)} %bitcast.me_ref, s32[1]{0:T(128)} %bitcast.1.refs_10_.spot_ref, s32[4]{0:T(128)S(1)} %copy-done.2, s32[8,2]{1,0:T(8,128)S(1)} %pad_add_fusion.refs_0_, s32[8,2]{1,0:T(8,128)S(1)} %collective-permute-done.6.refs_1_, s32[8,2]{1,0:T(8,128)S(1)} %collective-permute-done.7.refs_2_, ...), custom_call_target="tpu_custom_call" | custom-call | tf_op jit(solution)/shard_map/pallas_call | solution.py:738
  113.1 4.1 %shard_map.78.refs_8_ = f32[2,256,1024]{2,1,0:T(8,128)S(1)} custom-call(s32[1]{0:T(128)} %bitcast.me_ref, s32[1]{0:T(128)} %bitcast.1.refs_10_.spot_ref, s32[4]{0:T(128)S(1)} %copy-done.2, s32[8,2]{1,0:T(8,128)S(1)} %pad_add_fusion.refs_0_, s32[8,2]{1,0:T(8,128)S(1)} %collective-permute-done.6.refs_1_, s32[8,2]{1,0:T(8,128)S(1)} %collective-permute-done.7.refs_2_, ...), custom_call_target="tpu_custom_call" | custom-call | tf_op jit(solution)/shard_map/pallas_call | solution.py:738
  117.2 2.9 %shard_map.79 = f32[2,256,1024]{2,1,0:T(8,128)} custom-call(s32[1]{0:T(128)} %bitcast.me_ref, s32[1]{0:T(128)} %bitcast.1.refs_10_.spot_ref, s32[4]{0:T(128)S(1)} %copy-done.2, s32[8,2]{1,0:T(8,128)S(1)} %pad_add_fusion.refs_0_, s32[8,2]{1,0:T(8,128)S(1)} %collective-permute-done.6.refs_1_, s32[8,2]{1,0:T(8,128)S(1)} %collective-permute-done.7.refs_2_, ...), custom_call_target="tpu_custom_call" | custom-call | tf_op jit(solution)/shard_map/pallas_call | solution.py:738
  (55 shorter events, 7.5 us)
Async XLA Ops:
  0.6 4.7 %collective-permute-start = (s32[2,2]{1,0:T(2,128)}, s32[2,2]{1,0:T(2,128)S(1)}, u32[]{:S(2)}, u32[]{:S(2)}) collective-permute-start(s32[2,2]{1,0:T(2,128)} %off_ref.1), channel_id=1, source_target_pairs={{0,8},{4,12},{8,0},{12,4},{1,9},{5,13},{9,1},{13,5},{2,10},{6,14},... | collective-permute-start | bytes 56 | tf_op jit(solution)/shard_map/ppermute | solution.py:636
  1.0 9.0 %collective-permute-start.1 = (s32[2,2]{1,0:T(2,128)}, s32[2,2]{1,0:T(2,128)S(1)}, u32[]{:S(2)}, u32[]{:S(2)}) collective-permute-start(s32[2,2]{1,0:T(2,128)} %off_ref.1), channel_id=1, source_target_pairs={{0,12},{4,0},{8,4},{12,8},{1,13},{5,1},{9,5},{13,9},{2,14},{6,2},{... | collective-permute-start | bytes 56 | tf_op jit(solution)/shard_map/ppermute | solution.py:636
  3.7 6.3 %collective-permute-start.4 = (s32[2,2]{1,0:T(2,128)}, s32[2,2]{1,0:T(2,128)S(1)}, u32[]{:S(2)}, u32[]{:S(2)}) collective-permute-start(s32[2,2]{1,0:T(2,128)} %off_ref.1), channel_id=1, source_target_pairs={{0,4},{4,8},{8,12},{12,0},{1,5},{5,9},{9,13},{13,1},{2,6},{6,10},{... | collective-permute-start | bytes 56 | tf_op jit(solution)/shard_map/ppermute | solution.py:636
  6.0 2.0 %copy-start.3 = (s32[2,2]{1,0:T(2,128)S(1)}, s32[2,2]{1,0:T(2,128)}, u32[]{:S(2)}) copy-start(s32[2,2]{1,0:T(2,128)} %off_ref.1) | copy-start | bytes 52
  8.0 4.1 %copy-start.4 = (f32[256]{0:T(256)S(1)}, f32[256]{0:T(256)}, u32[]{:S(2)}) copy-start(f32[256]{0:T(256)} %param.11) | copy-start | bytes 3076
  10.0 16.8 %collective-permute-start.6 = (s32[8,2]{1,0:T(8,128)S(1)}, s32[8,2]{1,0:T(8,128)S(1)}, u32[]{:S(2)}, u32[]{:S(2)}) collective-permute-start(s32[8,2]{1,0:T(8,128)S(1)} %pad_add_fusion.refs_0_), channel_id=1, source_target_pairs={{0,2},{1,3},{2,0},{3,1},{4,6},{5,7},{6,4},{7,5},{8,10},{9,11},{10,... | collective-permute-start | bytes 200 | tf_op jit(solution)/shard_map/ppermute | solution.py:640
  11.6 15.4 %collective-permute-start.7 = (s32[8,2]{1,0:T(8,128)S(1)}, s32[8,2]{1,0:T(8,128)S(1)}, u32[]{:S(2)}, u32[]{:S(2)}) collective-permute-start(s32[8,2]{1,0:T(8,128)S(1)} %pad_add_fusion.refs_0_), channel_id=1, source_target_pairs={{0,1},{1,0},{2,3},{3,2},{4,5},{5,4},{6,7},{7,6},{8,9},{9,8},{10,11... | collective-permute-start | bytes 200 | tf_op jit(solution)/shard_map/ppermute | solution.py:640
  11.6 22.7 %collective-permute-start.3 = (bf16[2,320,256]{2,1,0:T(8,128)(2,1)S(1)}, bf16[2,320,256]{2,1,0:T(8,128)(2,1)}, u32[]{:S(2)}, u32[]{:S(2)}) collective-permute-start(bf16[2,320,256]{2,1,0:T(8,128)(2,1)S(1)} %pack.4), channel_id=1, source_target_pairs={{0,8},{4,12},{8,0},{12,4},{1,9},{5,13},{9,1},{13,5},{2,10},{6,14},... | collective-permute-start | bytes 983048 | tf_op jit(solution)/shard_map/ppermute | solution.py:636
  12.2 3.3 %copy-start.2 = (s32[4]{0:T(128)S(1)}, s32[4]{0:T(128)}, u32[]{:S(2)}) copy-start(s32[4]{0:T(128)} %owner_ref.15) | copy-start | bytes 52
  17.5 26.4 %collective-permute-start.2 = (bf16[2,320,256]{2,1,0:T(8,128)(2,1)S(1)}, bf16[2,320,256]{2,1,0:T(8,128)(2,1)}, u32[]{:S(2)}, u32[]{:S(2)}) collective-permute-start(bf16[2,320,256]{2,1,0:T(8,128)(2,1)S(1)} %pack.6), channel_id=1, source_target_pairs={{0,4},{4,8},{8,12},{12,0},{1,5},{5,9},{9,13},{13,1},{2,6},{6,10},{... | collective-permute-start | bytes 983048 | tf_op jit(solution)/shard_map/ppermute | solution.py:636
  20.9 22.9 %collective-permute-start.5 = (bf16[2,320,256]{2,1,0:T(8,128)(2,1)S(1)}, bf16[2,320,256]{2,1,0:T(8,128)(2,1)}, u32[]{:S(2)}, u32[]{:S(2)}) collective-permute-start(bf16[2,320,256]{2,1,0:T(8,128)(2,1)S(1)} %pack.7), channel_id=1, source_target_pairs={{0,12},{4,0},{8,4},{12,8},{1,13},{5,1},{9,5},{13,9},{2,14},{6,2},{... | collective-permute-start | bytes 983048 | tf_op jit(solution)/shard_map/ppermute | solution.py:636
  24.1 19.8 %copy-start = (f32[2,2,256,256]{3,2,1,0:T(8,128)S(1)}, f32[2,2,256,256]{3,2,1,0:T(8,128)}, u32[]{:S(2)}) copy-start(f32[2,2,256,256]{3,2,1,0:T(8,128)} %refs_4_.1) | copy-start | bytes 3145732
  26.9 1.2 %collective-permute-start.8 = (s32[8,2]{1,0:T(8,128)S(1)}, s32[8,2]{1,0:T(8,128)S(1)}, u32[]{:S(2)}, u32[]{:S(2)}) collective-permute-start(s32[8,2]{1,0:T(8,128)S(1)} %collective-permute-done.6.refs_1_), channel_id=1, source_target_pairs={{0,1},{1,0},{2,3},{3,2},{4,5},{5,4},{6,7},{7,6},{8,9},{9,8},{10,11... | collective-permute-start | bytes 200 | tf_op jit(solution)/shard_map/ppermute | solution.py:640
  55.7 2.0 %collective-permute-start.24 = (f32[2,2,2,64,256]{4,3,2,1,0:T(8,128)S(1)}, f32[2,2,2,64,256]{4,3,2,1,0:T(8,128)S(1)}, u32[]{:S(2)}, u32[]{:S(2)}) collective-permute-start(f32[2,2,2,64,256]{4,3,2,1,0:T(8,128)S(1)} %get-tuple-element.37), channel_id=1, source_target_pairs={{0,1},{1,0},{2,3},{3,2},{4,5},{5,4},{6,7},{7,6},{8,9},{9,8},{10,11... | collective-permute-start | bytes 1572872 | tf_op jit(solution)/shard_map/ppermute | solution.py:640
  57.8 6.6 %collective-permute-start.25 = (s16[272,256]{1,0:T(8,128)(2,1)S(1)}, s16[272,256]{1,0:T(8,128)(2,1)S(1)}, u32[]{:S(2)}, u32[]{:S(2)}) collective-permute-start(s16[272,256]{1,0:T(8,128)(2,1)S(1)} %get-tuple-element.39), channel_id=1, source_target_pairs={{0,2},{1,3},{2,0},{3,1},{4,6},{5,7},{6,4},{7,5},{8,10},{9,11},{10,... | collective-permute-start | bytes 417800 | tf_op jit(solution)/shard_map/ppermute | solution.py:640
  58.4 12.5 %collective-permute-start.21 = (s16[2,336,256]{2,1,0:T(8,128)(2,1)S(1)}, s16[2,336,256]{2,1,0:T(8,128)(2,1)S(1)}, u32[]{:S(2)}, u32[]{:S(2)}) collective-permute-start(s16[2,336,256]{2,1,0:T(8,128)(2,1)S(1)} %get-tuple-element.35.refs_4_), channel_id=1, source_target_pairs={{0,2},{1,3},{2,0},{3,1},{4,6},{5,7},{6,4},{7,5},{8,10},{9,11},{10,... | collective-permute-start | bytes 1032200 | tf_op jit(solution)/shard_map/ppermute | solution.py:640
  59.9 11.1 %collective-permute-start.22 = (s16[2,336,256]{2,1,0:T(8,128)(2,1)S(1)}, s16[2,336,256]{2,1,0:T(8,128)(2,1)S(1)}, u32[]{:S(2)}, u32[]{:S(2)}) collective-permute-start(s16[2,336,256]{2,1,0:T(8,128)(2,1)S(1)} %get-tuple-element.35.refs_4_), channel_id=1, source_target_pairs={{0,1},{1,0},{2,3},{3,2},{4,5},{5,4},{6,7},{7,6},{8,9},{9,8},{10,11... | collective-permute-start | bytes 1032200 | tf_op jit(solution)/shard_map/ppermute | solution.py:640
  59.9 25.7 %collective-permute-start.13 = (s16[2,336,256]{2,1,0:T(8,128)(2,1)S(1)}, s16[2,336,256]{2,1,0:T(8,128)(2,1)S(1)}, u32[]{:S(2)}, u32[]{:S(2)}) collective-permute-start(s16[2,336,256]{2,1,0:T(8,128)(2,1)S(1)} %get-tuple-element.33), channel_id=1, source_target_pairs={{0,4},{4,8},{8,12},{12,0},{1,5},{5,9},{9,13},{13,1},{2,6},{6,10},{... | collective-permute-start | bytes 1032200 | tf_op jit(solution)/shard_map/ppermute | solution.py:636
  59.9 26.2 %collective-permute-start.17 = (s16[2,336,256]{2,1,0:T(8,128)(2,1)S(1)}, s16[2,336,256]{2,1,0:T(8,128)(2,1)S(1)}, u32[]{:S(2)}, u32[]{:S(2)}) collective-permute-start(s16[2,336,256]{2,1,0:T(8,128)(2,1)S(1)} %get-tuple-element.34), channel_id=1, source_target_pairs={{0,12},{4,0},{8,4},{12,8},{1,13},{5,1},{9,5},{13,9},{2,14},{6,2},{... | collective-permute-start | bytes 1032200 | tf_op jit(solution)/shard_map/ppermute | solution.py:636
  64.4 27.0 %collective-permute-start.9 = (s16[2,336,256]{2,1,0:T(8,128)(2,1)S(1)}, s16[2,336,256]{2,1,0:T(8,128)(2,1)S(1)}, u32[]{:S(2)}, u32[]{:S(2)}) collective-permute-start(s16[2,336,256]{2,1,0:T(8,128)(2,1)S(1)} %get-tuple-element.32), channel_id=1, source_target_pairs={{0,8},{4,12},{8,0},{12,4},{1,9},{5,13},{9,1},{13,5},{2,10},{6,14},... | collective-permute-start | bytes 1032200 | tf_op jit(solution)/shard_map/ppermute | solution.py:636
  71.0 20.5 %collective-permute-start.26 = (s16[272,256]{1,0:T(8,128)(2,1)S(1)}, s16[272,256]{1,0:T(8,128)(2,1)S(1)}, u32[]{:S(2)}, u32[]{:S(2)}) collective-permute-start(s16[272,256]{1,0:T(8,128)(2,1)S(1)} %shard_map.81.own_ref), channel_id=1, source_target_pairs={{0,4},{4,0},{8,12},{12,8},{1,5},{5,1},{9,13},{13,9},{2,6},{6,2},{1... | collective-permute-start | bytes 417800 | tf_op jit(solution)/shard_map/ppermute | solution.py:640
  71.0 21.2 %collective-permute-start.23 = (s16[2,336,256]{2,1,0:T(8,128)(2,1)S(1)}, s16[2,336,256]{2,1,0:T(8,128)(2,1)S(1)}, u32[]{:S(2)}, u32[]{:S(2)}) collective-permute-start(s16[2,336,256]{2,1,0:T(8,128)(2,1)S(1)} %collective-permute-done.21.refs_5_), channel_id=1, source_target_pairs={{0,1},{1,0},{2,3},{3,2},{4,5},{5,4},{6,7},{7,6},{8,9},{9,8},{10,11... | collective-permute-start | bytes 1032200 | tf_op jit(solution)/shard_map/ppermute | solution.py:640
  85.6 10.9 %collective-permute-start.14 = (s16[2,336,256]{2,1,0:T(8,128)(2,1)S(1)}, s16[2,336,256]{2,1,0:T(8,128)(2,1)S(1)}, u32[]{:S(2)}, u32[]{:S(2)}) collective-permute-start(s16[2,336,256]{2,1,0:T(8,128)(2,1)S(1)} %collective-permute-done.13.refs_4_), channel_id=1, source_target_pairs={{0,2},{1,3},{2,0},{3,1},{4,6},{5,7},{6,4},{7,5},{8,10},{9,11},{10,... | collective-permute-start | bytes 1032200 | tf_op jit(solution)/shard_map/ppermute | solution.py:640
  86.1 17.8 %collective-permute-start.18 = (s16[2,336,256]{2,1,0:T(8,128)(2,1)S(1)}, s16[2,336,256]{2,1,0:T(8,128)(2,1)S(1)}, u32[]{:S(2)}, u32[]{:S(2)}) collective-permute-start(s16[2,336,256]{2,1,0:T(8,128)(2,1)S(1)} %collective-permute-done.17.refs_8_), channel_id=1, source_target_pairs={{0,2},{1,3},{2,0},{3,1},{4,6},{5,7},{6,4},{7,5},{8,10},{9,11},{10,... | collective-permute-start | bytes 1032200 | tf_op jit(solution)/shard_map/ppermute | solution.py:640
  91.4 12.5 %collective-permute-start.15 = (s16[2,336,256]{2,1,0:T(8,128)(2,1)S(1)}, s16[2,336,256]{2,1,0:T(8,128)(2,1)S(1)}, u32[]{:S(2)}, u32[]{:S(2)}) collective-permute-start(s16[2,336,256]{2,1,0:T(8,128)(2,1)S(1)} %collective-permute-done.13.refs_4_), channel_id=1, source_target_pairs={{0,1},{1,0},{2,3},{3,2},{4,5},{5,4},{6,7},{7,6},{8,9},{9,8},{10,11... | collective-permute-start | bytes 1032200 | tf_op jit(solution)/shard_map/ppermute | solution.py:640
  91.5 18.0 %collective-permute-start.10 = (s16[2,336,256]{2,1,0:T(8,128)(2,1)S(1)}, s16[2,336,256]{2,1,0:T(8,128)(2,1)S(1)}, u32[]{:S(2)}, u32[]{:S(2)}) collective-permute-start(s16[2,336,256]{2,1,0:T(8,128)(2,1)S(1)} %collective-permute-done.9.refs_4_), channel_id=1, source_target_pairs={{0,2},{1,3},{2,0},{3,1},{4,6},{5,7},{6,4},{7,5},{8,10},{9,11},{10,... | collective-permute-start | bytes 1032200 | tf_op jit(solution)/shard_map/ppermute | solution.py:640
  92.2 17.3 %collective-permute-start.27 = (s16[272,256]{1,0:T(8,128)(2,1)S(1)}, s16[272,256]{1,0:T(8,128)(2,1)S(1)}, u32[]{:S(2)}, u32[]{:S(2)}) collective-permute-start(s16[272,256]{1,0:T(8,128)(2,1)S(1)} %shard_map.82.own_ref), channel_id=1, source_target_pairs={{0,8},{4,12},{8,0},{12,4},{1,9},{5,13},{9,1},{13,5},{2,10},{6,14},... | collective-permute-start | bytes 417800 | tf_op jit(solution)/shard_map/ppermute | solution.py:640
  96.5 16.5 %collective-permute-start.19 = (s16[2,336,256]{2,1,0:T(8,128)(2,1)S(1)}, s16[2,336,256]{2,1,0:T(8,128)(2,1)S(1)}, u32[]{:S(2)}, u32[]{:S(2)}) collective-permute-start(s16[2,336,256]{2,1,0:T(8,128)(2,1)S(1)} %collective-permute-done.17.refs_8_), channel_id=1, source_target_pairs={{0,1},{1,0},{2,3},{3,2},{4,5},{5,4},{6,7},{7,6},{8,9},{9,8},{10,11... | collective-permute-start | bytes 1032200 | tf_op jit(solution)/shard_map/ppermute | solution.py:640
  103.9 9.1 %collective-permute-start.16 = (s16[2,336,256]{2,1,0:T(8,128)(2,1)S(1)}, s16[2,336,256]{2,1,0:T(8,128)(2,1)S(1)}, u32[]{:S(2)}, u32[]{:S(2)}) collective-permute-start(s16[2,336,256]{2,1,0:T(8,128)(2,1)S(1)} %collective-permute-done.14.refs_5_), channel_id=1, source_target_pairs={{0,1},{1,0},{2,3},{3,2},{4,5},{5,4},{6,7},{7,6},{8,9},{9,8},{10,11... | collective-permute-start | bytes 1032200 | tf_op jit(solution)/shard_map/ppermute | solution.py:640
  103.9 9.1 %collective-permute-start.20 = (s16[2,336,256]{2,1,0:T(8,128)(2,1)S(1)}, s16[2,336,256]{2,1,0:T(8,128)(2,1)S(1)}, u32[]{:S(2)}, u32[]{:S(2)}) collective-permute-start(s16[2,336,256]{2,1,0:T(8,128)(2,1)S(1)} %collective-permute-done.18.refs_9_), channel_id=1, source_target_pairs={{0,1},{1,0},{2,3},{3,2},{4,5},{5,4},{6,7},{7,6},{8,9},{9,8},{10,11... | collective-permute-start | bytes 1032200 | tf_op jit(solution)/shard_map/ppermute | solution.py:640
  109.4 7.7 %collective-permute-start.11 = (s16[2,336,256]{2,1,0:T(8,128)(2,1)S(1)}, s16[2,336,256]{2,1,0:T(8,128)(2,1)S(1)}, u32[]{:S(2)}, u32[]{:S(2)}) collective-permute-start(s16[2,336,256]{2,1,0:T(8,128)(2,1)S(1)} %collective-permute-done.9.refs_4_), channel_id=1, source_target_pairs={{0,1},{1,0},{2,3},{3,2},{4,5},{5,4},{6,7},{7,6},{8,9},{9,8},{10,11... | collective-permute-start | bytes 1032200 | tf_op jit(solution)/shard_map/ppermute | solution.py:640
  109.4 7.7 %collective-permute-start.12 = (s16[2,336,256]{2,1,0:T(8,128)(2,1)S(1)}, s16[2,336,256]{2,1,0:T(8,128)(2,1)S(1)}, u32[]{:S(2)}, u32[]{:S(2)}) collective-permute-start(s16[2,336,256]{2,1,0:T(8,128)(2,1)S(1)} %collective-permute-done.10.refs_5_), channel_id=1, source_target_pairs={{0,1},{1,0},{2,3},{3,2},{4,5},{5,4},{6,7},{7,6},{8,9},{9,8},{10,11... | collective-permute-start | bytes 1032200 | tf_op jit(solution)/shard_map/ppermute | solution.py:640
  (1 other events, 0.7 us)
